TPU v7x, 256 devices: a whole 4x4x8 slice. The times are simulated.
256 devices in a mesh: dp: 8 (over y, x_lo), mp: 32 (over z, x_hi, core).
Axes of the slice: x: 4 (x_hi: 2, x_lo: 2; x = x_hi * 2 + x_lo), y: 4, z: 8, core: 2. Of those that a mesh axis runs over, the one named last changes fastest.
Arguments:
- inputs: bfloat16 [4096, 1024], P('dp'), may hold values from -60 to 60
- norm_gain_vector: float32 [1024], replicated, may hold values from 0.5 to 1.5
- query_saved: bfloat16 [4096, 16384], P('dp', 'mp'), may hold values from -5 to 5
- key_saved: bfloat16 [4096, 16384], P('dp', 'mp'), may hold values from -2 to 2
- value_saved: bfloat16 [4096, 16384], P('dp', 'mp'), may hold values from -6 to 6
- w_query: bfloat16 [1024, 16384], P(None, 'mp'), may hold values from -0.1875 to 0.1875
- w_key: bfloat16 [1024, 16384], P(None, 'mp'), may hold values from -0.1875 to 0.1875
- w_value: bfloat16 [1024, 16384], P(None, 'mp'), may hold values from -0.1875 to 0.1875
- w_out: bfloat16 [16384, 1024], P('mp'), may hold values from -0.046875 to 0.046875
- output_gradient: bfloat16 [4096, 1024], P('dp'), may hold values from -4 to 4
Outputs:
- grad_inputs: bfloat16 [4096, 1024], P('dp')
- grad_w_query: bfloat16 [1024, 16384], P(None, 'mp')
- grad_w_key: bfloat16 [1024, 16384], P(None, 'mp')
- grad_w_value: bfloat16 [1024, 16384], P(None, 'mp')
- grad_w_out: bfloat16 [16384, 1024], P('mp')
- grad_gain: float32 [1024], replicated
All inputs are finite; a program needn't handle non-finite values.
Results may differ from a plain program's by a relative error of at most 0.034.
Values may be sent and summed in bfloat16 or wider, within the bound.
No kernel may reach another device: no remote copies, remote signals or barrier semaphores. Data moves between devices by JAX's collectives and lax.ppermute only.
A program may use at most 64 MiB of HBM per device.

v0:
```python
import functools

import jax
import jax.numpy as jnp
from jax import lax
from jax.experimental import pallas as pl
from jax.experimental.pallas import tpu as pltpu
from jax.sharding import PartitionSpec as P

HD = 128
F32 = jnp.float32
BF16 = jnp.bfloat16
EXTRA = 16


def gray(z):
    return z ^ (z >> 1)


RING = {gray(z): z for z in range(8)}


def dp_pairs(flip):
    return [(y * 2 + x, (lambda t: t[0] * 2 + t[1])(flip(y, x))) for y in range(4) for x in range(2)]


def mp_pairs(flip):
    return [
        (z * 4 + h * 2 + c, (lambda t: t[0] * 4 + t[1] * 2 + t[2])(flip(z, h, c)))
        for z in range(8)
        for h in range(2)
        for c in range(2)
    ]


PAIRS = {
    "y1": ("dp", dp_pairs(lambda y, x: (y ^ 1, x))),
    "y3": ("dp", dp_pairs(lambda y, x: (3 - y, x))),
    "x": ("dp", dp_pairs(lambda y, x: (y, 1 - x))),
    "core": ("mp", mp_pairs(lambda z, h, c: (z, h, 1 - c))),
    "g0": ("mp", mp_pairs(lambda z, h, c: (RING[gray(z) ^ 1], h, c))),
    "g1": ("mp", mp_pairs(lambda z, h, c: (RING[gray(z) ^ 2], h, c))),
    "g2": ("mp", mp_pairs(lambda z, h, c: (RING[gray(z) ^ 4], h, c))),
    "xh": ("mp", mp_pairs(lambda z, h, c: (z, 1 - h, c))),
}

ORDERS = (("y1", "y3", "x"), ("y3", "x", "y1"), ("x", "y1", "y3"))
PIECES = (
    (("out", 0, 8), ("value", 0, 3)),
    (("value", 3, 5), ("query", 0, 5)),
    (("query", 5, 3), ("key", 0, 8)),
)
UNIT = 16


def piece_rows(piece):
    return sum(count for _, _, count in piece) * UNIT


def swap(value, step):
    axis, pairs = PAIRS[step]
    return lax.ppermute(value, axis, pairs)


def codes():
    dp = lax.axis_index("dp").astype(jnp.int32)
    mp = lax.axis_index("mp").astype(jnp.int32)
    y, x = dp >> 1, dp & 1
    z, c = mp >> 2, mp & 1
    y1, y3 = (y ^ (y >> 1)) & 1, y >> 1
    g = z ^ (z >> 1)
    bit = {"y1": y1, "y3": y3, "x": x}
    piece = [bit[o[0]] * 4 + bit[o[1]] * 2 + bit[o[2]] for o in ORDERS]
    return jnp.stack([*piece, c * 4 + (g & 1) * 2 + ((g >> 1) & 1)])


def mm(a, b, ca, cb):
    return lax.dot_general(a, b, (((ca,), (cb,)), ((), ())), preferred_element_type=F32)


def split(g):
    high = g.astype(BF16)
    low = (g - high.astype(F32)).astype(BF16)
    return high, low


def joined(high, low):
    return high.astype(F32) + low.astype(F32)


def gain_rows(g):
    high, low = split(g)
    width = g.shape[1]
    row = lax.broadcasted_iota(jnp.int32, (EXTRA, width), 0)
    high = jnp.broadcast_to(high.astype(F32), (EXTRA, width))
    low = jnp.broadcast_to(low.astype(F32), (EXTRA, width))
    return jnp.where(row == 0, high, jnp.where(row == 1, low, 0.0)).astype(BF16)


def gain_of(rows):
    rows = rows.astype(F32)
    return rows[0:1] + rows[1:2]


def attention_kernel(q_ref, k_ref, v_ref, wo_ref, og_ref, att_ref, gq_ref, gk_ref, gv_ref):
    q, k, v = q_ref[...], k_ref[...], v_ref[...]
    scores = mm(q, k, 1, 1)
    top = jnp.max(scores, axis=-1, keepdims=True)
    e = jnp.exp(scores - top)
    probs = e * (1.0 / jnp.sum(e, axis=-1, keepdims=True))
    low = probs.astype(BF16)
    att_ref[...] = mm(low, v, 1, 0).astype(BF16)
    grad_att = mm(og_ref[...], wo_ref[...], 1, 1).astype(BF16)
    gv_ref[...] = mm(low, grad_att, 0, 0).astype(BF16)
    grad_prob = mm(grad_att, v, 1, 1)
    delta = jnp.sum(probs * grad_prob, axis=-1, keepdims=True)
    grad_score = (probs * (grad_prob - delta)).astype(BF16)
    gq_ref[...] = mm(grad_score, k, 1, 0).astype(BF16)
    gk_ref[...] = mm(grad_score, q, 0, 0).astype(BF16)


def attention(q, k, v, wo, og):
    length, width = q.shape
    depth = og.shape[1]
    column = pl.BlockSpec((length, HD), lambda h: (0, h))
    return pl.pallas_call(
        attention_kernel,
        grid=(width // HD,),
        in_specs=[
            column,
            column,
            column,
            pl.BlockSpec((HD, depth), lambda h: (h, 0)),
            pl.BlockSpec((length, depth), lambda h: (0, 0)),
        ],
        out_specs=[column] * 4,
        out_shape=[jax.ShapeDtypeStruct((length, width), BF16)] * 4,
        compiler_params=pltpu.CompilerParams(vmem_limit_bytes=20 << 20),
        cost_estimate=pl.CostEstimate(flops=6 << 30, bytes_accessed=8 << 20, transcendentals=1 << 20),
        name="attention",
    )(q, k, v, wo, og)


def norm_of(rows):
    rows = rows.astype(F32)
    rstd = lax.rsqrt(jnp.mean(rows * rows, axis=-1, keepdims=True) + 1e-06)
    return rows * rstd, rstd


def parts_kernel(code_ref, x_ref, gain_ref, og_ref, att_ref, gq_ref, gk_ref, gv_ref, *refs):
    outs, scratch = refs[:6], dict(zip(("out", "value", "query", "key"), refs[6:]))
    unit, _ = norm_of(x_ref[...])
    normed = (unit * gain_ref[...]).astype(BF16)
    scratch["out"][...] = mm(att_ref[...], og_ref[...], 0, 0).astype(BF16)
    scratch["value"][...] = mm(normed, gv_ref[...], 0, 0).astype(BF16)
    scratch["query"][...] = mm(normed, gq_ref[...], 0, 0).astype(BF16)
    scratch["key"][...] = mm(normed, gk_ref[...], 0, 0).astype(BF16)
    for i, piece in enumerate(PIECES):
        size = piece_rows(piece)
        for p in range(8):
            block = p ^ code_ref[i]
            dst = outs[2 * i] if p >= 4 else outs[2 * i + 1]
            at = (p % 4) * size
            for name, first, count in piece:
                if name == "out":
                    rows = pl.ds(pl.multiple_of(block * 64, 64), 64)
                    dst[pl.ds(at, 64), :] = scratch[name][rows, :512]
                    dst[pl.ds(at + 64, 64), :] = scratch[name][rows, 512:]
                else:
                    n = count * UNIT
                    rows = pl.ds(pl.multiple_of(block * 128 + first * UNIT, UNIT), n)
                    dst[pl.ds(at, n), :] = scratch[name][rows, :]
                at += count * UNIT


def whole(count):
    return [pl.BlockSpec(memory_space=pltpu.VMEM)] * count


SCALARS = pl.BlockSpec(memory_space=pltpu.SMEM)


def parts(code, inputs, gain, og, att, gq, gk, gv):
    depth, width = inputs.shape[1], gq.shape[1]
    shapes = []
    for piece in PIECES:
        shapes += [jax.ShapeDtypeStruct((4 * piece_rows(piece), width), BF16)] * 2
    return pl.pallas_call(
        parts_kernel,
        in_specs=[SCALARS, *whole(7)],
        out_specs=whole(6),
        out_shape=shapes,
        scratch_shapes=[pltpu.VMEM((width, depth), BF16)] + [pltpu.VMEM((depth, width), BF16)] * 3,
        compiler_params=pltpu.CompilerParams(vmem_limit_bytes=24 << 20),
        cost_estimate=pl.CostEstimate(flops=2 << 30, bytes_accessed=8 << 20, transcendentals=0),
        name="parts",
    )(code, inputs, gain, og, att, gq, gk, gv)


def total_kernel(code_ref, x_ref, gq_ref, gk_ref, gv_ref, wq_ref, wk_ref, wv_ref, send_ref, keep_ref, gain_ref, low_ref):
    total = mm(gq_ref[...], wq_ref[...], 1, 1)
    total = total + mm(gk_ref[...], wk_ref[...], 1, 1)
    total = total + mm(gv_ref[...], wv_ref[...], 1, 1)
    unit, _ = norm_of(x_ref[...])
    g = jnp.sum(total * unit, axis=0, keepdims=True)
    low_ref[...] = total.astype(BF16)
    for p in range(8):
        block = p ^ code_ref[3]
        dst = send_ref if p >= 4 else keep_ref
        dst[pl.ds((p % 4) * 64, 64), :] = low_ref[pl.ds(pl.multiple_of(block * 64, 64), 64), :]
    send_ref[pl.ds(256, EXTRA), :] = gain_rows(g)
    gain_ref[...] = joined(*split(g))


def total_share(code, inputs, gq, gk, gv, wq, wk, wv):
    length, depth = inputs.shape
    half = length // 2
    return pl.pallas_call(
        total_kernel,
        in_specs=[SCALARS, *whole(7)],
        out_specs=whole(3),
        out_shape=[
            jax.ShapeDtypeStruct((half + EXTRA, depth), BF16),
            jax.ShapeDtypeStruct((half, depth), BF16),
            jax.ShapeDtypeStruct((1, depth), F32),
        ],
        scratch_shapes=[pltpu.VMEM((length, depth), BF16)],
        compiler_params=pltpu.CompilerParams(vmem_limit_bytes=20 << 20),
        cost_estimate=pl.CostEstimate(flops=2 << 30, bytes_accessed=8 << 20, transcendentals=0),
        name="total_share",
    )(code, inputs, gq, gk, gv, wq, wk, wv)


def mp_step_kernel(rows, first, gain_ref, *refs):
    *sums, last, send_ref, out_ref = refs
    value = sums[0][pl.ds(first, rows), :].astype(F32)
    for ref in (*sums[1:], last):
        value = value + ref[pl.ds(first, rows), :].astype(F32)
    send_ref[pl.ds(0, rows), :] = value.astype(BF16)
    got = last[pl.ds(last.shape[0] - EXTRA, EXTRA), :]
    g = gain_ref[...] + gain_of(got)
    send_ref[pl.ds(rows, EXTRA), :] = gain_rows(g)
    out_ref[...] = joined(*split(g))


def mp_step(gain, sums, rows, first):
    depth = gain.shape[1]
    return pl.pallas_call(
        functools.partial(mp_step_kernel, rows, first),
        in_specs=whole(1 + len(sums)),
        out_specs=whole(2),
        out_shape=[jax.ShapeDtypeStruct((rows + EXTRA, depth), BF16), jax.ShapeDtypeStruct((1, depth), F32)],
        compiler_params=pltpu.CompilerParams(vmem_limit_bytes=4 << 20),
        cost_estimate=pl.CostEstimate(flops=1 << 20, bytes_accessed=2 << 20, transcendentals=0),
        name="mp_step",
    )(gain, *sums)


def rows_kernel(code_ref, x_ref, og_ref, weight_ref, gain_ref, mine_ref, got_ref, out_ref, sum_ref):
    n = out_ref.shape[0]
    gradient = mine_ref[pl.ds(0, n), :].astype(F32) + got_ref[pl.ds(0, n), :].astype(F32)
    unit, rstd = norm_of(x_ref[...])
    scaled = gradient * weight_ref[...]
    inner = jnp.mean(scaled * unit, axis=-1, keepdims=True)
    out_ref[...] = (og_ref[...].astype(F32) + rstd * (scaled - unit * inner)).astype(BF16)
    sum_ref[...] = gain_ref[...] + gain_of(got_ref[pl.ds(n, EXTRA), :])


def own_rows(code, inputs, og, weight, gain, mine, got):
    n, depth = mine.shape[0] - EXTRA, mine.shape[1]

    def fixed(shape):
        return pl.BlockSpec(shape, lambda i, c: (0, 0))

    row = pl.BlockSpec((n, depth), lambda i, c: (c[3], 0))
    return pl.pallas_call(
        rows_kernel,
        grid_spec=pltpu.PrefetchScalarGridSpec(
            num_scalar_prefetch=1,
            grid=(1,),
            in_specs=[row, row, fixed((1, depth)), fixed((1, depth)), fixed(mine.shape), fixed(got.shape)],
            out_specs=[fixed((n, depth)), fixed((1, depth))],
        ),
        out_shape=[jax.ShapeDtypeStruct((n, depth), BF16), jax.ShapeDtypeStruct((1, depth), F32)],
        compiler_params=pltpu.CompilerParams(vmem_limit_bytes=4 << 20),
        cost_estimate=pl.CostEstimate(flops=1 << 20, bytes_accessed=1 << 20, transcendentals=0),
        name="own_rows",
    )(code, inputs, og, weight, gain, mine, got)


def finish_kernel(code_ref, *refs):
    halves, outs = refs[:8], refs[8:]
    grad_inputs_ref = outs[0]
    named = dict(zip(("query", "key", "value", "out"), outs[1:]))
    for p in range(8):
        block = p ^ code_ref[3]
        src = halves[7] if p >= 4 else halves[6]
        grad_inputs_ref[pl.ds(pl.multiple_of(block * 64, 64), 64), :] = src[pl.ds((p % 4) * 64, 64), :]
    for i, piece in enumerate(PIECES):
        size = piece_rows(piece)
        for p in range(8):
            block = p ^ code_ref[i]
            src = halves[2 * i + 1] if p >= 4 else halves[2 * i]
            at = (p % 4) * size
            for name, first, count in piece:
                if name == "out":
                    rows = pl.ds(pl.multiple_of(block * 64, 64), 64)
                    named[name][rows, :512] = src[pl.ds(at, 64), :]
                    named[name][rows, 512:] = src[pl.ds(at + 64, 64), :]
                else:
                    n = count * UNIT
                    rows = pl.ds(pl.multiple_of(block * 128 + first * UNIT, UNIT), n)
                    named[name][rows, :] = src[pl.ds(at, n), :]
                at += count * UNIT


def finish(code, halves, length, depth, width):
    return pl.pallas_call(
        finish_kernel,
        in_specs=[SCALARS, *whole(8)],
        out_specs=whole(5),
        out_shape=[
            jax.ShapeDtypeStruct((length, depth), BF16),
            *[jax.ShapeDtypeStruct((depth, width), BF16)] * 3,
            jax.ShapeDtypeStruct((width, depth), BF16),
        ],
        compiler_params=pltpu.CompilerParams(vmem_limit_bytes=14 << 20),
        cost_estimate=pl.CostEstimate(flops=1 << 20, bytes_accessed=10 << 20, transcendentals=0),
        name="finish",
    )(code, *halves)


def plus(*values):
    total = values[0].astype(F32)
    for value in values[1:]:
        total = total + value.astype(F32)
    return total.astype(BF16)


def shards(
    inputs,
    norm_gain_vector,
    query_saved,
    key_saved,
    value_saved,
    w_query,
    w_key,
    w_value,
    w_out,
    output_gradient,
):
    length, depth = inputs.shape
    width = query_saved.shape[1]
    code = codes()
    weight = norm_gain_vector.reshape(1, depth)
    att, gq, gk, gv = attention(query_saved, key_saved, value_saved, w_out, output_gradient)
    pieces = parts(code, inputs, weight, output_gradient, att, gq, gk, gv)
    m_send, m_keep, gain = total_share(code, inputs, gq, gk, gv, w_query, w_key, w_value)

    sends, keeps = pieces[0::2], pieces[1::2]
    sizes = [piece_rows(piece) for piece in PIECES]
    first = [swap(s, o[0]) for s, o in zip(sends, ORDERS)]
    r1 = swap(m_send, "core")
    send, gain = mp_step(gain, (m_keep, r1), 128, 128)
    r2 = swap(send, "g0")
    second = [
        swap(plus(k[2 * n :], r[2 * n :]), o[1]) for k, r, o, n in zip(keeps, first, ORDERS, sizes)
    ]
    send, gain = mp_step(gain, (m_keep, r1, r2), 64, 64)
    r3 = swap(send, "g1")
    third = [
        swap(plus(k[n : 2 * n], r[n : 2 * n], s[n:]), o[2])
        for k, r, s, o, n in zip(keeps, first, second, ORDERS, sizes)
    ]
    send, gain = mp_step(gain, (m_keep, r1, r2, r3), 64, 0)
    r4 = swap(send, "g2")
    own = [plus(k[:n], r[:n], s[:n], t) for k, r, s, t, n in zip(keeps, first, second, third, sizes)]
    back = [swap(v, o[2]) for v, o in zip(own, ORDERS)]
    send, gain = mp_step(gain, (send, r4), 64, 0)
    r5 = swap(send, "xh")
    rows, gain = own_rows(code, inputs, output_gradient, weight, gain, send, r5)
    quarter = [jnp.concatenate([v, b]) for v, b in zip(own, back)]
    back = [swap(v, o[1]) for v, o in zip(quarter, ORDERS)]
    half = [jnp.concatenate([v, b]) for v, b in zip(quarter, back)]
    last = [swap(v, o[0]) for v, o in zip(half, ORDERS)]
    for step in ("g1", "g0"):
        rows = jnp.concatenate([rows, swap(rows, step)])
    rows_last = swap(rows, "core")
    for step in ("x", "y1", "y3"):
        gain = gain + swap(gain, step)
    halves = [v for pair in zip(half, last) for v in pair] + [rows, rows_last]
    outs = finish(code, halves, length, depth, width)
    return (*outs, gain.reshape(depth))


def solution(mesh):
    return jax.shard_map(
        shards,
        mesh=mesh,
        in_specs=(
            P("dp", None),
            P(),
            P("dp", "mp"),
            P("dp", "mp"),
            P("dp", "mp"),
            P(None, "mp"),
            P(None, "mp"),
            P(None, "mp"),
            P("mp", None),
            P("dp", None),
        ),
        out_specs=(P("dp", None), P(None, "mp"), P(None, "mp"), P(None, "mp"), P("mp", None), P()),
        check_vma=False,
    )
```

profile of v0, /device:TPU:34, one launch (start us, length us, event | category | flops | bytes accessed | tf_op | source)
XLA Modules:
  0.0 112.6 jit_solution(1307996003330752922)
XLA Ops:
  0.7 0.1 pad_add_fusion.code_ref
  0.7 1.2 %copy-done.1 = bf16[512,1024]{1,0:T(8,128)(2,1)S(1)} copy-done((bf16[512,1024]{1,0:T(8,128)(2,1)S(1)}, bf16[512,1024]{1,0:T(8,128)(2,1)}, u32[]{:S(2)}) %copy-start.1) | copy-done | bytes 1048600
  2.0 1.2 %copy-done.4 = bf16[512,1024]{1,0:T(8,128)(2,1)S(1)} copy-done((bf16[512,1024]{1,0:T(8,128)(2,1)S(1)}, bf16[512,1024]{1,0:T(8,128)(2,1)}, u32[]{:S(2)}) %copy-start.4) | copy-done | bytes 1048600
  3.2 1.0 copy-done.8
  4.2 1.0 copy-done.9
  5.3 1.0 copy-done.10
  6.3 7.8 %attention.1 = (bf16[512,512]{1,0:T(8,128)(2,1)S(1)}, bf16[512,512]{1,0:T(8,128)(2,1)S(1)}, bf16[512,512]{1,0:T(8,128)(2,1)S(1)}, bf16[512,512]{1,0:T(8,128)(2,1)S(1)}) custom-call(bf16[512,512]{1,0:T(8,128)(2,1)S(1)} %copy-done.8, bf16[512,512]{1,0:T(8,128)(2,1)S(1)} %copy-done.9, bf16[512,512]{1,0:T(8,128)(2,1)S(1)} %copy-done.10, ...), custom_call_target="tpu_custom_call" | custom-call | flops 6442450944 | bytes 8388608 | tf_op jit(solution)/shard_map/attention/pallas_call | solution.py:126
  14.2 3.1 %parts.1 = (bf16[704,512]{1,0:T(8,128)(2,1)S(1)}, bf16[704,512]{1,0:T(8,128)(2,1)S(1)}, bf16[640,512]{1,0:T(8,128)(2,1)S(1)}, bf16[640,512]{1,0:T(8,128)(2,1)S(1...) custom-call(s32[4]{0:T(128)S(1)} %pad_add_fusion.code_ref, bf16[512,1024]{1,0:T(8,128)(2,1)S(1)} %copy-done, ...), custom_call_target="tpu_custom_call" | custom-call | flops 2147483648 | bytes 8388608 | tf_op jit(solution)/shard_map/parts/pallas_call | solution.py:188
  17.4 3.1 %collective-permute-start.6 = (bf16[640,512]{1,0:T(8,128)(2,1)S(1)}, bf16[640,512]{1,0:T(8,128)(2,1)S(1)}, u32[]{:S(2)}, u32[]{:S(2)}) collective-permute-start(bf16[640,512]{1,0:T(8,128)(2,1)S(1)} %get-tuple-element.41), channel_id=1, source_target_pairs={{0,192},{32,224},{64,128},{96,160},{128,64},{160,96},{192,0},{224,... | collective-permute-start | bytes 1966088 | tf_op jit(solution)/shard_map/ppermute | solution.py:62
  20.5 2.5 %total_share.1 = (bf16[272,1024]{1,0:T(8,128)(2,1)S(1)}, bf16[256,1024]{1,0:T(8,128)(2,1)S(1)}, f32[1,1024]{1,0:T(1,128)S(1)}) custom-call(s32[4]{0:T(128)S(1)} %pad_add_fusion.code_ref, bf16[512,1024]{1,0:T(8,128)(2,1)S(1)} %copy-done, bf16[512,512]{1,0:T(8,128)(2,1)S(1)} %get-tuple-element.35.gq_ref, bf16[512,512]{1,0:T(8,128)(2,1)S(1)} %get-tuple-element.36.gk_ref, ...), custom_call_target="tpu_custom_call" | custom-call | flops 2147483648 | bytes 8388608 | tf_op jit(solution)/shard_map/total_share/pallas_call | solution.py:218
  23.0 0.1 collective-permute-start.18
  23.1 0.2 collective-permute-start
  23.3 0.5 collective-permute-start.12
  23.8 1.2 %collective-permute-done.18.refs_1_ = bf16[272,1024]{1,0:T(8,128)(2,1)S(1)} collective-permute-done((bf16[272,1024]{1,0:T(8,128)(2,1)S(1)}, bf16[272,1024]{1,0:T(8,128)(2,1)S(1)}, u32[]{:S(2)}, u32[]{:S(2)}) %collective-permute-start.18) | collective-permute-done | bytes 557088 | tf_op jit(solution)/shard_map/ppermute | solution.py:62
  25.0 0.1 mp_step.4
  25.1 0.2 collective-permute-start.19
  25.3 9.9 %collective-permute-done.6 = bf16[640,512]{1,0:T(8,128)(2,1)S(1)} collective-permute-done((bf16[640,512]{1,0:T(8,128)(2,1)S(1)}, bf16[640,512]{1,0:T(8,128)(2,1)S(1)}, u32[]{:S(2)}, u32[]{:S(2)}) %collective-permute-start.6) | collective-permute-done | bytes 655392 | tf_op jit(solution)/shard_map/ppermute | solution.py:62
  35.2 0.1 add_convert_fusion.2
  35.3 0.6 collective-permute-start.7
  35.9 5.7 %collective-permute-done = bf16[704,512]{1,0:T(8,128)(2,1)S(1)} collective-permute-done((bf16[704,512]{1,0:T(8,128)(2,1)S(1)}, bf16[704,512]{1,0:T(8,128)(2,1)S(1)}, u32[]{:S(2)}, u32[]{:S(2)}) %collective-permute-start) | collective-permute-done | bytes 720928 | tf_op jit(solution)/shard_map/ppermute | solution.py:62
  41.6 0.1 add_convert_fusion.1
  41.7 0.3 collective-permute-start.1
  42.0 0.2 collective-permute-done.12
  42.2 0.1 add_convert_fusion
  42.3 2.0 %collective-permute-start.13 = (bf16[352,512]{1,0:T(8,128)(2,1)S(1)}, bf16[352,512]{1,0:T(8,128)(2,1)S(1)}, u32[]{:S(2)}, u32[]{:S(2)}) collective-permute-start(bf16[352,512]{1,0:T(8,128)(2,1)S(1)} %add_convert_fusion), channel_id=1, source_target_pairs={{0,64},{32,96},{64,0},{96,32},{128,192},{160,224},{192,128},{224,1... | collective-permute-start | bytes 1081352 | tf_op jit(solution)/shard_map/ppermute | solution.py:62
  44.3 0.1 mp_step.5
  44.4 2.0 %collective-permute-start.20 = (bf16[80,1024]{1,0:T(8,128)(2,1)S(1)}, bf16[80,1024]{1,0:T(8,128)(2,1)S(1)}, u32[]{:S(2)}, u32[]{:S(2)}) collective-permute-start(bf16[80,1024]{1,0:T(8,128)(2,1)S(1)} %get-tuple-element.50), channel_id=1, source_target_pairs={{0,12},{1,13},{2,14},{3,15},{4,8},{5,9},{6,10},{7,11},{8,4},{9,5},... | collective-permute-start | bytes 491528 | tf_op jit(solution)/shard_map/ppermute | solution.py:62
  46.4 2.2 %collective-permute-done.7 = bf16[320,512]{1,0:T(8,128)(2,1)S(1)} collective-permute-done((bf16[320,512]{1,0:T(8,128)(2,1)S(1)}, bf16[320,512]{1,0:T(8,128)(2,1)S(1)}, u32[]{:S(2)}, u32[]{:S(2)}) %collective-permute-start.7) | collective-permute-done | bytes 327712 | tf_op jit(solution)/shard_map/ppermute | solution.py:62
  48.7 1.8 %collective-permute-start.8 = (bf16[160,512]{1,0:T(8,128)(2,1)S(1)}, bf16[160,512]{1,0:T(8,128)(2,1)S(1)}, u32[]{:S(2)}, u32[]{:S(2)}) collective-permute-start(bf16[160,512]{1,0:T(8,128)(2,1)S(1)} %add_convert_fusion.8), channel_id=1, source_target_pairs={{0,64},{32,96},{64,0},{96,32},{128,192},{160,224},{192,128},{224,1... | collective-permute-start | bytes 491528 | tf_op jit(solution)/shard_map/ppermute | solution.py:62
  50.5 2.0 %collective-permute-done.20.refs_3_ = bf16[80,1024]{1,0:T(8,128)(2,1)S(1)} collective-permute-done((bf16[80,1024]{1,0:T(8,128)(2,1)S(1)}, bf16[80,1024]{1,0:T(8,128)(2,1)S(1)}, u32[]{:S(2)}, u32[]{:S(2)}) %collective-permute-start.20) | collective-permute-done | bytes 163872 | tf_op jit(solution)/shard_map/ppermute | solution.py:62
  52.6 0.1 mp_step.6
  52.7 5.8 %collective-permute-start.21 = (bf16[80,1024]{1,0:T(8,128)(2,1)S(1)}, bf16[80,1024]{1,0:T(8,128)(2,1)S(1)}, u32[]{:S(2)}, u32[]{:S(2)}) collective-permute-start(bf16[80,1024]{1,0:T(8,128)(2,1)S(1)} %get-tuple-element.52.refs_0_), channel_id=1, source_target_pairs={{0,28},{1,29},{2,30},{3,31},{4,24},{5,25},{6,26},{7,27},{8,20},{9,... | collective-permute-start | bytes 491528 | tf_op jit(solution)/shard_map/ppermute | solution.py:62
  58.4 0.1 add_convert_fusion.6
  58.5 0.8 collective-permute-start.2
  59.3 0.1 add_convert_fusion.4
  59.4 2.1 %collective-permute-start.14 = (bf16[176,512]{1,0:T(8,128)(2,1)S(1)}, bf16[176,512]{1,0:T(8,128)(2,1)S(1)}, u32[]{:S(2)}, u32[]{:S(2)}) collective-permute-start(bf16[176,512]{1,0:T(8,128)(2,1)S(1)} %add_convert_fusion.4), channel_id=1, source_target_pairs={{0,192},{32,224},{64,128},{96,160},{128,64},{160,96},{192,0},{224,... | collective-permute-start | bytes 540680 | tf_op jit(solution)/shard_map/ppermute | solution.py:62
  61.5 0.1 add_convert_fusion.7
  61.6 1.2 %collective-permute-start.9 = (bf16[160,512]{1,0:T(8,128)(2,1)S(1)}, bf16[160,512]{1,0:T(8,128)(2,1)S(1)}, u32[]{:S(2)}, u32[]{:S(2)}) collective-permute-start(bf16[160,512]{1,0:T(8,128)(2,1)S(1)} %add_convert_fusion.7), channel_id=1, source_target_pairs={{0,64},{32,96},{64,0},{96,32},{128,192},{160,224},{192,128},{224,1... | collective-permute-start | bytes 491528 | tf_op jit(solution)/shard_map/ppermute | solution.py:62
  62.9 2.5 %collective-permute-start.22 = (bf16[80,1024]{1,0:T(8,128)(2,1)S(1)}, bf16[80,1024]{1,0:T(8,128)(2,1)S(1)}, u32[]{:S(2)}, u32[]{:S(2)}) collective-permute-start(bf16[80,1024]{1,0:T(8,128)(2,1)S(1)} %get-tuple-element.54.mine_ref), channel_id=1, source_target_pairs={{0,2},{1,3},{2,0},{3,1},{4,6},{5,7},{6,4},{7,5},{8,10},{9,11},{10,... | collective-permute-start | bytes 491528 | tf_op jit(solution)/shard_map/ppermute | solution.py:62
  65.4 0.1 add_convert_fusion.5
  65.5 1.9 %collective-permute-start.3 = (bf16[176,512]{1,0:T(8,128)(2,1)S(1)}, bf16[176,512]{1,0:T(8,128)(2,1)S(1)}, u32[]{:S(2)}, u32[]{:S(2)}) collective-permute-start(bf16[176,512]{1,0:T(8,128)(2,1)S(1)} %add_convert_fusion.5), channel_id=1, source_target_pairs={{0,32},{32,0},{64,96},{96,64},{128,160},{160,128},{192,224},{224,1... | collective-permute-start | bytes 540680 | tf_op jit(solution)/shard_map/ppermute | solution.py:62
  67.3 0.1 add_convert_fusion.3
  67.4 0.9 collective-permute-start.15
  68.4 1.6 %collective-permute-start.10 = (bf16[320,512]{1,0:T(8,128)(2,1)S(1)}, bf16[320,512]{1,0:T(8,128)(2,1)S(1)}, u32[]{:S(2)}, u32[]{:S(2)}) collective-permute-start(bf16[320,512]{1,0:T(8,128)(2,1)S(1)} %pad_maximum_fusion.5), channel_id=1, source_target_pairs={{0,32},{32,0},{64,96},{96,64},{128,160},{160,128},{192,224},{224,1... | collective-permute-start | bytes 983048 | tf_op jit(solution)/shard_map/ppermute | solution.py:62
  70.0 1.6 %collective-permute-done.22.got_ref = bf16[80,1024]{1,0:T(8,128)(2,1)S(1)} collective-permute-done((bf16[80,1024]{1,0:T(8,128)(2,1)S(1)}, bf16[80,1024]{1,0:T(8,128)(2,1)S(1)}, u32[]{:S(2)}, u32[]{:S(2)}) %collective-permute-start.22) | collective-permute-done | bytes 163872 | tf_op jit(solution)/shard_map/ppermute | solution.py:62
  71.6 0.8 own_rows.1
  72.4 1.1 collective-permute-start.23
  73.5 2.6 %collective-permute-done.3 = bf16[176,512]{1,0:T(8,128)(2,1)S(1)} collective-permute-done((bf16[176,512]{1,0:T(8,128)(2,1)S(1)}, bf16[176,512]{1,0:T(8,128)(2,1)S(1)}, u32[]{:S(2)}, u32[]{:S(2)}) %collective-permute-start.3) | collective-permute-done | bytes 180256 | tf_op jit(solution)/shard_map/ppermute | solution.py:62
  76.1 0.8 collective-permute-start.4
  76.9 1.0 collective-permute-start.16
  77.9 3.6 %collective-permute-start.24 = (bf16[128,1024]{1,0:T(8,128)(2,1)S(1)}, bf16[128,1024]{1,0:T(8,128)(2,1)S(1)}, u32[]{:S(2)}, u32[]{:S(2)}) collective-permute-start(bf16[128,1024]{1,0:T(8,128)(2,1)S(1)} %pad_maximum_fusion.6), channel_id=1, source_target_pairs={{0,4},{1,5},{2,6},{3,7},{4,0},{5,1},{6,2},{7,3},{8,12},{9,13},{10,... | collective-permute-start | bytes 786440 | tf_op jit(solution)/shard_map/ppermute | solution.py:62
  81.6 1.3 %collective-permute-start.11 = (bf16[640,512]{1,0:T(8,128)(2,1)S(1)}, bf16[640,512]{1,0:T(8,128)(2,1)S(1)}, u32[]{:S(2)}, u32[]{:S(2)}) collective-permute-start(bf16[640,512]{1,0:T(8,128)(2,1)S(1)} %pad_maximum_fusion.2.refs_2_), channel_id=1, source_target_pairs={{0,192},{32,224},{64,128},{96,160},{128,64},{160,96},{192,0},{224,... | collective-permute-start | bytes 1966088 | tf_op jit(solution)/shard_map/ppermute | solution.py:62
  82.9 5.8 %collective-permute-done.4 = bf16[352,512]{1,0:T(8,128)(2,1)S(1)} collective-permute-done((bf16[352,512]{1,0:T(8,128)(2,1)S(1)}, bf16[352,512]{1,0:T(8,128)(2,1)S(1)}, u32[]{:S(2)}, u32[]{:S(2)}) %collective-permute-start.4) | collective-permute-done | bytes 360480 | tf_op jit(solution)/shard_map/ppermute | solution.py:62
  88.7 0.1 collective-permute-start.5
  88.9 0.3 collective-permute-start.17
  89.3 0.1 collective-permute-start.25
  89.4 1.9 %collective-permute-start.26 = (f32[1,1024]{1,0:T(1,128)S(1)}, f32[1,1024]{1,0:T(1,128)S(1)}, u32[]{:S(2)}, u32[]{:S(2)}) collective-permute-start(f32[1,1024]{1,0:T(1,128)S(1)} %get-tuple-element.61), channel_id=1, source_target_pairs={{0,32},{32,0},{64,96},{96,64},{128,160},{160,128},{192,224},{224,1... | collective-permute-start | bytes 12296 | tf_op jit(solution)/shard_map/ppermute | solution.py:62
  91.3 9.1 %collective-permute-done.26 = f32[1,1024]{1,0:T(1,128)S(1)} collective-permute-done((f32[1,1024]{1,0:T(1,128)S(1)}, f32[1,1024]{1,0:T(1,128)S(1)}, u32[]{:S(2)}, u32[]{:S(2)}) %collective-permute-start.26) | collective-permute-done | bytes 4128 | tf_op jit(solution)/shard_map/ppermute | solution.py:62
  100.3 2.0 %collective-permute-start.27 = (f32[1,1024]{1,0:T(1,128)S(1)}, f32[1,1024]{1,0:T(1,128)S(1)}, u32[]{:S(2)}, u32[]{:S(2)}) collective-permute-start(f32[1,1024]{1,0:T(1,128)S(1)} %add.113), channel_id=1, source_target_pairs={{0,64},{32,96},{64,0},{96,32},{128,192},{160,224},{192,128},{224,1... | collective-permute-start | bytes 12296 | tf_op jit(solution)/shard_map/ppermute | solution.py:62
  102.3 1.6 %collective-permute-done.27 = f32[1,1024]{1,0:T(1,128)S(1)} collective-permute-done((f32[1,1024]{1,0:T(1,128)S(1)}, f32[1,1024]{1,0:T(1,128)S(1)}, u32[]{:S(2)}, u32[]{:S(2)}) %collective-permute-start.27) | collective-permute-done | bytes 4128 | tf_op jit(solution)/shard_map/ppermute | solution.py:62
  103.9 2.0 %collective-permute-start.28 = (f32[1,1024]{1,0:T(1,128)S(1)}, f32[1,1024]{1,0:T(1,128)S(1)}, u32[]{:S(2)}, u32[]{:S(2)}) collective-permute-start(f32[1,1024]{1,0:T(1,128)S(1)} %add.114), channel_id=1, source_target_pairs={{0,192},{32,224},{64,128},{96,160},{128,64},{160,96},{192,0},{224,... | collective-permute-start | bytes 12296 | tf_op jit(solution)/shard_map/ppermute | solution.py:62
  106.0 2.8 %collective-permute-done.28 = f32[1,1024]{1,0:T(1,128)S(1)} collective-permute-done((f32[1,1024]{1,0:T(1,128)S(1)}, f32[1,1024]{1,0:T(1,128)S(1)}, u32[]{:S(2)}, u32[]{:S(2)}) %collective-permute-start.28) | collective-permute-done | bytes 4128 | tf_op jit(solution)/shard_map/ppermute | solution.py:62
  108.8 0.6 add.115
  109.4 3.2 %finish.1 = (bf16[512,1024]{1,0:T(8,128)(2,1)}, bf16[1024,512]{1,0:T(8,128)(2,1)}, bf16[1024,512]{1,0:T(8,128)(2,1)}, bf16[1024,512]{1,0:T(8,128)(2,1)}, bf16[512,1024]{1,0:T(8,128)(2,1)}) custom-call(s32[4]{0:T(128)S(1)} %pad_add_fusion.code_ref, bf16[704,512]{1,0:T(8,128)(2,1)S(1)} %pad_maximum_fusion.refs_0_, ...), custom_call_target="tpu_custom_call" | custom-call | flops 1048576 | bytes 10485760 | tf_op jit(solution)/shard_map/finish/pallas_call | solution.py:318
  (48 shorter events, 0.5 us)
Async XLA Ops:
  0.7 1.2 %copy-start.1 = (bf16[512,1024]{1,0:T(8,128)(2,1)S(1)}, bf16[512,1024]{1,0:T(8,128)(2,1)}, u32[]{:S(2)}) copy-start(bf16[512,1024]{1,0:T(8,128)(2,1)} %og_ref.5) | copy-start | bytes 3145732
  2.0 1.2 %copy-start.4 = (bf16[512,1024]{1,0:T(8,128)(2,1)S(1)}, bf16[512,1024]{1,0:T(8,128)(2,1)}, u32[]{:S(2)}) copy-start(bf16[512,1024]{1,0:T(8,128)(2,1)} %wo_ref.1) | copy-start | bytes 3145732
  3.2 1.0 copy-start.8
  4.2 1.0 copy-start.9
  5.3 1.0 copy-start.10
  6.3 7.8 %copy-start = (bf16[512,1024]{1,0:T(8,128)(2,1)S(1)}, bf16[512,1024]{1,0:T(8,128)(2,1)}, u32[]{:S(2)}) copy-start(bf16[512,1024]{1,0:T(8,128)(2,1)} %x_ref.5) | copy-start | bytes 3145732
  6.3 7.9 %copy-start.2 = (bf16[512,1024]{1,0:T(8,128)(2,1)S(1)}, bf16[512,1024]{1,0:T(8,128)(2,1)}, u32[]{:S(2)}) copy-start(bf16[512,1024]{1,0:T(8,128)(2,1)} %og_ref.5) | copy-start | bytes 3145732
  6.3 7.9 %copy-start.3 = (f32[1024]{0:T(1024)S(1)}, f32[1024]{0:T(1024)}, u32[]{:S(2)}) copy-start(f32[1024]{0:T(1024)} %param.11) | copy-start | bytes 12292
  14.2 6.3 %copy-start.5 = (bf16[1024,512]{1,0:T(8,128)(2,1)S(1)}, bf16[1024,512]{1,0:T(8,128)(2,1)}, u32[]{:S(2)}) copy-start(bf16[1024,512]{1,0:T(8,128)(2,1)} %wq_ref.1) | copy-start | bytes 3145732
  14.2 6.3 %copy-start.6 = (bf16[1024,512]{1,0:T(8,128)(2,1)S(1)}, bf16[1024,512]{1,0:T(8,128)(2,1)}, u32[]{:S(2)}) copy-start(bf16[1024,512]{1,0:T(8,128)(2,1)} %wk_ref.1) | copy-start | bytes 3145732
  14.2 6.3 %copy-start.7 = (bf16[1024,512]{1,0:T(8,128)(2,1)S(1)}, bf16[1024,512]{1,0:T(8,128)(2,1)}, u32[]{:S(2)}) copy-start(bf16[1024,512]{1,0:T(8,128)(2,1)} %wv_ref.1) | copy-start | bytes 3145732
  17.4 17.8 %collective-permute-start.6 = (bf16[640,512]{1,0:T(8,128)(2,1)S(1)}, bf16[640,512]{1,0:T(8,128)(2,1)S(1)}, u32[]{:S(2)}, u32[]{:S(2)}) collective-permute-start(bf16[640,512]{1,0:T(8,128)(2,1)S(1)} %get-tuple-element.41), channel_id=1, source_target_pairs={{0,192},{32,224},{64,128},{96,160},{128,64},{160,96},{192,0},{224,... | collective-permute-start | bytes 1966088 | tf_op jit(solution)/shard_map/ppermute | solution.py:62
  23.0 2.0 %collective-permute-start.18 = (bf16[272,1024]{1,0:T(8,128)(2,1)S(1)}, bf16[272,1024]{1,0:T(8,128)(2,1)S(1)}, u32[]{:S(2)}, u32[]{:S(2)}) collective-permute-start(bf16[272,1024]{1,0:T(8,128)(2,1)S(1)} %get-tuple-element.46), channel_id=1, source_target_pairs={{0,1},{1,0},{2,3},{3,2},{4,5},{5,4},{6,7},{7,6},{8,9},{9,8},{10,11... | collective-permute-start | bytes 1671176 | tf_op jit(solution)/shard_map/ppermute | solution.py:62
  23.1 18.6 %collective-permute-start = (bf16[704,512]{1,0:T(8,128)(2,1)S(1)}, bf16[704,512]{1,0:T(8,128)(2,1)S(1)}, u32[]{:S(2)}, u32[]{:S(2)}) collective-permute-start(bf16[704,512]{1,0:T(8,128)(2,1)S(1)} %get-tuple-element.39), channel_id=1, source_target_pairs={{0,64},{32,96},{64,0},{96,32},{128,192},{160,224},{192,128},{224,1... | collective-permute-start | bytes 2162696 | tf_op jit(solution)/shard_map/ppermute | solution.py:62
  23.3 19.0 %collective-permute-start.12 = (bf16[704,512]{1,0:T(8,128)(2,1)S(1)}, bf16[704,512]{1,0:T(8,128)(2,1)S(1)}, u32[]{:S(2)}, u32[]{:S(2)}) collective-permute-start(bf16[704,512]{1,0:T(8,128)(2,1)S(1)} %get-tuple-element.43), channel_id=1, source_target_pairs={{0,32},{32,0},{64,96},{96,64},{128,160},{160,128},{192,224},{224,1... | collective-permute-start | bytes 2162696 | tf_op jit(solution)/shard_map/ppermute | solution.py:62
  25.1 19.2 %collective-permute-start.19 = (bf16[144,1024]{1,0:T(8,128)(2,1)S(1)}, bf16[144,1024]{1,0:T(8,128)(2,1)S(1)}, u32[]{:S(2)}, u32[]{:S(2)}) collective-permute-start(bf16[144,1024]{1,0:T(8,128)(2,1)S(1)} %get-tuple-element.48), channel_id=1, source_target_pairs={{0,4},{1,5},{2,6},{3,7},{4,0},{5,1},{6,2},{7,3},{8,12},{9,13},{10,... | collective-permute-start | bytes 884744 | tf_op jit(solution)/shard_map/ppermute | solution.py:62
  35.3 13.3 %collective-permute-start.7 = (bf16[320,512]{1,0:T(8,128)(2,1)S(1)}, bf16[320,512]{1,0:T(8,128)(2,1)S(1)}, u32[]{:S(2)}, u32[]{:S(2)}) collective-permute-start(bf16[320,512]{1,0:T(8,128)(2,1)S(1)} %add_convert_fusion.2), channel_id=1, source_target_pairs={{0,32},{32,0},{64,96},{96,64},{128,160},{160,128},{192,224},{224,1... | collective-permute-start | bytes 983048 | tf_op jit(solution)/shard_map/ppermute | solution.py:62
  41.7 16.7 %collective-permute-start.1 = (bf16[352,512]{1,0:T(8,128)(2,1)S(1)}, bf16[352,512]{1,0:T(8,128)(2,1)S(1)}, u32[]{:S(2)}, u32[]{:S(2)}) collective-permute-start(bf16[352,512]{1,0:T(8,128)(2,1)S(1)} %add_convert_fusion.1), channel_id=1, source_target_pairs={{0,192},{32,224},{64,128},{96,160},{128,64},{160,96},{192,0},{224,... | collective-permute-start | bytes 1081352 | tf_op jit(solution)/shard_map/ppermute | solution.py:62
  42.3 16.9 %collective-permute-start.13 = (bf16[352,512]{1,0:T(8,128)(2,1)S(1)}, bf16[352,512]{1,0:T(8,128)(2,1)S(1)}, u32[]{:S(2)}, u32[]{:S(2)}) collective-permute-start(bf16[352,512]{1,0:T(8,128)(2,1)S(1)} %add_convert_fusion), channel_id=1, source_target_pairs={{0,64},{32,96},{64,0},{96,32},{128,192},{160,224},{192,128},{224,1... | collective-permute-start | bytes 1081352 | tf_op jit(solution)/shard_map/ppermute | solution.py:62
  44.4 8.1 %collective-permute-start.20 = (bf16[80,1024]{1,0:T(8,128)(2,1)S(1)}, bf16[80,1024]{1,0:T(8,128)(2,1)S(1)}, u32[]{:S(2)}, u32[]{:S(2)}) collective-permute-start(bf16[80,1024]{1,0:T(8,128)(2,1)S(1)} %get-tuple-element.50), channel_id=1, source_target_pairs={{0,12},{1,13},{2,14},{3,15},{4,8},{5,9},{6,10},{7,11},{8,4},{9,5},... | collective-permute-start | bytes 491528 | tf_op jit(solution)/shard_map/ppermute | solution.py:62
  48.7 12.8 %collective-permute-start.8 = (bf16[160,512]{1,0:T(8,128)(2,1)S(1)}, bf16[160,512]{1,0:T(8,128)(2,1)S(1)}, u32[]{:S(2)}, u32[]{:S(2)}) collective-permute-start(bf16[160,512]{1,0:T(8,128)(2,1)S(1)} %add_convert_fusion.8), channel_id=1, source_target_pairs={{0,64},{32,96},{64,0},{96,32},{128,192},{160,224},{192,128},{224,1... | collective-permute-start | bytes 491528 | tf_op jit(solution)/shard_map/ppermute | solution.py:62
  52.7 10.1 %collective-permute-start.21 = (bf16[80,1024]{1,0:T(8,128)(2,1)S(1)}, bf16[80,1024]{1,0:T(8,128)(2,1)S(1)}, u32[]{:S(2)}, u32[]{:S(2)}) collective-permute-start(bf16[80,1024]{1,0:T(8,128)(2,1)S(1)} %get-tuple-element.52.refs_0_), channel_id=1, source_target_pairs={{0,28},{1,29},{2,30},{3,31},{4,24},{5,25},{6,26},{7,27},{8,20},{9,... | collective-permute-start | bytes 491528 | tf_op jit(solution)/shard_map/ppermute | solution.py:62
  58.5 6.9 %collective-permute-start.2 = (bf16[176,512]{1,0:T(8,128)(2,1)S(1)}, bf16[176,512]{1,0:T(8,128)(2,1)S(1)}, u32[]{:S(2)}, u32[]{:S(2)}) collective-permute-start(bf16[176,512]{1,0:T(8,128)(2,1)S(1)} %add_convert_fusion.6), channel_id=1, source_target_pairs={{0,32},{32,0},{64,96},{96,64},{128,160},{160,128},{192,224},{224,1... | collective-permute-start | bytes 540680 | tf_op jit(solution)/shard_map/ppermute | solution.py:62
  59.4 8.0 %collective-permute-start.14 = (bf16[176,512]{1,0:T(8,128)(2,1)S(1)}, bf16[176,512]{1,0:T(8,128)(2,1)S(1)}, u32[]{:S(2)}, u32[]{:S(2)}) collective-permute-start(bf16[176,512]{1,0:T(8,128)(2,1)S(1)} %add_convert_fusion.4), channel_id=1, source_target_pairs={{0,192},{32,224},{64,128},{96,160},{128,64},{160,96},{192,0},{224,... | collective-permute-start | bytes 540680 | tf_op jit(solution)/shard_map/ppermute | solution.py:62
  61.6 6.8 %collective-permute-start.9 = (bf16[160,512]{1,0:T(8,128)(2,1)S(1)}, bf16[160,512]{1,0:T(8,128)(2,1)S(1)}, u32[]{:S(2)}, u32[]{:S(2)}) collective-permute-start(bf16[160,512]{1,0:T(8,128)(2,1)S(1)} %add_convert_fusion.7), channel_id=1, source_target_pairs={{0,64},{32,96},{64,0},{96,32},{128,192},{160,224},{192,128},{224,1... | collective-permute-start | bytes 491528 | tf_op jit(solution)/shard_map/ppermute | solution.py:62
  62.9 8.7 %collective-permute-start.22 = (bf16[80,1024]{1,0:T(8,128)(2,1)S(1)}, bf16[80,1024]{1,0:T(8,128)(2,1)S(1)}, u32[]{:S(2)}, u32[]{:S(2)}) collective-permute-start(bf16[80,1024]{1,0:T(8,128)(2,1)S(1)} %get-tuple-element.54.mine_ref), channel_id=1, source_target_pairs={{0,2},{1,3},{2,0},{3,1},{4,6},{5,7},{6,4},{7,5},{8,10},{9,11},{10,... | collective-permute-start | bytes 491528 | tf_op jit(solution)/shard_map/ppermute | solution.py:62
  65.5 10.6 %collective-permute-start.3 = (bf16[176,512]{1,0:T(8,128)(2,1)S(1)}, bf16[176,512]{1,0:T(8,128)(2,1)S(1)}, u32[]{:S(2)}, u32[]{:S(2)}) collective-permute-start(bf16[176,512]{1,0:T(8,128)(2,1)S(1)} %add_convert_fusion.5), channel_id=1, source_target_pairs={{0,32},{32,0},{64,96},{96,64},{128,160},{160,128},{192,224},{224,1... | collective-permute-start | bytes 540680 | tf_op jit(solution)/shard_map/ppermute | solution.py:62
  67.4 9.4 %collective-permute-start.15 = (bf16[176,512]{1,0:T(8,128)(2,1)S(1)}, bf16[176,512]{1,0:T(8,128)(2,1)S(1)}, u32[]{:S(2)}, u32[]{:S(2)}) collective-permute-start(bf16[176,512]{1,0:T(8,128)(2,1)S(1)} %add_convert_fusion.3), channel_id=1, source_target_pairs={{0,192},{32,224},{64,128},{96,160},{128,64},{160,96},{192,0},{224,... | collective-permute-start | bytes 540680 | tf_op jit(solution)/shard_map/ppermute | solution.py:62
  68.4 13.2 %collective-permute-start.10 = (bf16[320,512]{1,0:T(8,128)(2,1)S(1)}, bf16[320,512]{1,0:T(8,128)(2,1)S(1)}, u32[]{:S(2)}, u32[]{:S(2)}) collective-permute-start(bf16[320,512]{1,0:T(8,128)(2,1)S(1)} %pad_maximum_fusion.5), channel_id=1, source_target_pairs={{0,32},{32,0},{64,96},{96,64},{128,160},{160,128},{192,224},{224,1... | collective-permute-start | bytes 983048 | tf_op jit(solution)/shard_map/ppermute | solution.py:62
  72.4 5.5 %collective-permute-start.23 = (bf16[64,1024]{1,0:T(8,128)(2,1)S(1)}, bf16[64,1024]{1,0:T(8,128)(2,1)S(1)}, u32[]{:S(2)}, u32[]{:S(2)}) collective-permute-start(bf16[64,1024]{1,0:T(8,128)(2,1)S(1)} %get-tuple-element.55), channel_id=1, source_target_pairs={{0,12},{1,13},{2,14},{3,15},{4,8},{5,9},{6,10},{7,11},{8,4},{9,5},... | collective-permute-start | bytes 393224 | tf_op jit(solution)/shard_map/ppermute | solution.py:62
  76.1 12.6 %collective-permute-start.4 = (bf16[352,512]{1,0:T(8,128)(2,1)S(1)}, bf16[352,512]{1,0:T(8,128)(2,1)S(1)}, u32[]{:S(2)}, u32[]{:S(2)}) collective-permute-start(bf16[352,512]{1,0:T(8,128)(2,1)S(1)} %pad_maximum_fusion.3), channel_id=1, source_target_pairs={{0,192},{32,224},{64,128},{96,160},{128,64},{160,96},{192,0},{224,... | collective-permute-start | bytes 1081352 | tf_op jit(solution)/shard_map/ppermute | solution.py:62
  76.9 11.9 %collective-permute-start.16 = (bf16[352,512]{1,0:T(8,128)(2,1)S(1)}, bf16[352,512]{1,0:T(8,128)(2,1)S(1)}, u32[]{:S(2)}, u32[]{:S(2)}) collective-permute-start(bf16[352,512]{1,0:T(8,128)(2,1)S(1)} %pad_maximum_fusion.4), channel_id=1, source_target_pairs={{0,64},{32,96},{64,0},{96,32},{128,192},{160,224},{192,128},{224,1... | collective-permute-start | bytes 1081352 | tf_op jit(solution)/shard_map/ppermute | solution.py:62
  77.9 11.3 %collective-permute-start.24 = (bf16[128,1024]{1,0:T(8,128)(2,1)S(1)}, bf16[128,1024]{1,0:T(8,128)(2,1)S(1)}, u32[]{:S(2)}, u32[]{:S(2)}) collective-permute-start(bf16[128,1024]{1,0:T(8,128)(2,1)S(1)} %pad_maximum_fusion.6), channel_id=1, source_target_pairs={{0,4},{1,5},{2,6},{3,7},{4,0},{5,1},{6,2},{7,3},{8,12},{9,13},{10,... | collective-permute-start | bytes 786440 | tf_op jit(solution)/shard_map/ppermute | solution.py:62
  81.6 27.8 %collective-permute-start.11 = (bf16[640,512]{1,0:T(8,128)(2,1)S(1)}, bf16[640,512]{1,0:T(8,128)(2,1)S(1)}, u32[]{:S(2)}, u32[]{:S(2)}) collective-permute-start(bf16[640,512]{1,0:T(8,128)(2,1)S(1)} %pad_maximum_fusion.2.refs_2_), channel_id=1, source_target_pairs={{0,192},{32,224},{64,128},{96,160},{128,64},{160,96},{192,0},{224,... | collective-permute-start | bytes 1966088 | tf_op jit(solution)/shard_map/ppermute | solution.py:62
  88.7 20.6 %collective-permute-start.5 = (bf16[704,512]{1,0:T(8,128)(2,1)S(1)}, bf16[704,512]{1,0:T(8,128)(2,1)S(1)}, u32[]{:S(2)}, u32[]{:S(2)}) collective-permute-start(bf16[704,512]{1,0:T(8,128)(2,1)S(1)} %pad_maximum_fusion.refs_0_), channel_id=1, source_target_pairs={{0,64},{32,96},{64,0},{96,32},{128,192},{160,224},{192,128},{224,1... | collective-permute-start | bytes 2162696 | tf_op jit(solution)/shard_map/ppermute | solution.py:62
  88.9 20.5 %collective-permute-start.17 = (bf16[704,512]{1,0:T(8,128)(2,1)S(1)}, bf16[704,512]{1,0:T(8,128)(2,1)S(1)}, u32[]{:S(2)}, u32[]{:S(2)}) collective-permute-start(bf16[704,512]{1,0:T(8,128)(2,1)S(1)} %pad_maximum_fusion.1.refs_4_), channel_id=1, source_target_pairs={{0,32},{32,0},{64,96},{96,64},{128,160},{160,128},{192,224},{224,1... | collective-permute-start | bytes 2162696 | tf_op jit(solution)/shard_map/ppermute | solution.py:62
  89.3 20.1 %collective-permute-start.25 = (bf16[256,1024]{1,0:T(8,128)(2,1)S(1)}, bf16[256,1024]{1,0:T(8,128)(2,1)S(1)}, u32[]{:S(2)}, u32[]{:S(2)}) collective-permute-start(bf16[256,1024]{1,0:T(8,128)(2,1)S(1)} %constant_dynamic-update-slice_fusion.refs_6_), channel_id=1, source_target_pairs={{0,1},{1,0},{2,3},{3,2},{4,5},{5,4},{6,7},{7,6},{8,9},{9,8},{10,11... | collective-permute-start | bytes 1572872 | tf_op jit(solution)/shard_map/ppermute | solution.py:62
  89.4 11.0 %collective-permute-start.26 = (f32[1,1024]{1,0:T(1,128)S(1)}, f32[1,1024]{1,0:T(1,128)S(1)}, u32[]{:S(2)}, u32[]{:S(2)}) collective-permute-start(f32[1,1024]{1,0:T(1,128)S(1)} %get-tuple-element.61), channel_id=1, source_target_pairs={{0,32},{32,0},{64,96},{96,64},{128,160},{160,128},{192,224},{224,1... | collective-permute-start | bytes 12296 | tf_op jit(solution)/shard_map/ppermute | solution.py:62
  100.3 3.6 %collective-permute-start.27 = (f32[1,1024]{1,0:T(1,128)S(1)}, f32[1,1024]{1,0:T(1,128)S(1)}, u32[]{:S(2)}, u32[]{:S(2)}) collective-permute-start(f32[1,1024]{1,0:T(1,128)S(1)} %add.113), channel_id=1, source_target_pairs={{0,64},{32,96},{64,0},{96,32},{128,192},{160,224},{192,128},{224,1... | collective-permute-start | bytes 12296 | tf_op jit(solution)/shard_map/ppermute | solution.py:62
  103.9 4.8 %collective-permute-start.28 = (f32[1,1024]{1,0:T(1,128)S(1)}, f32[1,1024]{1,0:T(1,128)S(1)}, u32[]{:S(2)}, u32[]{:S(2)}) collective-permute-start(f32[1,1024]{1,0:T(1,128)S(1)} %add.114), channel_id=1, source_target_pairs={{0,192},{32,224},{64,128},{96,160},{128,64},{160,96},{192,0},{224,... | collective-permute-start | bytes 12296 | tf_op jit(solution)/shard_map/ppermute | solution.py:62
where the time goes:
time: 113 us
  waiting for transfers between devices  44.7 us (40%)
  starting transfers between devices  41.9 us (37%)
  Pallas kernels  17.8 us (16%)
  local copies, waits for them, and re-layouts  5.64 us (5%)
  other arithmetic  1.69 us (1%)
    ppermute x29, waiting for transfers between devices, swap(): return lax.ppermute(value, axis, pairs)  44.7 us
    ppermute x29, starting transfers between devices, swap(): return lax.ppermute(value, axis, pairs)  41.9 us
    pallas_call x1, Pallas kernels, attention(): pl.pallas_call(attention_kernel, grid=(width // HD,), in_specs=[column, c...  7.83 us
    unnamed x24, local copies, waits for them, and re-layouts  5.62 us
    pallas_call x1, Pallas kernels, finish(): pl.pallas_call(finish_kernel, in_specs=[SCALARS, *whole(8)], out_specs=wh...  3.24 us
    pallas_call x1, Pallas kernels, parts(): pl.pallas_call(parts_kernel, in_specs=[SCALARS, *whole(7)], out_specs=who...  3.14 us
    pallas_call x1, Pallas kernels, total_share(): pl.pallas_call(total_kernel, in_specs=[SCALARS, *whole(7)], out_specs=who...  2.47 us
  transfers between devices with their start and end apart: 29, of which 12 were waited for; matrix products, arithmetic and copies ran while one was open for 1% of the time, Pallas kernels for 3%

commit v1 on v0

v1 whole, which is shorter than its diff:
```python
import functools

import jax
import jax.numpy as jnp
from jax import lax
from jax.experimental import pallas as pl
from jax.experimental.pallas import tpu as pltpu
from jax.sharding import PartitionSpec as P

HD = 128
F32 = jnp.float32
BF16 = jnp.bfloat16
EXTRA = 16


def gray(z):
    return z ^ (z >> 1)


RING = {gray(z): z for z in range(8)}


def dp_pairs(flip):
    return [(y * 2 + x, (lambda t: t[0] * 2 + t[1])(flip(y, x))) for y in range(4) for x in range(2)]


def mp_pairs(flip):
    return [
        (z * 4 + h * 2 + c, (lambda t: t[0] * 4 + t[1] * 2 + t[2])(flip(z, h, c)))
        for z in range(8)
        for h in range(2)
        for c in range(2)
    ]


PAIRS = {
    "y1": ("dp", dp_pairs(lambda y, x: (y ^ 1, x))),
    "y3": ("dp", dp_pairs(lambda y, x: (3 - y, x))),
    "x": ("dp", dp_pairs(lambda y, x: (y, 1 - x))),
    "core": ("mp", mp_pairs(lambda z, h, c: (z, h, 1 - c))),
    "g0": ("mp", mp_pairs(lambda z, h, c: (RING[gray(z) ^ 1], h, c))),
    "g1": ("mp", mp_pairs(lambda z, h, c: (RING[gray(z) ^ 2], h, c))),
    "g2": ("mp", mp_pairs(lambda z, h, c: (RING[gray(z) ^ 4], h, c))),
    "xh": ("mp", mp_pairs(lambda z, h, c: (z, 1 - h, c))),
}

ORDERS = (("y1", "y3", "x"), ("y3", "x", "y1"), ("x", "y1", "y3"))
PIECES = (
    (("out", 0, 8), ("value", 0, 3)),
    (("value", 3, 5), ("query", 0, 5)),
    (("query", 5, 3), ("key", 0, 8)),
)
UNIT = 16


def piece_rows(piece):
    return sum(count for _, _, count in piece) * UNIT


def swap(value, step):
    axis, pairs = PAIRS[step]
    return lax.ppermute(value, axis, pairs)


def position():
    return jnp.stack([lax.axis_index("dp").astype(jnp.int32), lax.axis_index("mp").astype(jnp.int32)])


def piece_code(where, i):
    dp = where[0]
    y, x = dp >> 1, dp & 1
    bit = {"y1": (y ^ (y >> 1)) & 1, "y3": y >> 1, "x": x}
    return bit[ORDERS[i][0]] * 4 + bit[ORDERS[i][1]] * 2


def row_code(where):
    mp = where[1]
    z, c = mp >> 2, mp & 1
    g = z ^ (z >> 1)
    return c * 4 + (g & 1) * 2 + ((g >> 1) & 1)


def mm(a, b, ca, cb):
    return lax.dot_general(a, b, (((ca,), (cb,)), ((), ())), preferred_element_type=F32)


def split(g):
    high = g.astype(BF16)
    low = (g - high.astype(F32)).astype(BF16)
    return high, low


def joined(high, low):
    return high.astype(F32) + low.astype(F32)


def gain_rows(g):
    high, low = split(g)
    width = g.shape[1]
    row = lax.broadcasted_iota(jnp.int32, (EXTRA, width), 0)
    high = jnp.broadcast_to(high.astype(F32), (EXTRA, width))
    low = jnp.broadcast_to(low.astype(F32), (EXTRA, width))
    return jnp.where(row == 0, high, jnp.where(row == 1, low, 0.0)).astype(BF16)


def gain_of(rows):
    rows = rows.astype(F32)
    return rows[0:1] + rows[1:2]


def norm_of(rows):
    rows = rows.astype(F32)
    rstd = lax.rsqrt(jnp.mean(rows * rows, axis=-1, keepdims=True) + 1e-06)
    return rows * rstd, rstd


def whole(count):
    return [pl.BlockSpec(memory_space=pltpu.VMEM)] * count


SCALARS = pl.BlockSpec(memory_space=pltpu.SMEM)


def front_kernel(where, gain_ref, *refs):
    sources, refs = refs[:6], refs[6:]
    outs, refs = refs[:6], refs[6:]
    (gq, gk, gv), refs = refs[:3], refs[3:]
    copied, refs = refs[:6], refs[6:]
    (att, grad_att), refs = refs[:2], refs[2:]
    scratch, sem = dict(zip(("out", "value", "query", "key"), refs[:4])), refs[4]
    copies = [pltpu.make_async_copy(a, b, sem.at[i]) for i, (a, b) in enumerate(zip(sources, copied))]
    for copy in copies:
        copy.start()
    og, wo, q_all, k_all, v_all, x = copied
    copies[0].wait()
    copies[1].wait()
    grad_att[...] = mm(og[...], wo[...], 1, 1).astype(BF16)
    for copy in copies[2:]:
        copy.wait()
    for h in range(q_all.shape[1] // HD):
        col = pl.ds(h * HD, HD)
        q, k, v, ga = q_all[:, col], k_all[:, col], v_all[:, col], grad_att[:, col]
        scores = mm(q, k, 1, 1)
        top = jnp.max(scores, axis=-1, keepdims=True)
        e = jnp.exp(scores - top)
        probs = e * (1.0 / jnp.sum(e, axis=-1, keepdims=True))
        low = probs.astype(BF16)
        att[:, col] = mm(low, v, 1, 0).astype(BF16)
        grad_prob = mm(ga, v, 1, 1)
        delta = jnp.sum(probs * grad_prob, axis=-1, keepdims=True)
        grad_score = (probs * (grad_prob - delta)).astype(BF16)
        gq[:, col] = mm(grad_score, k, 1, 0).astype(BF16)
        gv[col, :] = mm(ga, low, 0, 0).astype(BF16)
        gk[col, :] = mm(q, grad_score, 0, 0).astype(BF16)
    scratch["out"][...] = mm(att[...], og[...], 0, 0).astype(BF16)
    unit, _ = norm_of(x[...])
    normed = (unit * gain_ref[...]).astype(BF16)
    scratch["value"][...] = mm(normed, gv[...], 0, 1).astype(BF16)
    scratch["query"][...] = mm(normed, gq[...], 0, 0).astype(BF16)
    scratch["key"][...] = mm(normed, gk[...], 0, 1).astype(BF16)
    for i, piece in enumerate(PIECES):
        code = piece_code(where, i)
        size = piece_rows(piece)
        for p in range(8):
            dst = outs[2 * i] if p >= 4 else outs[2 * i + 1]
            for at, src, rows in spans(piece, p, p ^ code, size):
                if src == "out":
                    dst[pl.ds(at, 64), :] = scratch[src][rows, :512]
                    dst[pl.ds(at + 64, 64), :] = scratch[src][rows, 512:]
                else:
                    dst[pl.ds(at, rows.size), :] = scratch[src][rows, :]


def spans(piece, p, block, size):
    at = (p % 4) * size
    for name, first, count in piece:
        if name == "out":
            yield at, name, pl.ds(pl.multiple_of(block * 64, 64), 64)
        else:
            yield at, name, pl.ds(pl.multiple_of(block * 128 + first * UNIT, UNIT), count * UNIT)
        at += count * UNIT


def front(where, weight, og, wo, q, k, v, x):
    (length, depth), width = x.shape, q.shape[1]
    shapes = []
    for piece in PIECES:
        shapes += [jax.ShapeDtypeStruct((4 * piece_rows(piece), width), BF16)] * 2
    shapes += [jax.ShapeDtypeStruct((length, width), BF16)] + [jax.ShapeDtypeStruct((width, length), BF16)] * 2
    sources = [pltpu.with_memory_space_constraint(a, pltpu.HBM) for a in (og, wo, q, k, v, x)]
    return pl.pallas_call(
        front_kernel,
        in_specs=[SCALARS, *whole(1), *[pl.BlockSpec(memory_space=pltpu.HBM)] * 6],
        out_specs=whole(9),
        out_shape=shapes,
        scratch_shapes=[
            *[pltpu.VMEM(a.shape, BF16) for a in (og, wo, q, k, v, x)],
            *[pltpu.VMEM((length, width), BF16)] * 2,
            pltpu.VMEM((width, depth), BF16),
            *[pltpu.VMEM((depth, width), BF16)] * 3,
            pltpu.SemaphoreType.DMA((6,)),
        ],
        compiler_params=pltpu.CompilerParams(vmem_limit_bytes=40 << 20),
        cost_estimate=pl.CostEstimate(flops=8 << 30, bytes_accessed=16 << 20, transcendentals=1 << 20),
        name="front",
    )(where, weight, *sources)


def total_kernel(where, x_ref, gq_ref, gk_ref, gv_ref, wq_ref, wk_ref, wv_ref, send_ref, keep_ref, gain_ref, low_ref):
    total = mm(gq_ref[...], wq_ref[...], 1, 1)
    total = total + mm(gk_ref[...], wk_ref[...], 0, 1)
    total = total + mm(gv_ref[...], wv_ref[...], 0, 1)
    unit, _ = norm_of(x_ref[...])
    g = jnp.sum(total * unit, axis=0, keepdims=True)
    low_ref[...] = total.astype(BF16)
    for p in range(8):
        block = p ^ row_code(where)
        dst = send_ref if p >= 4 else keep_ref
        dst[pl.ds((p % 4) * 64, 64), :] = low_ref[pl.ds(pl.multiple_of(block * 64, 64), 64), :]
    send_ref[pl.ds(256, EXTRA), :] = gain_rows(g)
    gain_ref[...] = joined(*split(g))


def total_share(where, inputs, gq, gk, gv, wq, wk, wv):
    length, depth = inputs.shape
    half = length // 2
    return pl.pallas_call(
        total_kernel,
        in_specs=[SCALARS, *whole(7)],
        out_specs=whole(3),
        out_shape=[
            jax.ShapeDtypeStruct((half + EXTRA, depth), BF16),
            jax.ShapeDtypeStruct((half, depth), BF16),
            jax.ShapeDtypeStruct((1, depth), F32),
        ],
        scratch_shapes=[pltpu.VMEM((length, depth), BF16)],
        compiler_params=pltpu.CompilerParams(vmem_limit_bytes=20 << 20),
        cost_estimate=pl.CostEstimate(flops=2 << 30, bytes_accessed=8 << 20, transcendentals=0),
        name="total_share",
    )(where, inputs, gq, gk, gv, wq, wk, wv)


def mp_step_kernel(rows, first, gain_ref, *refs):
    *sums, last, send_ref, out_ref = refs
    value = sums[0][pl.ds(first, rows), :].astype(F32)
    for ref in (*sums[1:], last):
        value = value + ref[pl.ds(first, rows), :].astype(F32)
    send_ref[pl.ds(0, rows), :] = value.astype(BF16)
    got = last[pl.ds(last.shape[0] - EXTRA, EXTRA), :]
    g = gain_ref[...] + gain_of(got)
    send_ref[pl.ds(rows, EXTRA), :] = gain_rows(g)
    out_ref[...] = joined(*split(g))


def mp_step(gain, sums, rows, first):
    depth = gain.shape[1]
    return pl.pallas_call(
        functools.partial(mp_step_kernel, rows, first),
        in_specs=whole(1 + len(sums)),
        out_specs=whole(2),
        out_shape=[jax.ShapeDtypeStruct((rows + EXTRA, depth), BF16), jax.ShapeDtypeStruct((1, depth), F32)],
        compiler_params=pltpu.CompilerParams(vmem_limit_bytes=4 << 20),
        cost_estimate=pl.CostEstimate(flops=1 << 10, bytes_accessed=1 << 10, transcendentals=0),
        name="mp_step",
    )(gain, *sums)


def rows_kernel(where, x_ref, og_ref, weight_ref, gain_ref, mine_ref, got_ref, out_ref, sum_ref):
    n = out_ref.shape[0]
    gradient = mine_ref[pl.ds(0, n), :].astype(F32) + got_ref[pl.ds(0, n), :].astype(F32)
    unit, rstd = norm_of(x_ref[...])
    scaled = gradient * weight_ref[...]
    inner = jnp.mean(scaled * unit, axis=-1, keepdims=True)
    out_ref[...] = (og_ref[...].astype(F32) + rstd * (scaled - unit * inner)).astype(BF16)
    g = gain_ref[...] + gain_of(got_ref[pl.ds(n, EXTRA), :])
    for j in range(8):
        for i in range(8):
            sum_ref[i, pl.ds(j, 1), :] = g[:, j * 128 : (j + 1) * 128]


def own_rows(where, inputs, og, weight, gain, mine, got):
    n, depth = mine.shape[0] - EXTRA, mine.shape[1]

    def fixed(shape):
        return pl.BlockSpec(shape, lambda i, c: (0, 0))

    row = pl.BlockSpec((n, depth), lambda i, c: (row_code(c), 0))
    return pl.pallas_call(
        rows_kernel,
        grid_spec=pltpu.PrefetchScalarGridSpec(
            num_scalar_prefetch=1,
            grid=(1,),
            in_specs=[row, row, fixed((1, depth)), fixed((1, depth)), fixed(mine.shape), fixed(got.shape)],
            out_specs=[fixed((n, depth)), pl.BlockSpec((8, 8, 128), lambda i, c: (0, 0, 0))],
        ),
        out_shape=[jax.ShapeDtypeStruct((n, depth), BF16), jax.ShapeDtypeStruct((8, 8, 128), F32)],
        compiler_params=pltpu.CompilerParams(vmem_limit_bytes=4 << 20),
        cost_estimate=pl.CostEstimate(flops=1 << 10, bytes_accessed=1 << 10, transcendentals=0),
        name="own_rows",
    )(where, inputs, og, weight, gain, mine, got)


ANYWHERE = pl.BlockSpec(memory_space=pl.ANY)


def place_kernel(late, where, *refs):
    halves, outs, sem = refs[:3], refs[-5:-1], refs[-1]
    named = dict(zip(("query", "key", "value", "out"), outs))
    copies = []
    for i, piece in enumerate(PIECES):
        code = piece_code(where, i)
        for p in range(4 * late, 4 * late + 4):
            for at, name, rows in spans(piece, p, p ^ code, piece_rows(piece)):
                if name == "out":
                    pairs = [(at, 64, named[name].at[rows, pl.ds(0, 512)]), (at + 64, 64, named[name].at[rows, pl.ds(512, 512)])]
                else:
                    pairs = [(at, rows.size, named[name].at[rows, :])]
                for first, n, dst in pairs:
                    copy = pltpu.make_async_copy(halves[i].at[pl.ds(first, n), :], dst, sem.at[len(copies)])
                    copy.start()
                    copies.append(copy)
    for copy in copies:
        copy.wait()


def place(late, where, halves, outs, depth, width):
    shapes = [jax.ShapeDtypeStruct((depth, width), BF16)] * 3 + [jax.ShapeDtypeStruct((width, depth), BF16)]
    return pl.pallas_call(
        functools.partial(place_kernel, late),
        in_specs=[SCALARS, *[ANYWHERE] * (3 + len(outs))],
        out_specs=[ANYWHERE] * 4,
        out_shape=shapes,
        scratch_shapes=[pltpu.SemaphoreType.DMA((28,))],
        input_output_aliases={4 + i: i for i in range(len(outs))},
        compiler_params=pltpu.CompilerParams(vmem_limit_bytes=1 << 20),
        cost_estimate=pl.CostEstimate(flops=1 << 10, bytes_accessed=4 << 20, transcendentals=0),
        name="place_late" if late else "place_early",
    )(where, *halves, *outs)


def place_rows_kernel(where, low_ref, high_ref, out_ref, sem):
    code = row_code(where)
    copies = []
    for p in range(8):
        src = high_ref if p >= 4 else low_ref
        rows = pl.ds(pl.multiple_of((p ^ code) * 64, 64), 64)
        copy = pltpu.make_async_copy(src.at[pl.ds((p % 4) * 64, 64), :], out_ref.at[rows, :], sem.at[p])
        copy.start()
        copies.append(copy)
    for copy in copies:
        copy.wait()


def place_rows(where, low, high):
    return pl.pallas_call(
        place_rows_kernel,
        in_specs=[SCALARS, ANYWHERE, ANYWHERE],
        out_specs=ANYWHERE,
        out_shape=jax.ShapeDtypeStruct((2 * low.shape[0], low.shape[1]), BF16),
        scratch_shapes=[pltpu.SemaphoreType.DMA((8,))],
        compiler_params=pltpu.CompilerParams(vmem_limit_bytes=1 << 20),
        cost_estimate=pl.CostEstimate(flops=1 << 10, bytes_accessed=2 << 20, transcendentals=0),
        name="place_rows",
    )(where, low, high)


def plus(*values):
    total = values[0].astype(F32)
    for value in values[1:]:
        total = total + value.astype(F32)
    return total.astype(BF16)


def shards(
    inputs,
    norm_gain_vector,
    query_saved,
    key_saved,
    value_saved,
    w_query,
    w_key,
    w_value,
    w_out,
    output_gradient,
):
    length, depth = inputs.shape
    width = query_saved.shape[1]
    where = position()
    weight = norm_gain_vector.reshape(1, depth)
    *pieces, gq, gk, gv = front(where, weight, output_gradient, w_out, query_saved, key_saved, value_saved, inputs)
    m_send, m_keep, gain = total_share(where, inputs, gq, gk, gv, w_query, w_key, w_value)

    sends, keeps = pieces[0::2], pieces[1::2]
    sizes = [piece_rows(piece) for piece in PIECES]
    first = [swap(s, o[0]) for s, o in zip(sends, ORDERS)]
    r1 = swap(m_send, "core")
    send, gain = mp_step(gain, (m_keep, r1), 128, 128)
    r2 = swap(send, "g0")
    second = [
        swap(plus(k[2 * n :], r[2 * n :]), o[1]) for k, r, o, n in zip(keeps, first, ORDERS, sizes)
    ]
    send, gain = mp_step(gain, (m_keep, r1, r2), 64, 64)
    r3 = swap(send, "g1")
    mine = [plus(k[: 2 * n], r[: 2 * n], s) for k, r, s, n in zip(keeps, first, second, sizes)]
    third = [swap(v, o[2]) for v, o in zip(mine, ORDERS)]
    send, gain = mp_step(gain, (m_keep, r1, r2, r3), 64, 0)
    r4 = swap(send, "g2")
    quarter = [plus(v, t) for v, t in zip(mine, third)]
    send, gain = mp_step(gain, (send, r4), 64, 0)
    r5 = swap(send, "xh")
    rows, gains = own_rows(where, inputs, output_gradient, weight, gain, send, r5)
    gains = lax.all_to_all(gains, "dp", 0, 0)
    back = [swap(v, o[1]) for v, o in zip(quarter, ORDERS)]
    half = [jnp.concatenate([v, b]) for v, b in zip(quarter, back)]
    *half, gains = lax.optimization_barrier((*half, gains))
    last = [swap(v, o[0]) for v, o in zip(half, ORDERS)]
    outs = place(0, where, half, (), depth, width)
    for step in ("g1", "g0"):
        rows = jnp.concatenate([rows, swap(rows, step)])
    grad_inputs = place_rows(where, rows, swap(rows, "core"))
    outs = place(1, where, last, outs, depth, width)
    return (grad_inputs, *outs, jnp.sum(gains, axis=0).reshape(depth))


def solution(mesh):
    return jax.shard_map(
        shards,
        mesh=mesh,
        in_specs=(
            P("dp", None),
            P(),
            P("dp", "mp"),
            P("dp", "mp"),
            P("dp", "mp"),
            P(None, "mp"),
            P(None, "mp"),
            P(None, "mp"),
            P("mp", None),
            P("dp", None),
        ),
        out_specs=(P("dp", None), P(None, "mp"), P(None, "mp"), P(None, "mp"), P("mp", None), P()),
        check_vma=False,
    )
```

time: 113 us -> 162 us (1.43)
  the two profiles are of different devices: /device:TPU:34 before, /device:TPU:1 now
where the time goes in v1:
time: 162 us
  Pallas kernels  77.2 us (48%)
  starting transfers between devices  54.9 us (34%)
  waiting for transfers between devices  23.9 us (15%)
  other arithmetic  3.46 us (2%)
  local copies, waits for them, and re-layouts  1.7 us (1%)
    ppermute x23, starting transfers between devices, swap(): return lax.ppermute(value, axis, pairs)  51.6 us
    pallas_call x2, Pallas kernels, place(): pl.pallas_call(functools.partial(place_kernel, late), in_specs=[SCALARS,...  45.7 us
    ppermute x23, waiting for transfers between devices, swap(): return lax.ppermute(value, axis, pairs)  23.9 us
    pallas_call x1, Pallas kernels, place_rows(): pl.pallas_call(place_rows_kernel, in_specs=[SCALARS, ANYWHERE, ANYWHERE],...  17.6 us
    pallas_call x1, Pallas kernels, front(): pl.pallas_call(front_kernel, in_specs=[SCALARS, *whole(1), *[pl.BlockSpec...  9.71 us
    all_to_all x1, starting transfers between devices, shards(): gains = lax.all_to_all(gains, 'dp', 0, 0)  3.34 us
  transfers between devices with their start and end apart: 24, of which 8 were waited for; matrix products, arithmetic and copies ran while one was open for 3% of the time, Pallas kernels for 15%

profile of v1, /device:TPU:1, one launch (start us, length us, event | category | flops | bytes accessed | tf_op | source)
XLA Modules:
  0.0 162.1 jit_solution(14025338803728700115)
XLA Ops:
  0.6 0.1 pad_add_fusion.where
  0.7 0.7 copy-done.2
  1.4 9.7 %front.1 = (bf16[704,512]{1,0:T(8,128)(2,1)S(1)}, bf16[704,512]{1,0:T(8,128)(2,1)S(1)}, bf16[640,512]{1,0:T(8,128)(2,1)S(1)}, bf16[640,512]{1,0:T(8,128)(2,1)S(1...) custom-call(s32[2]{0:T(128)S(1)} %pad_add_fusion.where, ...), custom_call_target="tpu_custom_call" | custom-call | flops 8589934592 | bytes 16777216 | tf_op jit(solution)/shard_map/front/pallas_call | solution.py:191
  11.1 3.6 %collective-permute-start.12 = (bf16[640,512]{1,0:T(8,128)(2,1)S(1)}, bf16[640,512]{1,0:T(8,128)(2,1)S(1)}, u32[]{:S(2)}, u32[]{:S(2)}) collective-permute-start(bf16[640,512]{1,0:T(8,128)(2,1)S(1)} %get-tuple-element.58), channel_id=1, source_target_pairs={{0,192},{32,224},{64,128},{96,160},{128,64},{160,96},{192,0},{224,... | collective-permute-start | bytes 1966088 | tf_op jit(solution)/shard_map/ppermute | solution.py:62
  14.8 2.5 %total_share.1 = (bf16[272,1024]{1,0:T(8,128)(2,1)S(1)}, bf16[256,1024]{1,0:T(8,128)(2,1)S(1)}, f32[1,1024]{1,0:T(1,128)S(1)}) custom-call(s32[2]{0:T(128)S(1)} %pad_add_fusion.where, bf16[512,1024]{1,0:T(8,128)(2,1)S(1)} %copy-done, bf16[512,512]{1,0:T(8,128)(2,1)S(1)} %get-tuple-element.40.gq_ref, bf16[512,512]{1,0:T(8,128)(2,1)S(1)} %get-tuple-element.41.gk_ref, ...), custom_call_target="tpu_custom_call" | custom-call | flops 2147483648 | bytes 8388608 | tf_op jit(solution)/shard_map/total_share/pallas_call | solution.py:227
  17.3 1.0 collective-permute-start
  18.3 1.2 collective-permute-start.16
  19.5 0.0 collective-permute-start.8
  19.6 0.4 collective-permute-done.refs_1_
  19.9 0.1 mp_step.4
  20.0 1.7 %collective-permute-start.1 = (bf16[144,1024]{1,0:T(8,128)(2,1)S(1)}, bf16[144,1024]{1,0:T(8,128)(2,1)S(1)}, u32[]{:S(2)}, u32[]{:S(2)}) collective-permute-start(bf16[144,1024]{1,0:T(8,128)(2,1)S(1)} %get-tuple-element.47), channel_id=1, source_target_pairs={{0,4},{1,5},{2,6},{3,7},{4,0},{5,1},{6,2},{7,3},{8,12},{9,13},{10,... | collective-permute-start | bytes 884744 | tf_op jit(solution)/shard_map/ppermute | solution.py:62
  21.7 6.5 %collective-permute-done.12 = bf16[640,512]{1,0:T(8,128)(2,1)S(1)} collective-permute-done((bf16[640,512]{1,0:T(8,128)(2,1)S(1)}, bf16[640,512]{1,0:T(8,128)(2,1)S(1)}, u32[]{:S(2)}, u32[]{:S(2)}) %collective-permute-start.12) | collective-permute-done | bytes 655392 | tf_op jit(solution)/shard_map/ppermute | solution.py:62
  28.2 0.1 add_convert_fusion.8
  28.3 2.1 %collective-permute-start.13 = (bf16[320,512]{1,0:T(8,128)(2,1)S(1)}, bf16[320,512]{1,0:T(8,128)(2,1)S(1)}, u32[]{:S(2)}, u32[]{:S(2)}) collective-permute-start(bf16[320,512]{1,0:T(8,128)(2,1)S(1)} %add_convert_fusion.8), channel_id=1, source_target_pairs={{0,32},{32,0},{64,96},{96,64},{128,160},{160,128},{192,224},{224,1... | collective-permute-start | bytes 983048 | tf_op jit(solution)/shard_map/ppermute | solution.py:62
  30.4 5.6 %collective-permute-done.16 = bf16[704,512]{1,0:T(8,128)(2,1)S(1)} collective-permute-done((bf16[704,512]{1,0:T(8,128)(2,1)S(1)}, bf16[704,512]{1,0:T(8,128)(2,1)S(1)}, u32[]{:S(2)}, u32[]{:S(2)}) %collective-permute-start.16) | collective-permute-done | bytes 720928 | tf_op jit(solution)/shard_map/ppermute | solution.py:62
  36.0 0.1 add_convert_fusion.2
  36.1 0.3 collective-permute-start.17
  36.4 0.5 collective-permute-done.8
  36.9 0.1 add_convert_fusion.5
  37.0 1.3 collective-permute-start.9
  38.3 0.0 collective-permute-done.1.refs_2_
  38.3 0.1 mp_step.5
  38.4 3.4 %collective-permute-start.2 = (bf16[80,1024]{1,0:T(8,128)(2,1)S(1)}, bf16[80,1024]{1,0:T(8,128)(2,1)S(1)}, u32[]{:S(2)}, u32[]{:S(2)}) collective-permute-start(bf16[80,1024]{1,0:T(8,128)(2,1)S(1)} %get-tuple-element.49), channel_id=1, source_target_pairs={{0,12},{1,13},{2,14},{3,15},{4,8},{5,9},{6,10},{7,11},{8,4},{9,5},... | collective-permute-start | bytes 491528 | tf_op jit(solution)/shard_map/ppermute | solution.py:62
  41.7 1.3 collective-permute-done.13
  43.0 0.1 add_convert_fusion.7
  43.2 0.1 collective-permute-start.14
  43.3 1.3 collective-permute-done.2.refs_3_
  44.5 0.1 mp_step.6
  44.6 4.6 %collective-permute-start.3 = (bf16[80,1024]{1,0:T(8,128)(2,1)S(1)}, bf16[80,1024]{1,0:T(8,128)(2,1)S(1)}, u32[]{:S(2)}, u32[]{:S(2)}) collective-permute-start(bf16[80,1024]{1,0:T(8,128)(2,1)S(1)} %get-tuple-element.51.refs_0_), channel_id=1, source_target_pairs={{0,28},{1,29},{2,30},{3,31},{4,24},{5,25},{6,26},{7,27},{8,20},{9,... | collective-permute-start | bytes 491528 | tf_op jit(solution)/shard_map/ppermute | solution.py:62
  49.2 0.1 add_convert_fusion.1
  49.4 0.0 copy-start.1
  49.4 2.7 %collective-permute-start.18 = (bf16[352,512]{1,0:T(8,128)(2,1)S(1)}, bf16[352,512]{1,0:T(8,128)(2,1)S(1)}, u32[]{:S(2)}, u32[]{:S(2)}) collective-permute-start(bf16[352,512]{1,0:T(8,128)(2,1)S(1)} %add_convert_fusion.1), channel_id=1, source_target_pairs={{0,192},{32,224},{64,128},{96,160},{128,64},{160,96},{192,0},{224,... | collective-permute-start | bytes 1081352 | tf_op jit(solution)/shard_map/ppermute | solution.py:62
  52.0 0.1 add_convert_fusion.4
  52.2 0.8 collective-permute-start.10
  53.0 0.0 collective-permute-done.3.refs_1_
  53.0 0.1 mp_step.7
  53.0 2.5 %collective-permute-start.4 = (bf16[80,1024]{1,0:T(8,128)(2,1)S(1)}, bf16[80,1024]{1,0:T(8,128)(2,1)S(1)}, u32[]{:S(2)}, u32[]{:S(2)}) collective-permute-start(bf16[80,1024]{1,0:T(8,128)(2,1)S(1)} %get-tuple-element.53.mine_ref), channel_id=1, source_target_pairs={{0,2},{1,3},{2,0},{3,1},{4,6},{5,7},{6,4},{7,5},{8,10},{9,11},{10,... | collective-permute-start | bytes 491528 | tf_op jit(solution)/shard_map/ppermute | solution.py:62
  55.6 0.1 add_convert_fusion.6
  55.7 0.2 collective-permute-start.15
  55.9 7.8 %collective-permute-done.4.got_ref = bf16[80,1024]{1,0:T(8,128)(2,1)S(1)} collective-permute-done((bf16[80,1024]{1,0:T(8,128)(2,1)S(1)}, bf16[80,1024]{1,0:T(8,128)(2,1)S(1)}, u32[]{:S(2)}, u32[]{:S(2)}) %collective-permute-start.4) | collective-permute-done | bytes 163872 | tf_op jit(solution)/shard_map/ppermute | solution.py:62
  63.7 1.3 own_rows.1
  65.0 3.3 %all-to-all-start = ((f32[8,8,128]{2,1,0:T(8,128)}), f32[8,8,128]{2,1,0:T(8,128)S(1)}, u32[]{:S(2)}, u32[]{:S(2)}) async-start(f32[8,8,128]{2,1,0:T(8,128)} %get-tuple-element.61), calls=%async_computation | async-start | bytes 65536 | tf_op jit(solution)/shard_map/all_to_all | solution.py:412
  68.3 1.7 %collective-permute-start.5 = (bf16[64,1024]{1,0:T(8,128)(2,1)S(1)}, bf16[64,1024]{1,0:T(8,128)(2,1)S(1)}, u32[]{:S(2)}, u32[]{:S(2)}) collective-permute-start(bf16[64,1024]{1,0:T(8,128)(2,1)S(1)} %get-tuple-element.54), channel_id=1, source_target_pairs={{0,12},{1,13},{2,14},{3,15},{4,8},{5,9},{6,10},{7,11},{8,4},{9,5},... | collective-permute-start | bytes 393224 | tf_op jit(solution)/shard_map/ppermute | solution.py:62
  70.0 0.0 collective-permute-done.18
  70.1 0.1 add_convert_fusion
  70.2 1.4 collective-permute-start.19
  71.5 0.1 add_convert_fusion.3
  71.6 1.9 %collective-permute-start.11 = (bf16[352,512]{1,0:T(8,128)(2,1)S(1)}, bf16[352,512]{1,0:T(8,128)(2,1)S(1)}, u32[]{:S(2)}, u32[]{:S(2)}) collective-permute-start(bf16[352,512]{1,0:T(8,128)(2,1)S(1)} %add_convert_fusion.3), channel_id=1, source_target_pairs={{0,192},{32,224},{64,128},{96,160},{128,64},{160,96},{192,0},{224,... | collective-permute-start | bytes 1081352 | tf_op jit(solution)/shard_map/ppermute | solution.py:62
  73.5 0.5 collective-permute-done.5
  74.0 0.7 pad_maximum_fusion.3
  74.8 3.3 %collective-permute-start.6 = (bf16[128,1024]{1,0:T(8,128)(2,1)}, bf16[128,1024]{1,0:T(8,128)(2,1)}, u32[]{:S(2)}, u32[]{:S(2)}) collective-permute-start(bf16[128,1024]{1,0:T(8,128)(2,1)} %pad_maximum_fusion.3), channel_id=1, source_target_pairs={{0,4},{1,5},{2,6},{3,7},{4,0},{5,1},{6,2},{7,3},{8,12},{9,13},{10,... | collective-permute-start | bytes 786440 | tf_op jit(solution)/shard_map/ppermute | solution.py:62
  78.1 0.0 collective-permute-done.15
  78.1 1.0 pad_maximum_fusion.2.refs_1_
  79.2 0.0 collective-permute-done.11
  79.2 0.0 all-to-all-done
  79.3 1.0 collective-permute-start.20
  80.2 1.2 collective-permute-start.22
  81.4 1.8 %collective-permute-start.21 = (bf16[640,512]{1,0:T(8,128)(2,1)S(1)}, bf16[640,512]{1,0:T(8,128)(2,1)}, u32[]{:S(2)}, u32[]{:S(2)}) collective-permute-start(bf16[640,512]{1,0:T(8,128)(2,1)S(1)} %pad_maximum_fusion.2.refs_1_), channel_id=1, source_target_pairs={{0,192},{32,224},{64,128},{96,160},{128,64},{160,96},{192,0},{224,... | collective-permute-start | bytes 1966088 | tf_op jit(solution)/shard_map/ppermute | solution.py:62
  83.2 1.0 constant_dynamic-update-slice_fusion.low_ref
  84.2 13.8 %collective-permute-start.7 = (bf16[256,1024]{1,0:T(8,128)(2,1)S(1)}, bf16[256,1024]{1,0:T(8,128)(2,1)}, u32[]{:S(2)}, u32[]{:S(2)}) collective-permute-start(bf16[256,1024]{1,0:T(8,128)(2,1)S(1)} %constant_dynamic-update-slice_fusion.low_ref), channel_id=1, source_target_pairs={{0,1},{1,0},{2,3},{3,2},{4,5},{5,4},{6,7},{7,6},{8,9},{9,8},{10,11... | collective-permute-start | bytes 1572872 | tf_op jit(solution)/shard_map/ppermute | solution.py:62
  98.0 2.1 %place_early.1 = (bf16[1024,512]{1,0:T(8,128)(2,1)}, bf16[1024,512]{1,0:T(8,128)(2,1)}, bf16[1024,512]{1,0:T(8,128)(2,1)}, bf16[512,1024]{1,0:T(8,128)(2,1)}) custom-call(s32[2]{0:T(128)S(1)} %pad_add_fusion.where, bf16[704,512]{1,0:T(8,128)(2,1)S(1)} %pad_maximum_fusion.refs_0_, bf16[640,512]{1,0:T(8,128)(2,1)S(1)} %pad_maximum_fusion.2.refs_1_, ...), custom_call_target="tpu_custom_call" | custom-call | flops 1024 | bytes 4194304 | tf_op jit(solution)/shard_map/place_early/pallas_call | solution.py:328
  100.1 0.6 reduce_sum.9
  100.7 17.6 %place_rows.1 = bf16[512,1024]{1,0:T(8,128)(2,1)} custom-call(s32[2]{0:T(128)S(1)} %pad_add_fusion.where, bf16[256,1024]{1,0:T(8,128)(2,1)S(1)} %constant_dynamic-update-slice_fusion.low_ref, bf16[256,1024]{1,0:T(8,128)(2,1)} %collective-permute-done.7.high_ref), custom_call_target="tpu_custom_call" | custom-call | flops 1024 | bytes 2097152 | tf_op jit(solution)/shard_map/place_rows/pallas_call | solution.py:355
  118.4 43.6 %place_late.1 = (bf16[1024,512]{1,0:T(8,128)(2,1)}, bf16[1024,512]{1,0:T(8,128)(2,1)}, bf16[1024,512]{1,0:T(8,128)(2,1)}, bf16[512,1024]{1,0:T(8,128)(2,1)}) custom-call(s32[2]{0:T(128)S(1)} %pad_add_fusion.where, bf16[704,512]{1,0:T(8,128)(2,1)S(1)} %collective-permute-done.20.refs_0_, ...), custom_call_target="tpu_custom_call", output_to_operand_aliasing={{0}: (4, {}), {1}: (5, {}), {2}: (6, {}), {3}: (7, {})} | custom-call | flops 1024 | bytes 4194304 | tf_op jit(solution)/shard_map/place_late/pallas_call | solution.py:328
  (24 shorter events, 0.2 us)
Async XLA Ops:
  0.7 0.7 copy-start.2
  1.4 13.4 %copy-start = (bf16[512,1024]{1,0:T(8,128)(2,1)S(1)}, bf16[512,1024]{1,0:T(8,128)(2,1)}, u32[]{:S(2)}) copy-start(bf16[512,1024]{1,0:T(8,128)(2,1)} %x_ref.3) | copy-start | bytes 3145732
  1.4 13.4 %copy-start.3 = (bf16[1024,512]{1,0:T(8,128)(2,1)S(1)}, bf16[1024,512]{1,0:T(8,128)(2,1)}, u32[]{:S(2)}) copy-start(bf16[1024,512]{1,0:T(8,128)(2,1)} %wq_ref.1) | copy-start | bytes 3145732
  1.4 13.4 %copy-start.4 = (bf16[1024,512]{1,0:T(8,128)(2,1)S(1)}, bf16[1024,512]{1,0:T(8,128)(2,1)}, u32[]{:S(2)}) copy-start(bf16[1024,512]{1,0:T(8,128)(2,1)} %wk_ref.1) | copy-start | bytes 3145732
  1.4 13.4 %copy-start.5 = (bf16[1024,512]{1,0:T(8,128)(2,1)S(1)}, bf16[1024,512]{1,0:T(8,128)(2,1)}, u32[]{:S(2)}) copy-start(bf16[1024,512]{1,0:T(8,128)(2,1)} %wv_ref.1) | copy-start | bytes 3145732
  11.1 17.1 %collective-permute-start.12 = (bf16[640,512]{1,0:T(8,128)(2,1)S(1)}, bf16[640,512]{1,0:T(8,128)(2,1)S(1)}, u32[]{:S(2)}, u32[]{:S(2)}) collective-permute-start(bf16[640,512]{1,0:T(8,128)(2,1)S(1)} %get-tuple-element.58), channel_id=1, source_target_pairs={{0,192},{32,224},{64,128},{96,160},{128,64},{160,96},{192,0},{224,... | collective-permute-start | bytes 1966088 | tf_op jit(solution)/shard_map/ppermute | solution.py:62
  17.3 2.6 %collective-permute-start = (bf16[272,1024]{1,0:T(8,128)(2,1)S(1)}, bf16[272,1024]{1,0:T(8,128)(2,1)S(1)}, u32[]{:S(2)}, u32[]{:S(2)}) collective-permute-start(bf16[272,1024]{1,0:T(8,128)(2,1)S(1)} %get-tuple-element.45), channel_id=1, source_target_pairs={{0,1},{1,0},{2,3},{3,2},{4,5},{5,4},{6,7},{7,6},{8,9},{9,8},{10,11... | collective-permute-start | bytes 1671176 | tf_op jit(solution)/shard_map/ppermute | solution.py:62
  18.3 17.7 %collective-permute-start.16 = (bf16[704,512]{1,0:T(8,128)(2,1)S(1)}, bf16[704,512]{1,0:T(8,128)(2,1)S(1)}, u32[]{:S(2)}, u32[]{:S(2)}) collective-permute-start(bf16[704,512]{1,0:T(8,128)(2,1)S(1)} %get-tuple-element.60), channel_id=1, source_target_pairs={{0,32},{32,0},{64,96},{96,64},{128,160},{160,128},{192,224},{224,1... | collective-permute-start | bytes 2162696 | tf_op jit(solution)/shard_map/ppermute | solution.py:62
  19.5 17.4 %collective-permute-start.8 = (bf16[704,512]{1,0:T(8,128)(2,1)S(1)}, bf16[704,512]{1,0:T(8,128)(2,1)S(1)}, u32[]{:S(2)}, u32[]{:S(2)}) collective-permute-start(bf16[704,512]{1,0:T(8,128)(2,1)S(1)} %get-tuple-element.56), channel_id=1, source_target_pairs={{0,64},{32,96},{64,0},{96,32},{128,192},{160,224},{192,128},{224,1... | collective-permute-start | bytes 2162696 | tf_op jit(solution)/shard_map/ppermute | solution.py:62
  20.0 18.3 %collective-permute-start.1 = (bf16[144,1024]{1,0:T(8,128)(2,1)S(1)}, bf16[144,1024]{1,0:T(8,128)(2,1)S(1)}, u32[]{:S(2)}, u32[]{:S(2)}) collective-permute-start(bf16[144,1024]{1,0:T(8,128)(2,1)S(1)} %get-tuple-element.47), channel_id=1, source_target_pairs={{0,4},{1,5},{2,6},{3,7},{4,0},{5,1},{6,2},{7,3},{8,12},{9,13},{10,... | collective-permute-start | bytes 884744 | tf_op jit(solution)/shard_map/ppermute | solution.py:62
  28.3 14.8 %collective-permute-start.13 = (bf16[320,512]{1,0:T(8,128)(2,1)S(1)}, bf16[320,512]{1,0:T(8,128)(2,1)S(1)}, u32[]{:S(2)}, u32[]{:S(2)}) collective-permute-start(bf16[320,512]{1,0:T(8,128)(2,1)S(1)} %add_convert_fusion.8), channel_id=1, source_target_pairs={{0,32},{32,0},{64,96},{96,64},{128,160},{160,128},{192,224},{224,1... | collective-permute-start | bytes 983048 | tf_op jit(solution)/shard_map/ppermute | solution.py:62
  36.1 13.1 %collective-permute-start.17 = (bf16[352,512]{1,0:T(8,128)(2,1)S(1)}, bf16[352,512]{1,0:T(8,128)(2,1)S(1)}, u32[]{:S(2)}, u32[]{:S(2)}) collective-permute-start(bf16[352,512]{1,0:T(8,128)(2,1)S(1)} %add_convert_fusion.2), channel_id=1, source_target_pairs={{0,64},{32,96},{64,0},{96,32},{128,192},{160,224},{192,128},{224,1... | collective-permute-start | bytes 1081352 | tf_op jit(solution)/shard_map/ppermute | solution.py:62
  37.0 15.0 %collective-permute-start.9 = (bf16[352,512]{1,0:T(8,128)(2,1)S(1)}, bf16[352,512]{1,0:T(8,128)(2,1)S(1)}, u32[]{:S(2)}, u32[]{:S(2)}) collective-permute-start(bf16[352,512]{1,0:T(8,128)(2,1)S(1)} %add_convert_fusion.5), channel_id=1, source_target_pairs={{0,192},{32,224},{64,128},{96,160},{128,64},{160,96},{192,0},{224,... | collective-permute-start | bytes 1081352 | tf_op jit(solution)/shard_map/ppermute | solution.py:62
  38.4 6.2 %collective-permute-start.2 = (bf16[80,1024]{1,0:T(8,128)(2,1)S(1)}, bf16[80,1024]{1,0:T(8,128)(2,1)S(1)}, u32[]{:S(2)}, u32[]{:S(2)}) collective-permute-start(bf16[80,1024]{1,0:T(8,128)(2,1)S(1)} %get-tuple-element.49), channel_id=1, source_target_pairs={{0,12},{1,13},{2,14},{3,15},{4,8},{5,9},{6,10},{7,11},{8,4},{9,5},... | collective-permute-start | bytes 491528 | tf_op jit(solution)/shard_map/ppermute | solution.py:62
  43.2 12.4 %collective-permute-start.14 = (bf16[320,512]{1,0:T(8,128)(2,1)S(1)}, bf16[320,512]{1,0:T(8,128)(2,1)S(1)}, u32[]{:S(2)}, u32[]{:S(2)}) collective-permute-start(bf16[320,512]{1,0:T(8,128)(2,1)S(1)} %add_convert_fusion.7), channel_id=1, source_target_pairs={{0,64},{32,96},{64,0},{96,32},{128,192},{160,224},{192,128},{224,1... | collective-permute-start | bytes 983048 | tf_op jit(solution)/shard_map/ppermute | solution.py:62
  44.6 8.3 %collective-permute-start.3 = (bf16[80,1024]{1,0:T(8,128)(2,1)S(1)}, bf16[80,1024]{1,0:T(8,128)(2,1)S(1)}, u32[]{:S(2)}, u32[]{:S(2)}) collective-permute-start(bf16[80,1024]{1,0:T(8,128)(2,1)S(1)} %get-tuple-element.51.refs_0_), channel_id=1, source_target_pairs={{0,28},{1,29},{2,30},{3,31},{4,24},{5,25},{6,26},{7,27},{8,20},{9,... | collective-permute-start | bytes 491528 | tf_op jit(solution)/shard_map/ppermute | solution.py:62
  49.4 14.3 %copy-start.1 = (bf16[512,1024]{1,0:T(8,128)(2,1)S(1)}, bf16[512,1024]{1,0:T(8,128)(2,1)}, u32[]{:S(2)}) copy-start(bf16[512,1024]{1,0:T(8,128)(2,1)} %og_ref.1) | copy-start | bytes 3145732
  49.4 20.7 %collective-permute-start.18 = (bf16[352,512]{1,0:T(8,128)(2,1)S(1)}, bf16[352,512]{1,0:T(8,128)(2,1)S(1)}, u32[]{:S(2)}, u32[]{:S(2)}) collective-permute-start(bf16[352,512]{1,0:T(8,128)(2,1)S(1)} %add_convert_fusion.1), channel_id=1, source_target_pairs={{0,192},{32,224},{64,128},{96,160},{128,64},{160,96},{192,0},{224,... | collective-permute-start | bytes 1081352 | tf_op jit(solution)/shard_map/ppermute | solution.py:62
  52.2 19.3 %collective-permute-start.10 = (bf16[352,512]{1,0:T(8,128)(2,1)S(1)}, bf16[352,512]{1,0:T(8,128)(2,1)S(1)}, u32[]{:S(2)}, u32[]{:S(2)}) collective-permute-start(bf16[352,512]{1,0:T(8,128)(2,1)S(1)} %add_convert_fusion.4), channel_id=1, source_target_pairs={{0,32},{32,0},{64,96},{96,64},{128,160},{160,128},{192,224},{224,1... | collective-permute-start | bytes 1081352 | tf_op jit(solution)/shard_map/ppermute | solution.py:62
  53.0 10.6 %collective-permute-start.4 = (bf16[80,1024]{1,0:T(8,128)(2,1)S(1)}, bf16[80,1024]{1,0:T(8,128)(2,1)S(1)}, u32[]{:S(2)}, u32[]{:S(2)}) collective-permute-start(bf16[80,1024]{1,0:T(8,128)(2,1)S(1)} %get-tuple-element.53.mine_ref), channel_id=1, source_target_pairs={{0,2},{1,3},{2,0},{3,1},{4,6},{5,7},{6,4},{7,5},{8,10},{9,11},{10,... | collective-permute-start | bytes 491528 | tf_op jit(solution)/shard_map/ppermute | solution.py:62
  55.7 22.4 %collective-permute-start.15 = (bf16[320,512]{1,0:T(8,128)(2,1)S(1)}, bf16[320,512]{1,0:T(8,128)(2,1)}, u32[]{:S(2)}, u32[]{:S(2)}) collective-permute-start(bf16[320,512]{1,0:T(8,128)(2,1)S(1)} %add_convert_fusion.6), channel_id=1, source_target_pairs={{0,32},{32,0},{64,96},{96,64},{128,160},{160,128},{192,224},{224,1... | collective-permute-start | bytes 983048 | tf_op jit(solution)/shard_map/ppermute | solution.py:62
  65.0 14.3 %all-to-all-start = ((f32[8,8,128]{2,1,0:T(8,128)}), f32[8,8,128]{2,1,0:T(8,128)S(1)}, u32[]{:S(2)}, u32[]{:S(2)}) async-start(f32[8,8,128]{2,1,0:T(8,128)} %get-tuple-element.61), calls=%async_computation | async-start | bytes 65536 | tf_op jit(solution)/shard_map/all_to_all | solution.py:412
  68.3 5.7 %collective-permute-start.5 = (bf16[64,1024]{1,0:T(8,128)(2,1)S(1)}, bf16[64,1024]{1,0:T(8,128)(2,1)S(1)}, u32[]{:S(2)}, u32[]{:S(2)}) collective-permute-start(bf16[64,1024]{1,0:T(8,128)(2,1)S(1)} %get-tuple-element.54), channel_id=1, source_target_pairs={{0,12},{1,13},{2,14},{3,15},{4,8},{5,9},{6,10},{7,11},{8,4},{9,5},... | collective-permute-start | bytes 393224 | tf_op jit(solution)/shard_map/ppermute | solution.py:62
  70.2 8.9 %collective-permute-start.19 = (bf16[352,512]{1,0:T(8,128)(2,1)S(1)}, bf16[352,512]{1,0:T(8,128)(2,1)S(1)}, u32[]{:S(2)}, u32[]{:S(2)}) collective-permute-start(bf16[352,512]{1,0:T(8,128)(2,1)S(1)} %add_convert_fusion), channel_id=1, source_target_pairs={{0,64},{32,96},{64,0},{96,32},{128,192},{160,224},{192,128},{224,1... | collective-permute-start | bytes 1081352 | tf_op jit(solution)/shard_map/ppermute | solution.py:62
  71.6 7.6 %collective-permute-start.11 = (bf16[352,512]{1,0:T(8,128)(2,1)S(1)}, bf16[352,512]{1,0:T(8,128)(2,1)S(1)}, u32[]{:S(2)}, u32[]{:S(2)}) collective-permute-start(bf16[352,512]{1,0:T(8,128)(2,1)S(1)} %add_convert_fusion.3), channel_id=1, source_target_pairs={{0,192},{32,224},{64,128},{96,160},{128,64},{160,96},{192,0},{224,... | collective-permute-start | bytes 1081352 | tf_op jit(solution)/shard_map/ppermute | solution.py:62
  74.8 8.4 %collective-permute-start.6 = (bf16[128,1024]{1,0:T(8,128)(2,1)}, bf16[128,1024]{1,0:T(8,128)(2,1)}, u32[]{:S(2)}, u32[]{:S(2)}) collective-permute-start(bf16[128,1024]{1,0:T(8,128)(2,1)} %pad_maximum_fusion.3), channel_id=1, source_target_pairs={{0,4},{1,5},{2,6},{3,7},{4,0},{5,1},{6,2},{7,3},{8,12},{9,13},{10,... | collective-permute-start | bytes 786440 | tf_op jit(solution)/shard_map/ppermute | solution.py:62
  79.3 39.1 %collective-permute-start.20 = (bf16[704,512]{1,0:T(8,128)(2,1)S(1)}, bf16[704,512]{1,0:T(8,128)(2,1)S(1)}, u32[]{:S(2)}, u32[]{:S(2)}) collective-permute-start(bf16[704,512]{1,0:T(8,128)(2,1)S(1)} %pad_maximum_fusion.refs_0_), channel_id=1, source_target_pairs={{0,64},{32,96},{64,0},{96,32},{128,192},{160,224},{192,128},{224,1... | collective-permute-start | bytes 2162696 | tf_op jit(solution)/shard_map/ppermute | solution.py:62
  80.2 38.2 %collective-permute-start.22 = (bf16[704,512]{1,0:T(8,128)(2,1)S(1)}, bf16[704,512]{1,0:T(8,128)(2,1)}, u32[]{:S(2)}, u32[]{:S(2)}) collective-permute-start(bf16[704,512]{1,0:T(8,128)(2,1)S(1)} %pad_maximum_fusion.1.refs_2_), channel_id=1, source_target_pairs={{0,32},{32,0},{64,96},{96,64},{128,160},{160,128},{192,224},{224,1... | collective-permute-start | bytes 2162696 | tf_op jit(solution)/shard_map/ppermute | solution.py:62
  81.4 36.9 %collective-permute-start.21 = (bf16[640,512]{1,0:T(8,128)(2,1)S(1)}, bf16[640,512]{1,0:T(8,128)(2,1)}, u32[]{:S(2)}, u32[]{:S(2)}) collective-permute-start(bf16[640,512]{1,0:T(8,128)(2,1)S(1)} %pad_maximum_fusion.2.refs_1_), channel_id=1, source_target_pairs={{0,192},{32,224},{64,128},{96,160},{128,64},{160,96},{192,0},{224,... | collective-permute-start | bytes 1966088 | tf_op jit(solution)/shard_map/ppermute | solution.py:62
  84.2 16.5 %collective-permute-start.7 = (bf16[256,1024]{1,0:T(8,128)(2,1)S(1)}, bf16[256,1024]{1,0:T(8,128)(2,1)}, u32[]{:S(2)}, u32[]{:S(2)}) collective-permute-start(bf16[256,1024]{1,0:T(8,128)(2,1)S(1)} %constant_dynamic-update-slice_fusion.low_ref), channel_id=1, source_target_pairs={{0,1},{1,0},{2,3},{3,2},{4,5},{5,4},{6,7},{7,6},{8,9},{9,8},{10,11... | collective-permute-start | bytes 1572872 | tf_op jit(solution)/shard_map/ppermute | solution.py:62

commit v2 on v1

--- a/solution.py
+++ b/solution.py
@@ -121,17 +121,17 @@
 SCALARS = pl.BlockSpec(memory_space=pltpu.SMEM)
 
 
-def front_kernel(where, gain_ref, *refs):
-    sources, refs = refs[:6], refs[6:]
+def front_kernel(where, *refs):
+    sources, refs = refs[:7], refs[7:]
     outs, refs = refs[:6], refs[6:]
     (gq, gk, gv), refs = refs[:3], refs[3:]
-    copied, refs = refs[:6], refs[6:]
+    copied, refs = refs[:7], refs[7:]
     (att, grad_att), refs = refs[:2], refs[2:]
     scratch, sem = dict(zip(("out", "value", "query", "key"), refs[:4])), refs[4]
     copies = [pltpu.make_async_copy(a, b, sem.at[i]) for i, (a, b) in enumerate(zip(sources, copied))]
     for copy in copies:
         copy.start()
-    og, wo, q_all, k_all, v_all, x = copied
+    og, wo, q_all, k_all, v_all, x, gain_ref = copied
     copies[0].wait()
     copies[1].wait()
     grad_att[...] = mm(og[...], wo[...], 1, 1).astype(BF16)
@@ -187,23 +187,23 @@
     for piece in PIECES:
         shapes += [jax.ShapeDtypeStruct((4 * piece_rows(piece), width), BF16)] * 2
     shapes += [jax.ShapeDtypeStruct((length, width), BF16)] + [jax.ShapeDtypeStruct((width, length), BF16)] * 2
-    sources = [pltpu.with_memory_space_constraint(a, pltpu.HBM) for a in (og, wo, q, k, v, x)]
+    sources = [pltpu.with_memory_space_constraint(a, pltpu.HBM) for a in (og, wo, q, k, v, x, weight)]
     return pl.pallas_call(
         front_kernel,
-        in_specs=[SCALARS, *whole(1), *[pl.BlockSpec(memory_space=pltpu.HBM)] * 6],
+        in_specs=[SCALARS, *[pl.BlockSpec(memory_space=pltpu.HBM)] * 7],
         out_specs=whole(9),
         out_shape=shapes,
         scratch_shapes=[
-            *[pltpu.VMEM(a.shape, BF16) for a in (og, wo, q, k, v, x)],
+            *[pltpu.VMEM(a.shape, a.dtype) for a in (og, wo, q, k, v, x, weight)],
             *[pltpu.VMEM((length, width), BF16)] * 2,
             pltpu.VMEM((width, depth), BF16),
             *[pltpu.VMEM((depth, width), BF16)] * 3,
-            pltpu.SemaphoreType.DMA((6,)),
+            pltpu.SemaphoreType.DMA((7,)),
         ],
         compiler_params=pltpu.CompilerParams(vmem_limit_bytes=40 << 20),
         cost_estimate=pl.CostEstimate(flops=8 << 30, bytes_accessed=16 << 20, transcendentals=1 << 20),
         name="front",
-    )(where, weight, *sources)
+    )(where, *sources)
 
 
 def total_kernel(where, x_ref, gq_ref, gk_ref, gv_ref, wq_ref, wk_ref, wv_ref, send_ref, keep_ref, gain_ref, low_ref):
@@ -240,8 +240,9 @@
     )(where, inputs, gq, gk, gv, wq, wk, wv)
 
 
-def mp_step_kernel(rows, first, gain_ref, *refs):
-    *sums, last, send_ref, out_ref = refs
+def mp_step_kernel(rows, first, ties, gain_ref, *refs):
+    *sums, last = refs[: -2 - ties]
+    send_ref, out_ref = refs[-2:]
     value = sums[0][pl.ds(first, rows), :].astype(F32)
     for ref in (*sums[1:], last):
         value = value + ref[pl.ds(first, rows), :].astype(F32)
@@ -252,20 +253,21 @@
     out_ref[...] = joined(*split(g))
 
 
-def mp_step(gain, sums, rows, first):
+def mp_step(gain, sums, rows, first, ties=()):
     depth = gain.shape[1]
     return pl.pallas_call(
-        functools.partial(mp_step_kernel, rows, first),
-        in_specs=whole(1 + len(sums)),
+        functools.partial(mp_step_kernel, rows, first, len(ties)),
+        in_specs=[*whole(1 + len(sums)), *[ANYWHERE] * len(ties)],
         out_specs=whole(2),
         out_shape=[jax.ShapeDtypeStruct((rows + EXTRA, depth), BF16), jax.ShapeDtypeStruct((1, depth), F32)],
         compiler_params=pltpu.CompilerParams(vmem_limit_bytes=4 << 20),
         cost_estimate=pl.CostEstimate(flops=1 << 10, bytes_accessed=1 << 10, transcendentals=0),
         name="mp_step",
-    )(gain, *sums)
-
-
-def rows_kernel(where, x_ref, og_ref, weight_ref, gain_ref, mine_ref, got_ref, out_ref, sum_ref):
+    )(gain, *sums, *ties)
+
+
+def rows_kernel(where, x_ref, og_ref, weight_ref, gain_ref, mine_ref, got_ref, *refs):
+    out_ref, sum_ref = refs[-2:]
     n = out_ref.shape[0]
     gradient = mine_ref[pl.ds(0, n), :].astype(F32) + got_ref[pl.ds(0, n), :].astype(F32)
     unit, rstd = norm_of(x_ref[...])
@@ -278,7 +280,7 @@
             sum_ref[i, pl.ds(j, 1), :] = g[:, j * 128 : (j + 1) * 128]
 
 
-def own_rows(where, inputs, og, weight, gain, mine, got):
+def own_rows(where, inputs, og, weight, gain, mine, got, ties):
     n, depth = mine.shape[0] - EXTRA, mine.shape[1]
 
     def fixed(shape):
@@ -290,21 +292,24 @@
         grid_spec=pltpu.PrefetchScalarGridSpec(
             num_scalar_prefetch=1,
             grid=(1,),
-            in_specs=[row, row, fixed((1, depth)), fixed((1, depth)), fixed(mine.shape), fixed(got.shape)],
+            in_specs=[row, row, fixed((1, depth)), fixed((1, depth)), fixed(mine.shape), fixed(got.shape), *[ANYWHERE] * len(ties)],
             out_specs=[fixed((n, depth)), pl.BlockSpec((8, 8, 128), lambda i, c: (0, 0, 0))],
         ),
         out_shape=[jax.ShapeDtypeStruct((n, depth), BF16), jax.ShapeDtypeStruct((8, 8, 128), F32)],
         compiler_params=pltpu.CompilerParams(vmem_limit_bytes=4 << 20),
         cost_estimate=pl.CostEstimate(flops=1 << 10, bytes_accessed=1 << 10, transcendentals=0),
         name="own_rows",
-    )(where, inputs, og, weight, gain, mine, got)
+    )(where, inputs, og, weight, gain, mine, got, *ties)
 
 
 ANYWHERE = pl.BlockSpec(memory_space=pl.ANY)
 
 
 def place_kernel(late, where, *refs):
-    halves, outs, sem = refs[:3], refs[-5:-1], refs[-1]
+    halves, sem = refs[:3], refs[-1]
+    outs = refs[7:11] if late else refs[3:7]
+    if not late:
+        refs[7][...] = jnp.zeros(refs[7].shape, F32)
     named = dict(zip(("query", "key", "value", "out"), outs))
     copies = []
     for i, piece in enumerate(PIECES):
@@ -327,13 +332,13 @@
     shapes = [jax.ShapeDtypeStruct((depth, width), BF16)] * 3 + [jax.ShapeDtypeStruct((width, depth), BF16)]
     return pl.pallas_call(
         functools.partial(place_kernel, late),
-        in_specs=[SCALARS, *[ANYWHERE] * (3 + len(outs))],
-        out_specs=[ANYWHERE] * 4,
-        out_shape=shapes,
+        in_specs=[SCALARS, *whole(3), *[ANYWHERE] * len(outs)],
+        out_specs=[ANYWHERE] * 4 + whole(1 - late),
+        out_shape=shapes + [jax.ShapeDtypeStruct((8, 128), F32)] * (1 - late),
         scratch_shapes=[pltpu.SemaphoreType.DMA((28,))],
         input_output_aliases={4 + i: i for i in range(len(outs))},
-        compiler_params=pltpu.CompilerParams(vmem_limit_bytes=1 << 20),
-        cost_estimate=pl.CostEstimate(flops=1 << 10, bytes_accessed=4 << 20, transcendentals=0),
+        compiler_params=pltpu.CompilerParams(vmem_limit_bytes=4 << 20),
+        cost_estimate=pl.CostEstimate(flops=(1 << 36) if late else (1 << 10), bytes_accessed=1 << 10, transcendentals=0),
         name="place_late" if late else "place_early",
     )(where, *halves, *outs)
 
@@ -354,11 +359,11 @@
 def place_rows(where, low, high):
     return pl.pallas_call(
         place_rows_kernel,
-        in_specs=[SCALARS, ANYWHERE, ANYWHERE],
+        in_specs=[SCALARS, *whole(2)],
         out_specs=ANYWHERE,
         out_shape=jax.ShapeDtypeStruct((2 * low.shape[0], low.shape[1]), BF16),
         scratch_shapes=[pltpu.SemaphoreType.DMA((8,))],
-        compiler_params=pltpu.CompilerParams(vmem_limit_bytes=1 << 20),
+        compiler_params=pltpu.CompilerParams(vmem_limit_bytes=4 << 20),
         cost_estimate=pl.CostEstimate(flops=1 << 10, bytes_accessed=2 << 20, transcendentals=0),
         name="place_rows",
     )(where, low, high)
@@ -369,6 +374,10 @@
     for value in values[1:]:
         total = total + value.astype(F32)
     return total.astype(BF16)
+
+
+def after(value, first):
+    return lax.optimization_barrier((value, *first))[0]
 
 
 def shards(
@@ -396,27 +405,26 @@
     r1 = swap(m_send, "core")
     send, gain = mp_step(gain, (m_keep, r1), 128, 128)
     r2 = swap(send, "g0")
-    second = [
-        swap(plus(k[2 * n :], r[2 * n :]), o[1]) for k, r, o, n in zip(keeps, first, ORDERS, sizes)
-    ]
-    send, gain = mp_step(gain, (m_keep, r1, r2), 64, 64)
+    second = [plus(k[2 * n :], r[2 * n :]) for k, r, n in zip(keeps, first, sizes)]
+    send, gain = mp_step(gain, (m_keep, r1, r2), 64, 64, second)
+    second = [swap(v, o[1]) for v, o in zip(second, ORDERS)]
     r3 = swap(send, "g1")
     mine = [plus(k[: 2 * n], r[: 2 * n], s) for k, r, s, n in zip(keeps, first, second, sizes)]
     third = [swap(v, o[2]) for v, o in zip(mine, ORDERS)]
-    send, gain = mp_step(gain, (m_keep, r1, r2, r3), 64, 0)
+    send, gain = mp_step(gain, (m_keep, r1, r2, r3), 64, 0, mine)
     r4 = swap(send, "g2")
     quarter = [plus(v, t) for v, t in zip(mine, third)]
-    send, gain = mp_step(gain, (send, r4), 64, 0)
-    r5 = swap(send, "xh")
-    rows, gains = own_rows(where, inputs, output_gradient, weight, gain, send, r5)
-    gains = lax.all_to_all(gains, "dp", 0, 0)
     back = [swap(v, o[1]) for v, o in zip(quarter, ORDERS)]
     half = [jnp.concatenate([v, b]) for v, b in zip(quarter, back)]
-    *half, gains = lax.optimization_barrier((*half, gains))
     last = [swap(v, o[0]) for v, o in zip(half, ORDERS)]
-    outs = place(0, where, half, (), depth, width)
+    send, gain = mp_step(gain, (send, r4), 64, 0, quarter)
+    r5 = swap(send, "xh")
+    rows, gains = own_rows(where, inputs, output_gradient, weight, gain, send, r5, half)
+    *outs, placed = place(0, where, half, (), depth, width)
     for step in ("g1", "g0"):
         rows = jnp.concatenate([rows, swap(rows, step)])
+    gains = lax.all_to_all(gains + placed, "dp", 0, 0)
+    rows = after(rows, last)
     grad_inputs = place_rows(where, rows, swap(rows, "core"))
     outs = place(1, where, last, outs, depth, width)
     return (grad_inputs, *outs, jnp.sum(gains, axis=0).reshape(depth))

time: 162 us -> 101 us (0.62)
  Pallas kernels: 77.2 us -> 19.9 us
  starting transfers between devices: 54.9 us -> 46.8 us
  blocking collectives: 0 us -> 7.63 us
  local copies, waits for them, and re-layouts: 1.7 us -> 0.03 us
    pallas_call x2, Pallas kernels: 45.7 us -> 4.96 us  [place(): pl.pallas_call(functools.partial(place_kernel, late), in_specs=[SCALARS,...]
    pallas_call x6, Pallas kernels: 27.7 us -> 11.7 us  [the longest x1 9.79 us: front(): pl.pallas_call(front_kernel, in_specs=[SCALARS, *[pl.BlockSpec(memory_spa...]
    all_to_all x0 -> x1, blocking collectives: none -> 7.63 us  [shards(): gains = lax.all_to_all(gains + placed, 'dp', 0, 0)]
    ppermute x23, starting transfers between devices: 51.6 us -> 46.8 us  [swap(): return lax.ppermute(value, axis, pairs)]
    all_to_all x1 -> x0, starting transfers between devices: 3.34 us -> none  [shards(): gains = lax.all_to_all(gains, 'dp', 0, 0)]
    ppermute x23, waiting for transfers between devices: 23.9 us -> 22.3 us  [swap(): return lax.ppermute(value, axis, pairs)]
  transfers between devices with their start and end apart: 24 -> 23, of which waited for: 8 -> 10; matrix products, arithmetic and copies ran while one was open for 3% -> 3% of each run, Pallas kernels for 15% -> 9%
where the time goes in v2:
time: 101 us; the launch traced here: 100 us
  starting transfers between devices  46.8 us (46%)
  waiting for transfers between devices  22.3 us (22%)
  Pallas kernels  19.9 us (20%)
  blocking collectives  7.63 us (8%)
  other arithmetic  2.76 us (3%)
  between operations  1.01 us (1%)
    ppermute x23, starting transfers between devices, swap(): return lax.ppermute(value, axis, pairs)  46.8 us
    ppermute x23, waiting for transfers between devices, swap(): return lax.ppermute(value, axis, pairs)  22.3 us
    pallas_call x1, Pallas kernels, front(): pl.pallas_call(front_kernel, in_specs=[SCALARS, *[pl.BlockSpec(memory_spa...  9.79 us
    all_to_all x1, blocking collectives, shards(): gains = lax.all_to_all(gains + placed, 'dp', 0, 0)  7.63 us
    pallas_call x2, Pallas kernels, place(): pl.pallas_call(functools.partial(place_kernel, late), in_specs=[SCALARS,...  4.96 us
    pallas_call x1, Pallas kernels, total_share(): pl.pallas_call(total_kernel, in_specs=[SCALARS, *whole(7)], out_specs=who...  2.48 us
  transfers between devices with their start and end apart: 23, of which 10 were waited for; matrix products, arithmetic and copies ran while one was open for 3% of the time, Pallas kernels for 9%

profile of v2, /device:TPU:1, one launch (start us, length us, event | category | flops | bytes accessed | tf_op | source)
XLA Modules:
  0.0 100.4 jit_solution(3068472978636131075)
XLA Ops:
  0.6 0.1 pad_add_fusion.where
  0.7 9.8 %front.1 = (bf16[704,512]{1,0:T(8,128)(2,1)S(1)}, bf16[704,512]{1,0:T(8,128)(2,1)S(1)}, bf16[640,512]{1,0:T(8,128)(2,1)S(1)}, bf16[640,512]{1,0:T(8,128)(2,1)S(1...) custom-call(s32[2]{0:T(128)S(1)} %pad_add_fusion.where, ...), custom_call_target="tpu_custom_call" | custom-call | flops 8589934592 | bytes 16777216 | tf_op jit(solution)/shard_map/front/pallas_call | solution.py:191
  10.5 2.2 %collective-permute-start.2 = (bf16[704,512]{1,0:T(8,128)(2,1)S(1)}, bf16[704,512]{1,0:T(8,128)(2,1)S(1)}, u32[]{:S(2)}, u32[]{:S(2)}) collective-permute-start(bf16[704,512]{1,0:T(8,128)(2,1)S(1)} %get-tuple-element.47), channel_id=1, source_target_pairs={{0,64},{32,96},{64,0},{96,32},{128,192},{160,224},{192,128},{224,1... | collective-permute-start | bytes 2162696 | tf_op jit(solution)/shard_map/ppermute | solution.py:62
  12.7 2.5 %total_share.1 = (bf16[272,1024]{1,0:T(8,128)(2,1)S(1)}, bf16[256,1024]{1,0:T(8,128)(2,1)S(1)}, f32[1,1024]{1,0:T(1,128)S(1)}) custom-call(s32[2]{0:T(128)S(1)} %pad_add_fusion.where, bf16[512,1024]{1,0:T(8,128)(2,1)S(1)} %copy-done, bf16[512,512]{1,0:T(8,128)(2,1)S(1)} %get-tuple-element.38.gq_ref, bf16[512,512]{1,0:T(8,128)(2,1)S(1)} %get-tuple-element.39.gk_ref, ...), custom_call_target="tpu_custom_call" | custom-call | flops 2147483648 | bytes 8388608 | tf_op jit(solution)/shard_map/total_share/pallas_call | solution.py:227
  15.2 1.2 %collective-permute-start = (bf16[272,1024]{1,0:T(8,128)(2,1)S(1)}, bf16[272,1024]{1,0:T(8,128)(2,1)S(1)}, u32[]{:S(2)}, u32[]{:S(2)}) collective-permute-start(bf16[272,1024]{1,0:T(8,128)(2,1)S(1)} %get-tuple-element.43), channel_id=1, source_target_pairs={{0,1},{1,0},{2,3},{3,2},{4,5},{5,4},{6,7},{7,6},{8,9},{9,8},{10,11... | collective-permute-start | bytes 1671176 | tf_op jit(solution)/shard_map/ppermute | solution.py:62
  16.5 1.0 %collective-permute-start.4 = (bf16[704,512]{1,0:T(8,128)(2,1)S(1)}, bf16[704,512]{1,0:T(8,128)(2,1)S(1)}, u32[]{:S(2)}, u32[]{:S(2)}) collective-permute-start(bf16[704,512]{1,0:T(8,128)(2,1)S(1)} %get-tuple-element.51), channel_id=1, source_target_pairs={{0,32},{32,0},{64,96},{96,64},{128,160},{160,128},{192,224},{224,1... | collective-permute-start | bytes 2162696 | tf_op jit(solution)/shard_map/ppermute | solution.py:62
  17.5 1.9 %collective-permute-start.3 = (bf16[640,512]{1,0:T(8,128)(2,1)S(1)}, bf16[640,512]{1,0:T(8,128)(2,1)S(1)}, u32[]{:S(2)}, u32[]{:S(2)}) collective-permute-start(bf16[640,512]{1,0:T(8,128)(2,1)S(1)} %get-tuple-element.49), channel_id=1, source_target_pairs={{0,192},{32,224},{64,128},{96,160},{128,64},{160,96},{192,0},{224,... | collective-permute-start | bytes 1966088 | tf_op jit(solution)/shard_map/ppermute | solution.py:62
  19.4 0.1 mp_step.4
  19.5 1.7 %collective-permute-start.1 = (bf16[144,1024]{1,0:T(8,128)(2,1)S(1)}, bf16[144,1024]{1,0:T(8,128)(2,1)S(1)}, u32[]{:S(2)}, u32[]{:S(2)}) collective-permute-start(bf16[144,1024]{1,0:T(8,128)(2,1)S(1)} %get-tuple-element.45), channel_id=1, source_target_pairs={{0,4},{1,5},{2,6},{3,7},{4,0},{5,1},{6,2},{7,3},{8,12},{9,13},{10,... | collective-permute-start | bytes 884744 | tf_op jit(solution)/shard_map/ppermute | solution.py:62
  21.3 6.1 %collective-permute-done.2 = bf16[704,512]{1,0:T(8,128)(2,1)S(1)} collective-permute-done((bf16[704,512]{1,0:T(8,128)(2,1)S(1)}, bf16[704,512]{1,0:T(8,128)(2,1)S(1)}, u32[]{:S(2)}, u32[]{:S(2)}) %collective-permute-start.2) | collective-permute-done | bytes 720928 | tf_op jit(solution)/shard_map/ppermute | solution.py:62
  27.4 0.1 add_convert_fusion.5.refs_3_
  27.4 3.9 %collective-permute-start.6 = (bf16[352,512]{1,0:T(8,128)(2,1)S(1)}, bf16[352,512]{1,0:T(8,128)(2,1)S(1)}, u32[]{:S(2)}, u32[]{:S(2)}) collective-permute-start(bf16[352,512]{1,0:T(8,128)(2,1)S(1)} %add_convert_fusion.5.refs_3_), channel_id=1, source_target_pairs={{0,192},{32,224},{64,128},{96,160},{128,64},{160,96},{192,0},{224,... | collective-permute-start | bytes 1081352 | tf_op jit(solution)/shard_map/ppermute | solution.py:62
  31.4 2.8 %collective-permute-done.4 = bf16[704,512]{1,0:T(8,128)(2,1)S(1)} collective-permute-done((bf16[704,512]{1,0:T(8,128)(2,1)S(1)}, bf16[704,512]{1,0:T(8,128)(2,1)S(1)}, u32[]{:S(2)}, u32[]{:S(2)}) %collective-permute-start.4) | collective-permute-done | bytes 720928 | tf_op jit(solution)/shard_map/ppermute | solution.py:62
  34.2 0.1 add_convert_fusion.4.refs_5_
  34.3 2.0 %collective-permute-start.8 = (bf16[352,512]{1,0:T(8,128)(2,1)S(1)}, bf16[352,512]{1,0:T(8,128)(2,1)S(1)}, u32[]{:S(2)}, u32[]{:S(2)}) collective-permute-start(bf16[352,512]{1,0:T(8,128)(2,1)S(1)} %add_convert_fusion.4.refs_5_), channel_id=1, source_target_pairs={{0,64},{32,96},{64,0},{96,32},{128,192},{160,224},{192,128},{224,1... | collective-permute-start | bytes 1081352 | tf_op jit(solution)/shard_map/ppermute | solution.py:62
  36.2 0.1 add_convert_fusion.8.refs_4_
  36.3 0.3 collective-permute-start.7
  36.6 0.0 collective-permute-done.1.refs_2_
  36.6 0.1 mp_step.5
  36.7 3.7 %collective-permute-start.5 = (bf16[80,1024]{1,0:T(8,128)(2,1)S(1)}, bf16[80,1024]{1,0:T(8,128)(2,1)S(1)}, u32[]{:S(2)}, u32[]{:S(2)}) collective-permute-start(bf16[80,1024]{1,0:T(8,128)(2,1)S(1)} %get-tuple-element.53), channel_id=1, source_target_pairs={{0,12},{1,13},{2,14},{3,15},{4,8},{5,9},{6,10},{7,11},{8,4},{9,5},... | collective-permute-start | bytes 491528 | tf_op jit(solution)/shard_map/ppermute | solution.py:62
  40.4 2.0 %collective-permute-done.6 = bf16[352,512]{1,0:T(8,128)(2,1)S(1)} collective-permute-done((bf16[352,512]{1,0:T(8,128)(2,1)S(1)}, bf16[352,512]{1,0:T(8,128)(2,1)S(1)}, u32[]{:S(2)}, u32[]{:S(2)}) %collective-permute-start.6) | collective-permute-done | bytes 360480 | tf_op jit(solution)/shard_map/ppermute | solution.py:62
  42.4 0.1 add_convert_fusion.3.refs_4_
  42.5 0.5 collective-permute-start.10
  43.1 1.0 %collective-permute-done.8 = bf16[352,512]{1,0:T(8,128)(2,1)S(1)} collective-permute-done((bf16[352,512]{1,0:T(8,128)(2,1)S(1)}, bf16[352,512]{1,0:T(8,128)(2,1)S(1)}, u32[]{:S(2)}, u32[]{:S(2)}) %collective-permute-start.8) | collective-permute-done | bytes 360480 | tf_op jit(solution)/shard_map/ppermute | solution.py:62
  44.1 0.1 add_convert_fusion.2.refs_6_
  44.2 1.3 %collective-permute-start.12 = (bf16[352,512]{1,0:T(8,128)(2,1)S(1)}, bf16[352,512]{1,0:T(8,128)(2,1)S(1)}, u32[]{:S(2)}, u32[]{:S(2)}) collective-permute-start(bf16[352,512]{1,0:T(8,128)(2,1)S(1)} %add_convert_fusion.2.refs_6_), channel_id=1, source_target_pairs={{0,192},{32,224},{64,128},{96,160},{128,64},{160,96},{192,0},{224,... | collective-permute-start | bytes 1081352 | tf_op jit(solution)/shard_map/ppermute | solution.py:62
  45.5 0.1 add_convert_fusion.7.refs_5_
  45.7 0.5 collective-permute-start.11
  46.1 0.0 collective-permute-done.5.refs_3_
  46.1 0.1 mp_step.6
  46.2 5.7 %collective-permute-start.9 = (bf16[80,1024]{1,0:T(8,128)(2,1)S(1)}, bf16[80,1024]{1,0:T(8,128)(2,1)S(1)}, u32[]{:S(2)}, u32[]{:S(2)}) collective-permute-start(bf16[80,1024]{1,0:T(8,128)(2,1)S(1)} %get-tuple-element.55.refs_0_), channel_id=1, source_target_pairs={{0,28},{1,29},{2,30},{3,31},{4,24},{5,25},{6,26},{7,27},{8,20},{9,... | collective-permute-start | bytes 491528 | tf_op jit(solution)/shard_map/ppermute | solution.py:62
  51.9 1.1 %collective-permute-done.10 = bf16[352,512]{1,0:T(8,128)(2,1)S(1)} collective-permute-done((bf16[352,512]{1,0:T(8,128)(2,1)S(1)}, bf16[352,512]{1,0:T(8,128)(2,1)S(1)}, u32[]{:S(2)}, u32[]{:S(2)}) %collective-permute-start.10) | collective-permute-done | bytes 360480 | tf_op jit(solution)/shard_map/ppermute | solution.py:62
  53.0 0.1 add_convert_fusion.1.refs_2_
  53.1 0.4 collective-permute-start.14
  53.4 0.5 collective-permute-done.12
  54.0 0.1 add_convert_fusion.refs_4_
  54.0 0.1 collective-permute-start.16
  54.1 0.0 collective-permute-done.11
  54.2 0.1 add_convert_fusion.6.refs_3_
  54.2 1.5 %collective-permute-start.15 = (bf16[320,512]{1,0:T(8,128)(2,1)S(1)}, bf16[320,512]{1,0:T(8,128)(2,1)S(1)}, u32[]{:S(2)}, u32[]{:S(2)}) collective-permute-start(bf16[320,512]{1,0:T(8,128)(2,1)S(1)} %add_convert_fusion.6.refs_3_), channel_id=1, source_target_pairs={{0,32},{32,0},{64,96},{96,64},{128,160},{160,128},{192,224},{224,1... | collective-permute-start | bytes 983048 | tf_op jit(solution)/shard_map/ppermute | solution.py:62
  55.7 3.6 %collective-permute-done.9.refs_1_ = bf16[80,1024]{1,0:T(8,128)(2,1)S(1)} collective-permute-done((bf16[80,1024]{1,0:T(8,128)(2,1)S(1)}, bf16[80,1024]{1,0:T(8,128)(2,1)S(1)}, u32[]{:S(2)}, u32[]{:S(2)}) %collective-permute-start.9) | collective-permute-done | bytes 163872 | tf_op jit(solution)/shard_map/ppermute | solution.py:62
  59.4 0.1 mp_step.7
  59.4 2.8 %collective-permute-start.13 = (bf16[80,1024]{1,0:T(8,128)(2,1)S(1)}, bf16[80,1024]{1,0:T(8,128)(2,1)S(1)}, u32[]{:S(2)}, u32[]{:S(2)}) collective-permute-start(bf16[80,1024]{1,0:T(8,128)(2,1)S(1)} %get-tuple-element.57.mine_ref), channel_id=1, source_target_pairs={{0,2},{1,3},{2,0},{3,1},{4,6},{5,7},{6,4},{7,5},{8,10},{9,11},{10,... | collective-permute-start | bytes 491528 | tf_op jit(solution)/shard_map/ppermute | solution.py:62
  62.3 0.5 collective-permute-done.14
  62.8 0.0 copy-start.1
  62.8 0.0 copy-start.2
  62.8 0.7 collective-permute-start.19
  63.5 0.0 collective-permute-done.16
  63.6 0.4 collective-permute-start.21
  64.0 0.9 collective-permute-start.20
  64.9 2.1 %collective-permute-done.13.got_ref = bf16[80,1024]{1,0:T(8,128)(2,1)S(1)} collective-permute-done((bf16[80,1024]{1,0:T(8,128)(2,1)S(1)}, bf16[80,1024]{1,0:T(8,128)(2,1)S(1)}, u32[]{:S(2)}, u32[]{:S(2)}) %collective-permute-start.13) | collective-permute-done | bytes 163872 | tf_op jit(solution)/shard_map/ppermute | solution.py:62
  67.0 0.8 own_rows.1
  67.8 4.4 %collective-permute-start.17 = (bf16[64,1024]{1,0:T(8,128)(2,1)S(1)}, bf16[64,1024]{1,0:T(8,128)(2,1)S(1)}, u32[]{:S(2)}, u32[]{:S(2)}) collective-permute-start(bf16[64,1024]{1,0:T(8,128)(2,1)S(1)} %get-tuple-element.58), channel_id=1, source_target_pairs={{0,12},{1,13},{2,14},{3,15},{4,8},{5,9},{6,10},{7,11},{8,4},{9,5},... | collective-permute-start | bytes 393224 | tf_op jit(solution)/shard_map/ppermute | solution.py:62
  72.2 2.5 %collective-permute-done.17 = bf16[64,1024]{1,0:T(8,128)(2,1)S(1)} collective-permute-done((bf16[64,1024]{1,0:T(8,128)(2,1)S(1)}, bf16[64,1024]{1,0:T(8,128)(2,1)S(1)}, u32[]{:S(2)}, u32[]{:S(2)}) %collective-permute-start.17) | collective-permute-done | bytes 131104 | tf_op jit(solution)/shard_map/ppermute | solution.py:62
  74.7 0.1 collective-permute-start.18
  74.8 2.1 %place_early.1 = (bf16[1024,512]{1,0:T(8,128)(2,1)}, bf16[1024,512]{1,0:T(8,128)(2,1)}, bf16[1024,512]{1,0:T(8,128)(2,1)}, bf16[512,1024]{1,0:T(8,128)(2,1)}, f32[8,128]{1,0:T(8,128)S(1)}) custom-call(s32[2]{0:T(128)S(1)} %pad_add_fusion.where, bf16[704,512]{1,0:T(8,128)(2,1)S(1)} %pad_maximum_fusion.refs_0_, ...), custom_call_target="tpu_custom_call" | custom-call | flops 1024 | bytes 1024 | tf_op jit(solution)/shard_map/place_early/pallas_call | solution.py:333
  76.9 7.6 %all_to_all.5 = f32[8,8,128]{2,1,0:T(8,128)S(1)} all-to-all(f32[8,8,128]{2,1,0:T(8,128)S(1)} %broadcast_add_fusion), channel_id=1, replica_groups=mesh['dp'=8,'mp'=32] {'dp'}, dimensions={0} | all-to-all | bytes 65536 | tf_op jit(solution)/shard_map/all_to_all | solution.py:426
  84.6 0.6 reduce_sum.9
  85.2 0.0 collective-permute-done.18
  85.2 1.0 pad_maximum_fusion.3.low_ref
  86.1 0.0 collective-permute-done.20.refs_1_
  86.2 9.6 %collective-permute-start.22 = (bf16[256,1024]{1,0:T(8,128)(2,1)S(1)}, bf16[256,1024]{1,0:T(8,128)(2,1)S(1)}, u32[]{:S(2)}, u32[]{:S(2)}) collective-permute-start(bf16[256,1024]{1,0:T(8,128)(2,1)S(1)} %pad_maximum_fusion.3.low_ref), channel_id=1, source_target_pairs={{0,1},{1,0},{2,3},{3,2},{4,5},{5,4},{6,7},{7,6},{8,9},{9,8},{10,11... | collective-permute-start | bytes 1572872 | tf_op jit(solution)/shard_map/ppermute | solution.py:62
  95.7 2.9 %place_late.1 = (bf16[1024,512]{1,0:T(8,128)(2,1)}, bf16[1024,512]{1,0:T(8,128)(2,1)}, bf16[1024,512]{1,0:T(8,128)(2,1)}, bf16[512,1024]{1,0:T(8,128)(2,1)}) custom-call(s32[2]{0:T(128)S(1)} %pad_add_fusion.where, bf16[704,512]{1,0:T(8,128)(2,1)S(1)} %collective-permute-done.19.refs_0_, ...), custom_call_target="tpu_custom_call", output_to_operand_aliasing={{0}: (4, {}), {1}: (5, {}), {2}: (6, {}), {3}: (7, {})} | custom-call | flops 68719476736 | bytes 1024 | tf_op jit(solution)/shard_map/place_late/pallas_call | solution.py:333
  98.6 1.6 %place_rows.1 = bf16[512,1024]{1,0:T(8,128)(2,1)} custom-call(s32[2]{0:T(128)S(1)} %pad_add_fusion.where, bf16[256,1024]{1,0:T(8,128)(2,1)S(1)} %pad_maximum_fusion.3.low_ref, bf16[256,1024]{1,0:T(8,128)(2,1)S(1)} %collective-permute-done.22.high_ref), custom_call_target="tpu_custom_call" | custom-call | flops 1024 | bytes 2097152 | tf_op jit(solution)/shard_map/place_rows/pallas_call | solution.py:360
  (22 shorter events, 0.2 us)
Async XLA Ops:
  0.7 12.0 %copy-start = (bf16[512,1024]{1,0:T(8,128)(2,1)S(1)}, bf16[512,1024]{1,0:T(8,128)(2,1)}, u32[]{:S(2)}) copy-start(bf16[512,1024]{1,0:T(8,128)(2,1)} %x_ref.3) | copy-start | bytes 3145732
  0.7 12.0 %copy-start.3 = (bf16[1024,512]{1,0:T(8,128)(2,1)S(1)}, bf16[1024,512]{1,0:T(8,128)(2,1)}, u32[]{:S(2)}) copy-start(bf16[1024,512]{1,0:T(8,128)(2,1)} %wq_ref.1) | copy-start | bytes 3145732
  0.7 12.0 %copy-start.4 = (bf16[1024,512]{1,0:T(8,128)(2,1)S(1)}, bf16[1024,512]{1,0:T(8,128)(2,1)}, u32[]{:S(2)}) copy-start(bf16[1024,512]{1,0:T(8,128)(2,1)} %wk_ref.1) | copy-start | bytes 3145732
  0.7 12.0 %copy-start.5 = (bf16[1024,512]{1,0:T(8,128)(2,1)S(1)}, bf16[1024,512]{1,0:T(8,128)(2,1)}, u32[]{:S(2)}) copy-start(bf16[1024,512]{1,0:T(8,128)(2,1)} %wv_ref.1) | copy-start | bytes 3145732
  10.5 16.8 %collective-permute-start.2 = (bf16[704,512]{1,0:T(8,128)(2,1)S(1)}, bf16[704,512]{1,0:T(8,128)(2,1)S(1)}, u32[]{:S(2)}, u32[]{:S(2)}) collective-permute-start(bf16[704,512]{1,0:T(8,128)(2,1)S(1)} %get-tuple-element.47), channel_id=1, source_target_pairs={{0,64},{32,96},{64,0},{96,32},{128,192},{160,224},{192,128},{224,1... | collective-permute-start | bytes 2162696 | tf_op jit(solution)/shard_map/ppermute | solution.py:62
  15.2 4.2 %collective-permute-start = (bf16[272,1024]{1,0:T(8,128)(2,1)S(1)}, bf16[272,1024]{1,0:T(8,128)(2,1)S(1)}, u32[]{:S(2)}, u32[]{:S(2)}) collective-permute-start(bf16[272,1024]{1,0:T(8,128)(2,1)S(1)} %get-tuple-element.43), channel_id=1, source_target_pairs={{0,1},{1,0},{2,3},{3,2},{4,5},{5,4},{6,7},{7,6},{8,9},{9,8},{10,11... | collective-permute-start | bytes 1671176 | tf_op jit(solution)/shard_map/ppermute | solution.py:62
  16.5 17.7 %collective-permute-start.4 = (bf16[704,512]{1,0:T(8,128)(2,1)S(1)}, bf16[704,512]{1,0:T(8,128)(2,1)S(1)}, u32[]{:S(2)}, u32[]{:S(2)}) collective-permute-start(bf16[704,512]{1,0:T(8,128)(2,1)S(1)} %get-tuple-element.51), channel_id=1, source_target_pairs={{0,32},{32,0},{64,96},{96,64},{128,160},{160,128},{192,224},{224,1... | collective-permute-start | bytes 2162696 | tf_op jit(solution)/shard_map/ppermute | solution.py:62
  17.5 18.7 %collective-permute-start.3 = (bf16[640,512]{1,0:T(8,128)(2,1)S(1)}, bf16[640,512]{1,0:T(8,128)(2,1)S(1)}, u32[]{:S(2)}, u32[]{:S(2)}) collective-permute-start(bf16[640,512]{1,0:T(8,128)(2,1)S(1)} %get-tuple-element.49), channel_id=1, source_target_pairs={{0,192},{32,224},{64,128},{96,160},{128,64},{160,96},{192,0},{224,... | collective-permute-start | bytes 1966088 | tf_op jit(solution)/shard_map/ppermute | solution.py:62
  19.5 17.1 %collective-permute-start.1 = (bf16[144,1024]{1,0:T(8,128)(2,1)S(1)}, bf16[144,1024]{1,0:T(8,128)(2,1)S(1)}, u32[]{:S(2)}, u32[]{:S(2)}) collective-permute-start(bf16[144,1024]{1,0:T(8,128)(2,1)S(1)} %get-tuple-element.45), channel_id=1, source_target_pairs={{0,4},{1,5},{2,6},{3,7},{4,0},{5,1},{6,2},{7,3},{8,12},{9,13},{10,... | collective-permute-start | bytes 884744 | tf_op jit(solution)/shard_map/ppermute | solution.py:62
  27.4 15.0 %collective-permute-start.6 = (bf16[352,512]{1,0:T(8,128)(2,1)S(1)}, bf16[352,512]{1,0:T(8,128)(2,1)S(1)}, u32[]{:S(2)}, u32[]{:S(2)}) collective-permute-start(bf16[352,512]{1,0:T(8,128)(2,1)S(1)} %add_convert_fusion.5.refs_3_), channel_id=1, source_target_pairs={{0,192},{32,224},{64,128},{96,160},{128,64},{160,96},{192,0},{224,... | collective-permute-start | bytes 1081352 | tf_op jit(solution)/shard_map/ppermute | solution.py:62
  34.3 9.8 %collective-permute-start.8 = (bf16[352,512]{1,0:T(8,128)(2,1)S(1)}, bf16[352,512]{1,0:T(8,128)(2,1)S(1)}, u32[]{:S(2)}, u32[]{:S(2)}) collective-permute-start(bf16[352,512]{1,0:T(8,128)(2,1)S(1)} %add_convert_fusion.4.refs_5_), channel_id=1, source_target_pairs={{0,64},{32,96},{64,0},{96,32},{128,192},{160,224},{192,128},{224,1... | collective-permute-start | bytes 1081352 | tf_op jit(solution)/shard_map/ppermute | solution.py:62
  36.3 9.2 %collective-permute-start.7 = (bf16[320,512]{1,0:T(8,128)(2,1)S(1)}, bf16[320,512]{1,0:T(8,128)(2,1)S(1)}, u32[]{:S(2)}, u32[]{:S(2)}) collective-permute-start(bf16[320,512]{1,0:T(8,128)(2,1)S(1)} %add_convert_fusion.8.refs_4_), channel_id=1, source_target_pairs={{0,32},{32,0},{64,96},{96,64},{128,160},{160,128},{192,224},{224,1... | collective-permute-start | bytes 983048 | tf_op jit(solution)/shard_map/ppermute | solution.py:62
  36.7 9.5 %collective-permute-start.5 = (bf16[80,1024]{1,0:T(8,128)(2,1)S(1)}, bf16[80,1024]{1,0:T(8,128)(2,1)S(1)}, u32[]{:S(2)}, u32[]{:S(2)}) collective-permute-start(bf16[80,1024]{1,0:T(8,128)(2,1)S(1)} %get-tuple-element.53), channel_id=1, source_target_pairs={{0,12},{1,13},{2,14},{3,15},{4,8},{5,9},{6,10},{7,11},{8,4},{9,5},... | collective-permute-start | bytes 491528 | tf_op jit(solution)/shard_map/ppermute | solution.py:62
  42.5 10.4 %collective-permute-start.10 = (bf16[352,512]{1,0:T(8,128)(2,1)S(1)}, bf16[352,512]{1,0:T(8,128)(2,1)S(1)}, u32[]{:S(2)}, u32[]{:S(2)}) collective-permute-start(bf16[352,512]{1,0:T(8,128)(2,1)S(1)} %add_convert_fusion.3.refs_4_), channel_id=1, source_target_pairs={{0,32},{32,0},{64,96},{96,64},{128,160},{160,128},{192,224},{224,1... | collective-permute-start | bytes 1081352 | tf_op jit(solution)/shard_map/ppermute | solution.py:62
  44.2 9.7 %collective-permute-start.12 = (bf16[352,512]{1,0:T(8,128)(2,1)S(1)}, bf16[352,512]{1,0:T(8,128)(2,1)S(1)}, u32[]{:S(2)}, u32[]{:S(2)}) collective-permute-start(bf16[352,512]{1,0:T(8,128)(2,1)S(1)} %add_convert_fusion.2.refs_6_), channel_id=1, source_target_pairs={{0,192},{32,224},{64,128},{96,160},{128,64},{160,96},{192,0},{224,... | collective-permute-start | bytes 1081352 | tf_op jit(solution)/shard_map/ppermute | solution.py:62
  45.7 8.5 %collective-permute-start.11 = (bf16[320,512]{1,0:T(8,128)(2,1)S(1)}, bf16[320,512]{1,0:T(8,128)(2,1)S(1)}, u32[]{:S(2)}, u32[]{:S(2)}) collective-permute-start(bf16[320,512]{1,0:T(8,128)(2,1)S(1)} %add_convert_fusion.7.refs_5_), channel_id=1, source_target_pairs={{0,64},{32,96},{64,0},{96,32},{128,192},{160,224},{192,128},{224,1... | collective-permute-start | bytes 983048 | tf_op jit(solution)/shard_map/ppermute | solution.py:62
  46.2 13.1 %collective-permute-start.9 = (bf16[80,1024]{1,0:T(8,128)(2,1)S(1)}, bf16[80,1024]{1,0:T(8,128)(2,1)S(1)}, u32[]{:S(2)}, u32[]{:S(2)}) collective-permute-start(bf16[80,1024]{1,0:T(8,128)(2,1)S(1)} %get-tuple-element.55.refs_0_), channel_id=1, source_target_pairs={{0,28},{1,29},{2,30},{3,31},{4,24},{5,25},{6,26},{7,27},{8,20},{9,... | collective-permute-start | bytes 491528 | tf_op jit(solution)/shard_map/ppermute | solution.py:62
  53.1 9.7 %collective-permute-start.14 = (bf16[352,512]{1,0:T(8,128)(2,1)S(1)}, bf16[352,512]{1,0:T(8,128)(2,1)S(1)}, u32[]{:S(2)}, u32[]{:S(2)}) collective-permute-start(bf16[352,512]{1,0:T(8,128)(2,1)S(1)} %add_convert_fusion.1.refs_2_), channel_id=1, source_target_pairs={{0,192},{32,224},{64,128},{96,160},{128,64},{160,96},{192,0},{224,... | collective-permute-start | bytes 1081352 | tf_op jit(solution)/shard_map/ppermute | solution.py:62
  54.0 9.5 %collective-permute-start.16 = (bf16[352,512]{1,0:T(8,128)(2,1)S(1)}, bf16[352,512]{1,0:T(8,128)(2,1)S(1)}, u32[]{:S(2)}, u32[]{:S(2)}) collective-permute-start(bf16[352,512]{1,0:T(8,128)(2,1)S(1)} %add_convert_fusion.refs_4_), channel_id=1, source_target_pairs={{0,64},{32,96},{64,0},{96,32},{128,192},{160,224},{192,128},{224,1... | collective-permute-start | bytes 1081352 | tf_op jit(solution)/shard_map/ppermute | solution.py:62
  54.2 9.7 %collective-permute-start.15 = (bf16[320,512]{1,0:T(8,128)(2,1)S(1)}, bf16[320,512]{1,0:T(8,128)(2,1)S(1)}, u32[]{:S(2)}, u32[]{:S(2)}) collective-permute-start(bf16[320,512]{1,0:T(8,128)(2,1)S(1)} %add_convert_fusion.6.refs_3_), channel_id=1, source_target_pairs={{0,32},{32,0},{64,96},{96,64},{128,160},{160,128},{192,224},{224,1... | collective-permute-start | bytes 983048 | tf_op jit(solution)/shard_map/ppermute | solution.py:62
  59.4 7.6 %collective-permute-start.13 = (bf16[80,1024]{1,0:T(8,128)(2,1)S(1)}, bf16[80,1024]{1,0:T(8,128)(2,1)S(1)}, u32[]{:S(2)}, u32[]{:S(2)}) collective-permute-start(bf16[80,1024]{1,0:T(8,128)(2,1)S(1)} %get-tuple-element.57.mine_ref), channel_id=1, source_target_pairs={{0,2},{1,3},{2,0},{3,1},{4,6},{5,7},{6,4},{7,5},{8,10},{9,11},{10,... | collective-permute-start | bytes 491528 | tf_op jit(solution)/shard_map/ppermute | solution.py:62
  62.8 4.2 %copy-start.1 = (bf16[512,1024]{1,0:T(8,128)(2,1)S(1)}, bf16[512,1024]{1,0:T(8,128)(2,1)}, u32[]{:S(2)}) copy-start(bf16[512,1024]{1,0:T(8,128)(2,1)} %og_ref.1) | copy-start | bytes 3145732
  62.8 4.2 %copy-start.2 = (f32[1024]{0:T(1024)S(1)}, f32[1024]{0:T(1024)}, u32[]{:S(2)}) copy-start(f32[1024]{0:T(1024)} %param.11) | copy-start | bytes 12292
  62.8 23.4 %collective-permute-start.19 = (bf16[704,512]{1,0:T(8,128)(2,1)S(1)}, bf16[704,512]{1,0:T(8,128)(2,1)S(1)}, u32[]{:S(2)}, u32[]{:S(2)}) collective-permute-start(bf16[704,512]{1,0:T(8,128)(2,1)S(1)} %pad_maximum_fusion.refs_0_), channel_id=1, source_target_pairs={{0,64},{32,96},{64,0},{96,32},{128,192},{160,224},{192,128},{224,1... | collective-permute-start | bytes 2162696 | tf_op jit(solution)/shard_map/ppermute | solution.py:62
  63.6 22.6 %collective-permute-start.21 = (bf16[704,512]{1,0:T(8,128)(2,1)S(1)}, bf16[704,512]{1,0:T(8,128)(2,1)}, u32[]{:S(2)}, u32[]{:S(2)}) collective-permute-start(bf16[704,512]{1,0:T(8,128)(2,1)S(1)} %pad_maximum_fusion.1.refs_2_), channel_id=1, source_target_pairs={{0,32},{32,0},{64,96},{96,64},{128,160},{160,128},{192,224},{224,1... | collective-permute-start | bytes 2162696 | tf_op jit(solution)/shard_map/ppermute | solution.py:62
  64.0 22.1 %collective-permute-start.20 = (bf16[640,512]{1,0:T(8,128)(2,1)S(1)}, bf16[640,512]{1,0:T(8,128)(2,1)}, u32[]{:S(2)}, u32[]{:S(2)}) collective-permute-start(bf16[640,512]{1,0:T(8,128)(2,1)S(1)} %pad_maximum_fusion.2.refs_1_), channel_id=1, source_target_pairs={{0,192},{32,224},{64,128},{96,160},{128,64},{160,96},{192,0},{224,... | collective-permute-start | bytes 1966088 | tf_op jit(solution)/shard_map/ppermute | solution.py:62
  67.8 6.9 %collective-permute-start.17 = (bf16[64,1024]{1,0:T(8,128)(2,1)S(1)}, bf16[64,1024]{1,0:T(8,128)(2,1)S(1)}, u32[]{:S(2)}, u32[]{:S(2)}) collective-permute-start(bf16[64,1024]{1,0:T(8,128)(2,1)S(1)} %get-tuple-element.58), channel_id=1, source_target_pairs={{0,12},{1,13},{2,14},{3,15},{4,8},{5,9},{6,10},{7,11},{8,4},{9,5},... | collective-permute-start | bytes 393224 | tf_op jit(solution)/shard_map/ppermute | solution.py:62
  74.7 10.5 %collective-permute-start.18 = (bf16[128,1024]{1,0:T(8,128)(2,1)S(1)}, bf16[128,1024]{1,0:T(8,128)(2,1)}, u32[]{:S(2)}, u32[]{:S(2)}) collective-permute-start(bf16[128,1024]{1,0:T(8,128)(2,1)S(1)} %pad_maximum_fusion.4), channel_id=1, source_target_pairs={{0,4},{1,5},{2,6},{3,7},{4,0},{5,1},{6,2},{7,3},{8,12},{9,13},{10,... | collective-permute-start | bytes 786440 | tf_op jit(solution)/shard_map/ppermute | solution.py:62
  86.2 12.4 %collective-permute-start.22 = (bf16[256,1024]{1,0:T(8,128)(2,1)S(1)}, bf16[256,1024]{1,0:T(8,128)(2,1)S(1)}, u32[]{:S(2)}, u32[]{:S(2)}) collective-permute-start(bf16[256,1024]{1,0:T(8,128)(2,1)S(1)} %pad_maximum_fusion.3.low_ref), channel_id=1, source_target_pairs={{0,1},{1,0},{2,3},{3,2},{4,5},{5,4},{6,7},{7,6},{8,9},{9,8},{10,11... | collective-permute-start | bytes 1572872 | tf_op jit(solution)/shard_map/ppermute | solution.py:62

commit v3 on v2

--- a/solution.py
+++ b/solution.py
@@ -423,7 +423,7 @@
     *outs, placed = place(0, where, half, (), depth, width)
     for step in ("g1", "g0"):
         rows = jnp.concatenate([rows, swap(rows, step)])
-    gains = lax.all_to_all(gains + placed, "dp", 0, 0)
+    gains = lax.all_to_all(gains, "dp", 0, 0)
     rows = after(rows, last)
     grad_inputs = place_rows(where, rows, swap(rows, "core"))
     outs = place(1, where, last, outs, depth, width)

time: 101 us -> 99.1 us (0.981)
  blocking collectives: 7.63 us -> 0 us
  waiting for transfers between devices: 22.3 us -> 24.9 us
  starting transfers between devices: 46.8 us -> 49.1 us
  Pallas kernels: 19.9 us -> 21.1 us
    all_to_all x1 -> x0, blocking collectives: 7.63 us -> none  [shards(): gains = lax.all_to_all(gains + placed, 'dp', 0, 0)]
    all_to_all x0 -> x1, starting transfers between devices: none -> 3.35 us  [shards(): gains = lax.all_to_all(gains, 'dp', 0, 0)]
    all_to_all x0 -> x1, waiting for transfers between devices: none -> 2.69 us  [shards(): gains = lax.all_to_all(gains, 'dp', 0, 0)]
  transfers between devices with their start and end apart: 23 -> 24, of which waited for: 10 -> 11; matrix products, arithmetic and copies ran while one was open for 3% -> 3% of each run, Pallas kernels for 9% -> 10%
where the time goes in v3:
time: 99.1 us; the launch traced here: 98.9 us
  starting transfers between devices  49.1 us (50%)
  waiting for transfers between devices  24.9 us (25%)
  Pallas kernels  21.1 us (21%)
  other arithmetic  2.75 us (3%)
  between operations  1.01 us (1%)
    ppermute x23, starting transfers between devices, swap(): return lax.ppermute(value, axis, pairs)  45.8 us
    ppermute x23, waiting for transfers between devices, swap(): return lax.ppermute(value, axis, pairs)  22.3 us
    pallas_call x1, Pallas kernels, front(): pl.pallas_call(front_kernel, in_specs=[SCALARS, *[pl.BlockSpec(memory_spa...  9.79 us
    pallas_call x2, Pallas kernels, place(): pl.pallas_call(functools.partial(place_kernel, late), in_specs=[SCALARS,...  5.55 us
    all_to_all x1, starting transfers between devices, shards(): gains = lax.all_to_all(gains, 'dp', 0, 0)  3.35 us
    all_to_all x1, waiting for transfers between devices, shards(): gains = lax.all_to_all(gains, 'dp', 0, 0)  2.69 us
    pallas_call x1, Pallas kernels, total_share(): pl.pallas_call(total_kernel, in_specs=[SCALARS, *whole(7)], out_specs=who...  2.48 us
  transfers between devices with their start and end apart: 24, of which 11 were waited for; matrix products, arithmetic and copies ran while one was open for 3% of the time, Pallas kernels for 10%

profile of v3, /device:TPU:1, one launch (start us, length us, event | category | flops | bytes accessed | tf_op | source)
XLA Modules:
  0.0 98.9 jit_solution(13548373031174766614)
XLA Ops:
  0.6 0.1 pad_add_fusion.where
  0.7 9.8 %front.1 = (bf16[704,512]{1,0:T(8,128)(2,1)S(1)}, bf16[704,512]{1,0:T(8,128)(2,1)S(1)}, bf16[640,512]{1,0:T(8,128)(2,1)S(1)}, bf16[640,512]{1,0:T(8,128)(2,1)S(1...) custom-call(s32[2]{0:T(128)S(1)} %pad_add_fusion.where, ...), custom_call_target="tpu_custom_call" | custom-call | flops 8589934592 | bytes 16777216 | tf_op jit(solution)/shard_map/front/pallas_call | solution.py:191
  10.5 2.2 %collective-permute-start.2 = (bf16[704,512]{1,0:T(8,128)(2,1)S(1)}, bf16[704,512]{1,0:T(8,128)(2,1)S(1)}, u32[]{:S(2)}, u32[]{:S(2)}) collective-permute-start(bf16[704,512]{1,0:T(8,128)(2,1)S(1)} %get-tuple-element.46), channel_id=1, source_target_pairs={{0,64},{32,96},{64,0},{96,32},{128,192},{160,224},{192,128},{224,1... | collective-permute-start | bytes 2162696 | tf_op jit(solution)/shard_map/ppermute | solution.py:62
  12.7 2.5 %total_share.1 = (bf16[272,1024]{1,0:T(8,128)(2,1)S(1)}, bf16[256,1024]{1,0:T(8,128)(2,1)S(1)}, f32[1,1024]{1,0:T(1,128)S(1)}) custom-call(s32[2]{0:T(128)S(1)} %pad_add_fusion.where, bf16[512,1024]{1,0:T(8,128)(2,1)S(1)} %copy-done, bf16[512,512]{1,0:T(8,128)(2,1)S(1)} %get-tuple-element.37.gq_ref, bf16[512,512]{1,0:T(8,128)(2,1)S(1)} %get-tuple-element.38.gk_ref, ...), custom_call_target="tpu_custom_call" | custom-call | flops 2147483648 | bytes 8388608 | tf_op jit(solution)/shard_map/total_share/pallas_call | solution.py:227
  15.2 1.2 %collective-permute-start = (bf16[272,1024]{1,0:T(8,128)(2,1)S(1)}, bf16[272,1024]{1,0:T(8,128)(2,1)S(1)}, u32[]{:S(2)}, u32[]{:S(2)}) collective-permute-start(bf16[272,1024]{1,0:T(8,128)(2,1)S(1)} %get-tuple-element.42), channel_id=1, source_target_pairs={{0,1},{1,0},{2,3},{3,2},{4,5},{5,4},{6,7},{7,6},{8,9},{9,8},{10,11... | collective-permute-start | bytes 1671176 | tf_op jit(solution)/shard_map/ppermute | solution.py:62
  16.5 1.0 %collective-permute-start.4 = (bf16[704,512]{1,0:T(8,128)(2,1)S(1)}, bf16[704,512]{1,0:T(8,128)(2,1)S(1)}, u32[]{:S(2)}, u32[]{:S(2)}) collective-permute-start(bf16[704,512]{1,0:T(8,128)(2,1)S(1)} %get-tuple-element.50), channel_id=1, source_target_pairs={{0,32},{32,0},{64,96},{96,64},{128,160},{160,128},{192,224},{224,1... | collective-permute-start | bytes 2162696 | tf_op jit(solution)/shard_map/ppermute | solution.py:62
  17.5 1.9 %collective-permute-start.3 = (bf16[640,512]{1,0:T(8,128)(2,1)S(1)}, bf16[640,512]{1,0:T(8,128)(2,1)S(1)}, u32[]{:S(2)}, u32[]{:S(2)}) collective-permute-start(bf16[640,512]{1,0:T(8,128)(2,1)S(1)} %get-tuple-element.48), channel_id=1, source_target_pairs={{0,192},{32,224},{64,128},{96,160},{128,64},{160,96},{192,0},{224,... | collective-permute-start | bytes 1966088 | tf_op jit(solution)/shard_map/ppermute | solution.py:62
  19.4 0.0 collective-permute-done.refs_1_
  19.4 0.1 mp_step.4
  19.5 1.7 %collective-permute-start.1 = (bf16[144,1024]{1,0:T(8,128)(2,1)S(1)}, bf16[144,1024]{1,0:T(8,128)(2,1)S(1)}, u32[]{:S(2)}, u32[]{:S(2)}) collective-permute-start(bf16[144,1024]{1,0:T(8,128)(2,1)S(1)} %get-tuple-element.44), channel_id=1, source_target_pairs={{0,4},{1,5},{2,6},{3,7},{4,0},{5,1},{6,2},{7,3},{8,12},{9,13},{10,... | collective-permute-start | bytes 884744 | tf_op jit(solution)/shard_map/ppermute | solution.py:62
  21.3 6.1 %collective-permute-done.2 = bf16[704,512]{1,0:T(8,128)(2,1)S(1)} collective-permute-done((bf16[704,512]{1,0:T(8,128)(2,1)S(1)}, bf16[704,512]{1,0:T(8,128)(2,1)S(1)}, u32[]{:S(2)}, u32[]{:S(2)}) %collective-permute-start.2) | collective-permute-done | bytes 720928 | tf_op jit(solution)/shard_map/ppermute | solution.py:62
  27.4 0.1 add_convert_fusion.5.refs_3_
  27.4 3.9 %collective-permute-start.6 = (bf16[352,512]{1,0:T(8,128)(2,1)S(1)}, bf16[352,512]{1,0:T(8,128)(2,1)S(1)}, u32[]{:S(2)}, u32[]{:S(2)}) collective-permute-start(bf16[352,512]{1,0:T(8,128)(2,1)S(1)} %add_convert_fusion.5.refs_3_), channel_id=1, source_target_pairs={{0,192},{32,224},{64,128},{96,160},{128,64},{160,96},{192,0},{224,... | collective-permute-start | bytes 1081352 | tf_op jit(solution)/shard_map/ppermute | solution.py:62
  31.4 2.8 %collective-permute-done.4 = bf16[704,512]{1,0:T(8,128)(2,1)S(1)} collective-permute-done((bf16[704,512]{1,0:T(8,128)(2,1)S(1)}, bf16[704,512]{1,0:T(8,128)(2,1)S(1)}, u32[]{:S(2)}, u32[]{:S(2)}) %collective-permute-start.4) | collective-permute-done | bytes 720928 | tf_op jit(solution)/shard_map/ppermute | solution.py:62
  34.2 0.1 add_convert_fusion.4.refs_5_
  34.3 2.0 %collective-permute-start.8 = (bf16[352,512]{1,0:T(8,128)(2,1)S(1)}, bf16[352,512]{1,0:T(8,128)(2,1)S(1)}, u32[]{:S(2)}, u32[]{:S(2)}) collective-permute-start(bf16[352,512]{1,0:T(8,128)(2,1)S(1)} %add_convert_fusion.4.refs_5_), channel_id=1, source_target_pairs={{0,64},{32,96},{64,0},{96,32},{128,192},{160,224},{192,128},{224,1... | collective-permute-start | bytes 1081352 | tf_op jit(solution)/shard_map/ppermute | solution.py:62
  36.2 0.0 collective-permute-done.3
  36.2 0.1 add_convert_fusion.8.refs_4_
  36.3 0.3 collective-permute-start.7
  36.6 0.1 mp_step.5
  36.7 3.7 %collective-permute-start.5 = (bf16[80,1024]{1,0:T(8,128)(2,1)S(1)}, bf16[80,1024]{1,0:T(8,128)(2,1)S(1)}, u32[]{:S(2)}, u32[]{:S(2)}) collective-permute-start(bf16[80,1024]{1,0:T(8,128)(2,1)S(1)} %get-tuple-element.52), channel_id=1, source_target_pairs={{0,12},{1,13},{2,14},{3,15},{4,8},{5,9},{6,10},{7,11},{8,4},{9,5},... | collective-permute-start | bytes 491528 | tf_op jit(solution)/shard_map/ppermute | solution.py:62
  40.4 2.0 %collective-permute-done.6 = bf16[352,512]{1,0:T(8,128)(2,1)S(1)} collective-permute-done((bf16[352,512]{1,0:T(8,128)(2,1)S(1)}, bf16[352,512]{1,0:T(8,128)(2,1)S(1)}, u32[]{:S(2)}, u32[]{:S(2)}) %collective-permute-start.6) | collective-permute-done | bytes 360480 | tf_op jit(solution)/shard_map/ppermute | solution.py:62
  42.4 0.1 add_convert_fusion.3.refs_4_
  42.5 0.5 collective-permute-start.10
  43.1 1.0 %collective-permute-done.8 = bf16[352,512]{1,0:T(8,128)(2,1)S(1)} collective-permute-done((bf16[352,512]{1,0:T(8,128)(2,1)S(1)}, bf16[352,512]{1,0:T(8,128)(2,1)S(1)}, u32[]{:S(2)}, u32[]{:S(2)}) %collective-permute-start.8) | collective-permute-done | bytes 360480 | tf_op jit(solution)/shard_map/ppermute | solution.py:62
  44.1 0.1 add_convert_fusion.2.refs_6_
  44.2 1.3 %collective-permute-start.12 = (bf16[352,512]{1,0:T(8,128)(2,1)S(1)}, bf16[352,512]{1,0:T(8,128)(2,1)S(1)}, u32[]{:S(2)}, u32[]{:S(2)}) collective-permute-start(bf16[352,512]{1,0:T(8,128)(2,1)S(1)} %add_convert_fusion.2.refs_6_), channel_id=1, source_target_pairs={{0,192},{32,224},{64,128},{96,160},{128,64},{160,96},{192,0},{224,... | collective-permute-start | bytes 1081352 | tf_op jit(solution)/shard_map/ppermute | solution.py:62
  45.5 0.0 collective-permute-done.7
  45.5 0.1 add_convert_fusion.7.refs_5_
  45.7 0.5 collective-permute-start.11
  46.1 0.0 collective-permute-done.5.refs_3_
  46.1 0.1 mp_step.6
  46.2 5.7 %collective-permute-start.9 = (bf16[80,1024]{1,0:T(8,128)(2,1)S(1)}, bf16[80,1024]{1,0:T(8,128)(2,1)S(1)}, u32[]{:S(2)}, u32[]{:S(2)}) collective-permute-start(bf16[80,1024]{1,0:T(8,128)(2,1)S(1)} %get-tuple-element.54.refs_0_), channel_id=1, source_target_pairs={{0,28},{1,29},{2,30},{3,31},{4,24},{5,25},{6,26},{7,27},{8,20},{9,... | collective-permute-start | bytes 491528 | tf_op jit(solution)/shard_map/ppermute | solution.py:62
  51.9 1.1 %collective-permute-done.10 = bf16[352,512]{1,0:T(8,128)(2,1)S(1)} collective-permute-done((bf16[352,512]{1,0:T(8,128)(2,1)S(1)}, bf16[352,512]{1,0:T(8,128)(2,1)S(1)}, u32[]{:S(2)}, u32[]{:S(2)}) %collective-permute-start.10) | collective-permute-done | bytes 360480 | tf_op jit(solution)/shard_map/ppermute | solution.py:62
  53.0 0.1 add_convert_fusion.1.refs_2_
  53.1 0.4 collective-permute-start.14
  53.4 0.5 collective-permute-done.12
  54.0 0.1 add_convert_fusion.refs_4_
  54.0 0.1 collective-permute-start.16
  54.1 0.0 collective-permute-done.11
  54.2 0.1 add_convert_fusion.6.refs_3_
  54.2 1.5 %collective-permute-start.15 = (bf16[320,512]{1,0:T(8,128)(2,1)S(1)}, bf16[320,512]{1,0:T(8,128)(2,1)S(1)}, u32[]{:S(2)}, u32[]{:S(2)}) collective-permute-start(bf16[320,512]{1,0:T(8,128)(2,1)S(1)} %add_convert_fusion.6.refs_3_), channel_id=1, source_target_pairs={{0,32},{32,0},{64,96},{96,64},{128,160},{160,128},{192,224},{224,1... | collective-permute-start | bytes 983048 | tf_op jit(solution)/shard_map/ppermute | solution.py:62
  55.7 3.6 %collective-permute-done.9.refs_1_ = bf16[80,1024]{1,0:T(8,128)(2,1)S(1)} collective-permute-done((bf16[80,1024]{1,0:T(8,128)(2,1)S(1)}, bf16[80,1024]{1,0:T(8,128)(2,1)S(1)}, u32[]{:S(2)}, u32[]{:S(2)}) %collective-permute-start.9) | collective-permute-done | bytes 163872 | tf_op jit(solution)/shard_map/ppermute | solution.py:62
  59.4 0.1 mp_step.7
  59.4 2.8 %collective-permute-start.13 = (bf16[80,1024]{1,0:T(8,128)(2,1)S(1)}, bf16[80,1024]{1,0:T(8,128)(2,1)S(1)}, u32[]{:S(2)}, u32[]{:S(2)}) collective-permute-start(bf16[80,1024]{1,0:T(8,128)(2,1)S(1)} %get-tuple-element.56.mine_ref), channel_id=1, source_target_pairs={{0,2},{1,3},{2,0},{3,1},{4,6},{5,7},{6,4},{7,5},{8,10},{9,11},{10,... | collective-permute-start | bytes 491528 | tf_op jit(solution)/shard_map/ppermute | solution.py:62
  62.3 0.5 collective-permute-done.14
  62.8 0.0 copy-start.1
  62.8 0.0 copy-start.2
  62.8 0.7 collective-permute-start.19
  63.6 0.4 collective-permute-start.21
  64.0 0.9 collective-permute-start.20
  64.9 2.1 %collective-permute-done.13.got_ref = bf16[80,1024]{1,0:T(8,128)(2,1)S(1)} collective-permute-done((bf16[80,1024]{1,0:T(8,128)(2,1)S(1)}, bf16[80,1024]{1,0:T(8,128)(2,1)S(1)}, u32[]{:S(2)}, u32[]{:S(2)}) %collective-permute-start.13) | collective-permute-done | bytes 163872 | tf_op jit(solution)/shard_map/ppermute | solution.py:62
  67.0 1.3 %own_rows.1 = (bf16[64,1024]{1,0:T(8,128)(2,1)S(1)}, f32[8,8,128]{2,1,0:T(8,128)}) custom-call(s32[2]{0:T(128)S(1)} %pad_add_fusion.where, bf16[512,1024]{1,0:T(8,128)(2,1)S(1)} %copy-done, bf16[512,1024]{1,0:T(8,128)(2,1)S(1)} %copy-done.1, f32[1,1024]{1,0:T(1,128)S(1)} %bitcast.5, f32[1,1024]{1,0:T(1,128)S(1)} %get-tuple-element.55.gain_ref, ...), custom_call_target="tpu_custom_call" | custom-call | flops 1024 | bytes 1024 | tf_op jit(solution)/shard_map/own_rows/pallas_call | solution.py:290
  68.3 4.3 %collective-permute-start.17 = (bf16[64,1024]{1,0:T(8,128)(2,1)S(1)}, bf16[64,1024]{1,0:T(8,128)(2,1)S(1)}, u32[]{:S(2)}, u32[]{:S(2)}) collective-permute-start(bf16[64,1024]{1,0:T(8,128)(2,1)S(1)} %get-tuple-element.57), channel_id=1, source_target_pairs={{0,12},{1,13},{2,14},{3,15},{4,8},{5,9},{6,10},{7,11},{8,4},{9,5},... | collective-permute-start | bytes 393224 | tf_op jit(solution)/shard_map/ppermute | solution.py:62
  72.7 2.5 %collective-permute-done.17 = bf16[64,1024]{1,0:T(8,128)(2,1)S(1)} collective-permute-done((bf16[64,1024]{1,0:T(8,128)(2,1)S(1)}, bf16[64,1024]{1,0:T(8,128)(2,1)S(1)}, u32[]{:S(2)}, u32[]{:S(2)}) %collective-permute-start.17) | collective-permute-done | bytes 131104 | tf_op jit(solution)/shard_map/ppermute | solution.py:62
  75.1 0.1 collective-permute-start.18
  75.2 3.4 %all-to-all-start = ((f32[8,8,128]{2,1,0:T(8,128)}), f32[8,8,128]{2,1,0:T(8,128)S(1)}, u32[]{:S(2)}, u32[]{:S(2)}) async-start(f32[8,8,128]{2,1,0:T(8,128)} %get-tuple-element.67), calls=%async_computation | async-start | bytes 65536 | tf_op jit(solution)/shard_map/all_to_all | solution.py:426
  78.6 2.7 %place_early.1 = (bf16[1024,512]{1,0:T(8,128)(2,1)}, bf16[1024,512]{1,0:T(8,128)(2,1)}, bf16[1024,512]{1,0:T(8,128)(2,1)}, bf16[512,1024]{1,0:T(8,128)(2,1)}, f32[8,128]{1,0:T(8,128)}) custom-call(s32[2]{0:T(128)S(1)} %pad_add_fusion.where, bf16[704,512]{1,0:T(8,128)(2,1)S(1)} %pad_maximum_fusion.refs_0_, bf16[640,512]{1,0:T(8,128)(2,1)S(1)} %pad_maximum_fusion.2.refs_1_, ...), custom_call_target="tpu_custom_call" | custom-call | flops 1024 | bytes 1024 | tf_op jit(solution)/shard_map/place_early/pallas_call | solution.py:333
  81.3 2.7 %all-to-all-done = f32[8,8,128]{2,1,0:T(8,128)S(1)} async-done(((f32[8,8,128]{2,1,0:T(8,128)}), f32[8,8,128]{2,1,0:T(8,128)S(1)}, u32[]{:S(2)}, u32[]{:S(2)}) %all-to-all-start) | async-done | bytes 32800 | tf_op jit(solution)/shard_map/all_to_all | solution.py:426
  84.0 0.6 reduce_sum.9
  84.6 1.0 pad_maximum_fusion.3.low_ref
  85.6 8.7 %collective-permute-start.22 = (bf16[256,1024]{1,0:T(8,128)(2,1)S(1)}, bf16[256,1024]{1,0:T(8,128)(2,1)S(1)}, u32[]{:S(2)}, u32[]{:S(2)}) collective-permute-start(bf16[256,1024]{1,0:T(8,128)(2,1)S(1)} %pad_maximum_fusion.3.low_ref), channel_id=1, source_target_pairs={{0,1},{1,0},{2,3},{3,2},{4,5},{5,4},{6,7},{7,6},{8,9},{9,8},{10,11... | collective-permute-start | bytes 1572872 | tf_op jit(solution)/shard_map/ppermute | solution.py:62
  94.3 2.9 %place_late.1 = (bf16[1024,512]{1,0:T(8,128)(2,1)}, bf16[1024,512]{1,0:T(8,128)(2,1)}, bf16[1024,512]{1,0:T(8,128)(2,1)}, bf16[512,1024]{1,0:T(8,128)(2,1)}) custom-call(s32[2]{0:T(128)S(1)} %pad_add_fusion.where, bf16[704,512]{1,0:T(8,128)(2,1)S(1)} %collective-permute-done.19.refs_0_, ...), custom_call_target="tpu_custom_call", output_to_operand_aliasing={{0}: (4, {}), {1}: (5, {}), {2}: (6, {}), {3}: (7, {})} | custom-call | flops 68719476736 | bytes 1024 | tf_op jit(solution)/shard_map/place_late/pallas_call | solution.py:333
  97.2 1.6 %place_rows.1 = bf16[512,1024]{1,0:T(8,128)(2,1)} custom-call(s32[2]{0:T(128)S(1)} %pad_add_fusion.where, bf16[256,1024]{1,0:T(8,128)(2,1)S(1)} %pad_maximum_fusion.3.low_ref, bf16[256,1024]{1,0:T(8,128)(2,1)S(1)} %collective-permute-done.22.high_ref), custom_call_target="tpu_custom_call" | custom-call | flops 1024 | bytes 2097152 | tf_op jit(solution)/shard_map/place_rows/pallas_call | solution.py:360
  (22 shorter events, 0.2 us)
Async XLA Ops:
  0.7 12.0 %copy-start = (bf16[512,1024]{1,0:T(8,128)(2,1)S(1)}, bf16[512,1024]{1,0:T(8,128)(2,1)}, u32[]{:S(2)}) copy-start(bf16[512,1024]{1,0:T(8,128)(2,1)} %x_ref.3) | copy-start | bytes 3145732
  0.7 12.0 %copy-start.3 = (bf16[1024,512]{1,0:T(8,128)(2,1)S(1)}, bf16[1024,512]{1,0:T(8,128)(2,1)}, u32[]{:S(2)}) copy-start(bf16[1024,512]{1,0:T(8,128)(2,1)} %wq_ref.1) | copy-start | bytes 3145732
  0.7 12.0 %copy-start.4 = (bf16[1024,512]{1,0:T(8,128)(2,1)S(1)}, bf16[1024,512]{1,0:T(8,128)(2,1)}, u32[]{:S(2)}) copy-start(bf16[1024,512]{1,0:T(8,128)(2,1)} %wk_ref.1) | copy-start | bytes 3145732
  0.7 12.0 %copy-start.5 = (bf16[1024,512]{1,0:T(8,128)(2,1)S(1)}, bf16[1024,512]{1,0:T(8,128)(2,1)}, u32[]{:S(2)}) copy-start(bf16[1024,512]{1,0:T(8,128)(2,1)} %wv_ref.1) | copy-start | bytes 3145732
  10.5 16.8 %collective-permute-start.2 = (bf16[704,512]{1,0:T(8,128)(2,1)S(1)}, bf16[704,512]{1,0:T(8,128)(2,1)S(1)}, u32[]{:S(2)}, u32[]{:S(2)}) collective-permute-start(bf16[704,512]{1,0:T(8,128)(2,1)S(1)} %get-tuple-element.46), channel_id=1, source_target_pairs={{0,64},{32,96},{64,0},{96,32},{128,192},{160,224},{192,128},{224,1... | collective-permute-start | bytes 2162696 | tf_op jit(solution)/shard_map/ppermute | solution.py:62
  15.2 4.2 %collective-permute-start = (bf16[272,1024]{1,0:T(8,128)(2,1)S(1)}, bf16[272,1024]{1,0:T(8,128)(2,1)S(1)}, u32[]{:S(2)}, u32[]{:S(2)}) collective-permute-start(bf16[272,1024]{1,0:T(8,128)(2,1)S(1)} %get-tuple-element.42), channel_id=1, source_target_pairs={{0,1},{1,0},{2,3},{3,2},{4,5},{5,4},{6,7},{7,6},{8,9},{9,8},{10,11... | collective-permute-start | bytes 1671176 | tf_op jit(solution)/shard_map/ppermute | solution.py:62
  16.5 17.7 %collective-permute-start.4 = (bf16[704,512]{1,0:T(8,128)(2,1)S(1)}, bf16[704,512]{1,0:T(8,128)(2,1)S(1)}, u32[]{:S(2)}, u32[]{:S(2)}) collective-permute-start(bf16[704,512]{1,0:T(8,128)(2,1)S(1)} %get-tuple-element.50), channel_id=1, source_target_pairs={{0,32},{32,0},{64,96},{96,64},{128,160},{160,128},{192,224},{224,1... | collective-permute-start | bytes 2162696 | tf_op jit(solution)/shard_map/ppermute | solution.py:62
  17.5 18.7 %collective-permute-start.3 = (bf16[640,512]{1,0:T(8,128)(2,1)S(1)}, bf16[640,512]{1,0:T(8,128)(2,1)S(1)}, u32[]{:S(2)}, u32[]{:S(2)}) collective-permute-start(bf16[640,512]{1,0:T(8,128)(2,1)S(1)} %get-tuple-element.48), channel_id=1, source_target_pairs={{0,192},{32,224},{64,128},{96,160},{128,64},{160,96},{192,0},{224,... | collective-permute-start | bytes 1966088 | tf_op jit(solution)/shard_map/ppermute | solution.py:62
  19.5 17.1 %collective-permute-start.1 = (bf16[144,1024]{1,0:T(8,128)(2,1)S(1)}, bf16[144,1024]{1,0:T(8,128)(2,1)S(1)}, u32[]{:S(2)}, u32[]{:S(2)}) collective-permute-start(bf16[144,1024]{1,0:T(8,128)(2,1)S(1)} %get-tuple-element.44), channel_id=1, source_target_pairs={{0,4},{1,5},{2,6},{3,7},{4,0},{5,1},{6,2},{7,3},{8,12},{9,13},{10,... | collective-permute-start | bytes 884744 | tf_op jit(solution)/shard_map/ppermute | solution.py:62
  27.4 15.0 %collective-permute-start.6 = (bf16[352,512]{1,0:T(8,128)(2,1)S(1)}, bf16[352,512]{1,0:T(8,128)(2,1)S(1)}, u32[]{:S(2)}, u32[]{:S(2)}) collective-permute-start(bf16[352,512]{1,0:T(8,128)(2,1)S(1)} %add_convert_fusion.5.refs_3_), channel_id=1, source_target_pairs={{0,192},{32,224},{64,128},{96,160},{128,64},{160,96},{192,0},{224,... | collective-permute-start | bytes 1081352 | tf_op jit(solution)/shard_map/ppermute | solution.py:62
  34.3 9.8 %collective-permute-start.8 = (bf16[352,512]{1,0:T(8,128)(2,1)S(1)}, bf16[352,512]{1,0:T(8,128)(2,1)S(1)}, u32[]{:S(2)}, u32[]{:S(2)}) collective-permute-start(bf16[352,512]{1,0:T(8,128)(2,1)S(1)} %add_convert_fusion.4.refs_5_), channel_id=1, source_target_pairs={{0,64},{32,96},{64,0},{96,32},{128,192},{160,224},{192,128},{224,1... | collective-permute-start | bytes 1081352 | tf_op jit(solution)/shard_map/ppermute | solution.py:62
  36.3 9.2 %collective-permute-start.7 = (bf16[320,512]{1,0:T(8,128)(2,1)S(1)}, bf16[320,512]{1,0:T(8,128)(2,1)S(1)}, u32[]{:S(2)}, u32[]{:S(2)}) collective-permute-start(bf16[320,512]{1,0:T(8,128)(2,1)S(1)} %add_convert_fusion.8.refs_4_), channel_id=1, source_target_pairs={{0,32},{32,0},{64,96},{96,64},{128,160},{160,128},{192,224},{224,1... | collective-permute-start | bytes 983048 | tf_op jit(solution)/shard_map/ppermute | solution.py:62
  36.7 9.5 %collective-permute-start.5 = (bf16[80,1024]{1,0:T(8,128)(2,1)S(1)}, bf16[80,1024]{1,0:T(8,128)(2,1)S(1)}, u32[]{:S(2)}, u32[]{:S(2)}) collective-permute-start(bf16[80,1024]{1,0:T(8,128)(2,1)S(1)} %get-tuple-element.52), channel_id=1, source_target_pairs={{0,12},{1,13},{2,14},{3,15},{4,8},{5,9},{6,10},{7,11},{8,4},{9,5},... | collective-permute-start | bytes 491528 | tf_op jit(solution)/shard_map/ppermute | solution.py:62
  42.5 10.4 %collective-permute-start.10 = (bf16[352,512]{1,0:T(8,128)(2,1)S(1)}, bf16[352,512]{1,0:T(8,128)(2,1)S(1)}, u32[]{:S(2)}, u32[]{:S(2)}) collective-permute-start(bf16[352,512]{1,0:T(8,128)(2,1)S(1)} %add_convert_fusion.3.refs_4_), channel_id=1, source_target_pairs={{0,32},{32,0},{64,96},{96,64},{128,160},{160,128},{192,224},{224,1... | collective-permute-start | bytes 1081352 | tf_op jit(solution)/shard_map/ppermute | solution.py:62
  44.2 9.7 %collective-permute-start.12 = (bf16[352,512]{1,0:T(8,128)(2,1)S(1)}, bf16[352,512]{1,0:T(8,128)(2,1)S(1)}, u32[]{:S(2)}, u32[]{:S(2)}) collective-permute-start(bf16[352,512]{1,0:T(8,128)(2,1)S(1)} %add_convert_fusion.2.refs_6_), channel_id=1, source_target_pairs={{0,192},{32,224},{64,128},{96,160},{128,64},{160,96},{192,0},{224,... | collective-permute-start | bytes 1081352 | tf_op jit(solution)/shard_map/ppermute | solution.py:62
  45.7 8.5 %collective-permute-start.11 = (bf16[320,512]{1,0:T(8,128)(2,1)S(1)}, bf16[320,512]{1,0:T(8,128)(2,1)S(1)}, u32[]{:S(2)}, u32[]{:S(2)}) collective-permute-start(bf16[320,512]{1,0:T(8,128)(2,1)S(1)} %add_convert_fusion.7.refs_5_), channel_id=1, source_target_pairs={{0,64},{32,96},{64,0},{96,32},{128,192},{160,224},{192,128},{224,1... | collective-permute-start | bytes 983048 | tf_op jit(solution)/shard_map/ppermute | solution.py:62
  46.2 13.1 %collective-permute-start.9 = (bf16[80,1024]{1,0:T(8,128)(2,1)S(1)}, bf16[80,1024]{1,0:T(8,128)(2,1)S(1)}, u32[]{:S(2)}, u32[]{:S(2)}) collective-permute-start(bf16[80,1024]{1,0:T(8,128)(2,1)S(1)} %get-tuple-element.54.refs_0_), channel_id=1, source_target_pairs={{0,28},{1,29},{2,30},{3,31},{4,24},{5,25},{6,26},{7,27},{8,20},{9,... | collective-permute-start | bytes 491528 | tf_op jit(solution)/shard_map/ppermute | solution.py:62
  53.1 9.7 %collective-permute-start.14 = (bf16[352,512]{1,0:T(8,128)(2,1)S(1)}, bf16[352,512]{1,0:T(8,128)(2,1)S(1)}, u32[]{:S(2)}, u32[]{:S(2)}) collective-permute-start(bf16[352,512]{1,0:T(8,128)(2,1)S(1)} %add_convert_fusion.1.refs_2_), channel_id=1, source_target_pairs={{0,192},{32,224},{64,128},{96,160},{128,64},{160,96},{192,0},{224,... | collective-permute-start | bytes 1081352 | tf_op jit(solution)/shard_map/ppermute | solution.py:62
  54.0 9.5 %collective-permute-start.16 = (bf16[352,512]{1,0:T(8,128)(2,1)S(1)}, bf16[352,512]{1,0:T(8,128)(2,1)S(1)}, u32[]{:S(2)}, u32[]{:S(2)}) collective-permute-start(bf16[352,512]{1,0:T(8,128)(2,1)S(1)} %add_convert_fusion.refs_4_), channel_id=1, source_target_pairs={{0,64},{32,96},{64,0},{96,32},{128,192},{160,224},{192,128},{224,1... | collective-permute-start | bytes 1081352 | tf_op jit(solution)/shard_map/ppermute | solution.py:62
  54.2 9.7 %collective-permute-start.15 = (bf16[320,512]{1,0:T(8,128)(2,1)S(1)}, bf16[320,512]{1,0:T(8,128)(2,1)S(1)}, u32[]{:S(2)}, u32[]{:S(2)}) collective-permute-start(bf16[320,512]{1,0:T(8,128)(2,1)S(1)} %add_convert_fusion.6.refs_3_), channel_id=1, source_target_pairs={{0,32},{32,0},{64,96},{96,64},{128,160},{160,128},{192,224},{224,1... | collective-permute-start | bytes 983048 | tf_op jit(solution)/shard_map/ppermute | solution.py:62
  59.4 7.6 %collective-permute-start.13 = (bf16[80,1024]{1,0:T(8,128)(2,1)S(1)}, bf16[80,1024]{1,0:T(8,128)(2,1)S(1)}, u32[]{:S(2)}, u32[]{:S(2)}) collective-permute-start(bf16[80,1024]{1,0:T(8,128)(2,1)S(1)} %get-tuple-element.56.mine_ref), channel_id=1, source_target_pairs={{0,2},{1,3},{2,0},{3,1},{4,6},{5,7},{6,4},{7,5},{8,10},{9,11},{10,... | collective-permute-start | bytes 491528 | tf_op jit(solution)/shard_map/ppermute | solution.py:62
  62.8 4.2 %copy-start.1 = (bf16[512,1024]{1,0:T(8,128)(2,1)S(1)}, bf16[512,1024]{1,0:T(8,128)(2,1)}, u32[]{:S(2)}) copy-start(bf16[512,1024]{1,0:T(8,128)(2,1)} %og_ref.1) | copy-start | bytes 3145732
  62.8 4.2 %copy-start.2 = (f32[1024]{0:T(1024)S(1)}, f32[1024]{0:T(1024)}, u32[]{:S(2)}) copy-start(f32[1024]{0:T(1024)} %param.11) | copy-start | bytes 12292
  62.8 22.8 %collective-permute-start.19 = (bf16[704,512]{1,0:T(8,128)(2,1)S(1)}, bf16[704,512]{1,0:T(8,128)(2,1)S(1)}, u32[]{:S(2)}, u32[]{:S(2)}) collective-permute-start(bf16[704,512]{1,0:T(8,128)(2,1)S(1)} %pad_maximum_fusion.refs_0_), channel_id=1, source_target_pairs={{0,64},{32,96},{64,0},{96,32},{128,192},{160,224},{192,128},{224,1... | collective-permute-start | bytes 2162696 | tf_op jit(solution)/shard_map/ppermute | solution.py:62
  63.6 22.1 %collective-permute-start.21 = (bf16[704,512]{1,0:T(8,128)(2,1)S(1)}, bf16[704,512]{1,0:T(8,128)(2,1)}, u32[]{:S(2)}, u32[]{:S(2)}) collective-permute-start(bf16[704,512]{1,0:T(8,128)(2,1)S(1)} %pad_maximum_fusion.1.refs_2_), channel_id=1, source_target_pairs={{0,32},{32,0},{64,96},{96,64},{128,160},{160,128},{192,224},{224,1... | collective-permute-start | bytes 2162696 | tf_op jit(solution)/shard_map/ppermute | solution.py:62
  64.0 21.6 %collective-permute-start.20 = (bf16[640,512]{1,0:T(8,128)(2,1)S(1)}, bf16[640,512]{1,0:T(8,128)(2,1)}, u32[]{:S(2)}, u32[]{:S(2)}) collective-permute-start(bf16[640,512]{1,0:T(8,128)(2,1)S(1)} %pad_maximum_fusion.2.refs_1_), channel_id=1, source_target_pairs={{0,192},{32,224},{64,128},{96,160},{128,64},{160,96},{192,0},{224,... | collective-permute-start | bytes 1966088 | tf_op jit(solution)/shard_map/ppermute | solution.py:62
  68.3 6.8 %collective-permute-start.17 = (bf16[64,1024]{1,0:T(8,128)(2,1)S(1)}, bf16[64,1024]{1,0:T(8,128)(2,1)S(1)}, u32[]{:S(2)}, u32[]{:S(2)}) collective-permute-start(bf16[64,1024]{1,0:T(8,128)(2,1)S(1)} %get-tuple-element.57), channel_id=1, source_target_pairs={{0,12},{1,13},{2,14},{3,15},{4,8},{5,9},{6,10},{7,11},{8,4},{9,5},... | collective-permute-start | bytes 393224 | tf_op jit(solution)/shard_map/ppermute | solution.py:62
  75.1 9.5 %collective-permute-start.18 = (bf16[128,1024]{1,0:T(8,128)(2,1)S(1)}, bf16[128,1024]{1,0:T(8,128)(2,1)}, u32[]{:S(2)}, u32[]{:S(2)}) collective-permute-start(bf16[128,1024]{1,0:T(8,128)(2,1)S(1)} %pad_maximum_fusion.4), channel_id=1, source_target_pairs={{0,4},{1,5},{2,6},{3,7},{4,0},{5,1},{6,2},{7,3},{8,12},{9,13},{10,... | collective-permute-start | bytes 786440 | tf_op jit(solution)/shard_map/ppermute | solution.py:62
  75.2 8.7 %all-to-all-start = ((f32[8,8,128]{2,1,0:T(8,128)}), f32[8,8,128]{2,1,0:T(8,128)S(1)}, u32[]{:S(2)}, u32[]{:S(2)}) async-start(f32[8,8,128]{2,1,0:T(8,128)} %get-tuple-element.67), calls=%async_computation | async-start | bytes 65536 | tf_op jit(solution)/shard_map/all_to_all | solution.py:426
  85.6 11.5 %collective-permute-start.22 = (bf16[256,1024]{1,0:T(8,128)(2,1)S(1)}, bf16[256,1024]{1,0:T(8,128)(2,1)S(1)}, u32[]{:S(2)}, u32[]{:S(2)}) collective-permute-start(bf16[256,1024]{1,0:T(8,128)(2,1)S(1)} %pad_maximum_fusion.3.low_ref), channel_id=1, source_target_pairs={{0,1},{1,0},{2,3},{3,2},{4,5},{5,4},{6,7},{7,6},{8,9},{9,8},{10,11... | collective-permute-start | bytes 1572872 | tf_op jit(solution)/shard_map/ppermute | solution.py:62

commit v4 on v3

--- a/solution.py
+++ b/solution.py
@@ -405,25 +405,26 @@
     r1 = swap(m_send, "core")
     send, gain = mp_step(gain, (m_keep, r1), 128, 128)
     r2 = swap(send, "g0")
-    second = [plus(k[2 * n :], r[2 * n :]) for k, r, n in zip(keeps, first, sizes)]
-    send, gain = mp_step(gain, (m_keep, r1, r2), 64, 64, second)
-    second = [swap(v, o[1]) for v, o in zip(second, ORDERS)]
+    send, gain = mp_step(gain, (m_keep, r1, r2), 64, 64)
+    second = [after(plus(k[2 * n :], r[2 * n :]), [send]) for k, r, n in zip(keeps, first, sizes)]
     r3 = swap(send, "g1")
-    mine = [plus(k[: 2 * n], r[: 2 * n], s) for k, r, s, n in zip(keeps, first, second, sizes)]
+    received = [swap(v, o[1]) for v, o in zip(second, ORDERS)]
+    send, gain = mp_step(gain, (m_keep, r1, r2, r3), 64, 0, second)
+    r4 = swap(send, "g2")
+    mine = [plus(k[: 2 * n], r[: 2 * n], s) for k, r, s, n in zip(keeps, first, received, sizes)]
     third = [swap(v, o[2]) for v, o in zip(mine, ORDERS)]
-    send, gain = mp_step(gain, (m_keep, r1, r2, r3), 64, 0, mine)
-    r4 = swap(send, "g2")
-    quarter = [plus(v, t) for v, t in zip(mine, third)]
+    send, gain = mp_step(gain, (send, r4), 64, 0, mine)
+    r5 = swap(send, "xh")
+    quarter = [after(plus(v, t), [send]) for v, t in zip(mine, third)]
     back = [swap(v, o[1]) for v, o in zip(quarter, ORDERS)]
     half = [jnp.concatenate([v, b]) for v, b in zip(quarter, back)]
     last = [swap(v, o[0]) for v, o in zip(half, ORDERS)]
-    send, gain = mp_step(gain, (send, r4), 64, 0, quarter)
-    r5 = swap(send, "xh")
-    rows, gains = own_rows(where, inputs, output_gradient, weight, gain, send, r5, half)
+    rows, gains = own_rows(where, inputs, output_gradient, weight, gain, send, r5, quarter)
     *outs, placed = place(0, where, half, (), depth, width)
-    for step in ("g1", "g0"):
-        rows = jnp.concatenate([rows, swap(rows, step)])
-    gains = lax.all_to_all(gains, "dp", 0, 0)
+    got = swap(rows, "g1")
+    rows = jnp.concatenate([after(rows, half), got])
+    rows = jnp.concatenate([rows, swap(rows, "g0")])
+    gains = lax.all_to_all(after(gains, half), "dp", 0, 0)
     rows = after(rows, last)
     grad_inputs = place_rows(where, rows, swap(rows, "core"))
     outs = place(1, where, last, outs, depth, width)

time: 99.1 us -> 102 us (1.029)
  waiting for transfers between devices: 24.9 us -> 37 us
  starting transfers between devices: 49.1 us -> 40.4 us
    ppermute x23, waiting for transfers between devices: 22.3 us -> 34.6 us  [swap(): return lax.ppermute(value, axis, pairs)]
    ppermute x23, starting transfers between devices: 45.8 us -> 36.5 us  [swap(): return lax.ppermute(value, axis, pairs)]
  transfers between devices with their start and end apart: 24 -> 24, of which waited for: 11 -> 12; matrix products, arithmetic and copies ran while one was open for 3% -> 3% of each run, Pallas kernels for 10% -> 9%
where the time goes in v4:
time: 102 us
  starting transfers between devices  40.4 us (40%)
  waiting for transfers between devices  37 us (36%)
  Pallas kernels  21.1 us (21%)
  other arithmetic  2.62 us (3%)
    ppermute x23, starting transfers between devices, swap(): return lax.ppermute(value, axis, pairs)  36.5 us
    ppermute x23, waiting for transfers between devices, swap(): return lax.ppermute(value, axis, pairs)  34.6 us
    pallas_call x1, Pallas kernels, front(): pl.pallas_call(front_kernel, in_specs=[SCALARS, *[pl.BlockSpec(memory_spa...  9.79 us
    pallas_call x2, Pallas kernels, place(): pl.pallas_call(functools.partial(place_kernel, late), in_specs=[SCALARS,...  5.54 us
    all_to_all x1, starting transfers between devices, shards(): gains = lax.all_to_all(after(gains, half), 'dp', 0, 0)  3.91 us
    pallas_call x1, Pallas kernels, total_share(): pl.pallas_call(total_kernel, in_specs=[SCALARS, *whole(7)], out_specs=who...  2.49 us
    all_to_all x1, waiting for transfers between devices, shards(): gains = lax.all_to_all(after(gains, half), 'dp', 0, 0)  2.42 us
  transfers between devices with their start and end apart: 24, of which 12 were waited for; matrix products, arithmetic and copies ran while one was open for 3% of the time, Pallas kernels for 9%

profile of v4, /device:TPU:1, one launch (start us, length us, event | category | flops | bytes accessed | tf_op | source)
XLA Modules:
  0.0 102.2 jit_solution(16199821671346372749)
XLA Ops:
  0.6 0.1 pad_add_fusion.where
  0.7 9.8 %front.1 = (bf16[704,512]{1,0:T(8,128)(2,1)S(1)}, bf16[704,512]{1,0:T(8,128)(2,1)S(1)}, bf16[640,512]{1,0:T(8,128)(2,1)S(1)}, bf16[640,512]{1,0:T(8,128)(2,1)S(1...) custom-call(s32[2]{0:T(128)S(1)} %pad_add_fusion.where, ...), custom_call_target="tpu_custom_call" | custom-call | flops 8589934592 | bytes 16777216 | tf_op jit(solution)/shard_map/front/pallas_call | solution.py:191
  10.5 3.7 %collective-permute-start.4 = (bf16[640,512]{1,0:T(8,128)(2,1)S(1)}, bf16[640,512]{1,0:T(8,128)(2,1)S(1)}, u32[]{:S(2)}, u32[]{:S(2)}) collective-permute-start(bf16[640,512]{1,0:T(8,128)(2,1)S(1)} %get-tuple-element.59), channel_id=1, source_target_pairs={{0,192},{32,224},{64,128},{96,160},{128,64},{160,96},{192,0},{224,... | collective-permute-start | bytes 1966088 | tf_op jit(solution)/shard_map/ppermute | solution.py:62
  14.2 2.5 %total_share.1 = (bf16[272,1024]{1,0:T(8,128)(2,1)S(1)}, bf16[256,1024]{1,0:T(8,128)(2,1)S(1)}, f32[1,1024]{1,0:T(1,128)S(1)}) custom-call(s32[2]{0:T(128)S(1)} %pad_add_fusion.where, bf16[512,1024]{1,0:T(8,128)(2,1)S(1)} %copy-done, bf16[512,512]{1,0:T(8,128)(2,1)S(1)} %get-tuple-element.45.gq_ref, bf16[512,512]{1,0:T(8,128)(2,1)S(1)} %get-tuple-element.46.gk_ref, ...), custom_call_target="tpu_custom_call" | custom-call | flops 2147483648 | bytes 8388608 | tf_op jit(solution)/shard_map/total_share/pallas_call | solution.py:227
  16.7 1.0 %collective-permute-start = (bf16[272,1024]{1,0:T(8,128)(2,1)S(1)}, bf16[272,1024]{1,0:T(8,128)(2,1)S(1)}, u32[]{:S(2)}, u32[]{:S(2)}) collective-permute-start(bf16[272,1024]{1,0:T(8,128)(2,1)S(1)} %get-tuple-element.50), channel_id=1, source_target_pairs={{0,1},{1,0},{2,3},{3,2},{4,5},{5,4},{6,7},{7,6},{8,9},{9,8},{10,11... | collective-permute-start | bytes 1671176 | tf_op jit(solution)/shard_map/ppermute | solution.py:62
  17.7 1.2 %collective-permute-start.5 = (bf16[704,512]{1,0:T(8,128)(2,1)S(1)}, bf16[704,512]{1,0:T(8,128)(2,1)S(1)}, u32[]{:S(2)}, u32[]{:S(2)}) collective-permute-start(bf16[704,512]{1,0:T(8,128)(2,1)S(1)} %get-tuple-element.62), channel_id=1, source_target_pairs={{0,32},{32,0},{64,96},{96,64},{128,160},{160,128},{192,224},{224,1... | collective-permute-start | bytes 2162696 | tf_op jit(solution)/shard_map/ppermute | solution.py:62
  18.9 0.4 collective-permute-done.refs_1_
  19.3 0.1 mp_step.4
  19.4 1.7 %collective-permute-start.1 = (bf16[144,1024]{1,0:T(8,128)(2,1)S(1)}, bf16[144,1024]{1,0:T(8,128)(2,1)S(1)}, u32[]{:S(2)}, u32[]{:S(2)}) collective-permute-start(bf16[144,1024]{1,0:T(8,128)(2,1)S(1)} %get-tuple-element.52), channel_id=1, source_target_pairs={{0,4},{1,5},{2,6},{3,7},{4,0},{5,1},{6,2},{7,3},{8,12},{9,13},{10,... | collective-permute-start | bytes 884744 | tf_op jit(solution)/shard_map/ppermute | solution.py:62
  21.1 6.4 %collective-permute-done.4 = bf16[640,512]{1,0:T(8,128)(2,1)S(1)} collective-permute-done((bf16[640,512]{1,0:T(8,128)(2,1)S(1)}, bf16[640,512]{1,0:T(8,128)(2,1)S(1)}, u32[]{:S(2)}, u32[]{:S(2)}) %collective-permute-start.4) | collective-permute-done | bytes 655392 | tf_op jit(solution)/shard_map/ppermute | solution.py:62
  27.6 0.1 add_convert_fusion.8.refs_5_
  27.7 0.4 collective-permute-done.1.refs_2_
  28.1 0.1 mp_step.5
  28.2 1.9 %collective-permute-start.8 = (bf16[320,512]{1,0:T(8,128)(2,1)S(1)}, bf16[320,512]{1,0:T(8,128)(2,1)S(1)}, u32[]{:S(2)}, u32[]{:S(2)}) collective-permute-start(bf16[320,512]{1,0:T(8,128)(2,1)S(1)} %add_convert_fusion.8.refs_5_), channel_id=1, source_target_pairs={{0,32},{32,0},{64,96},{96,64},{128,160},{160,128},{192,224},{224,1... | collective-permute-start | bytes 983048 | tf_op jit(solution)/shard_map/ppermute | solution.py:62
  30.0 5.4 %collective-permute-done.3 = bf16[704,512]{1,0:T(8,128)(2,1)S(1)} collective-permute-done((bf16[704,512]{1,0:T(8,128)(2,1)S(1)}, bf16[704,512]{1,0:T(8,128)(2,1)S(1)}, u32[]{:S(2)}, u32[]{:S(2)}) %collective-permute-start.3) | collective-permute-done | bytes 720928 | tf_op jit(solution)/shard_map/ppermute | solution.py:62
  35.4 0.1 add_convert_fusion.5.refs_4_
  35.5 4.4 %collective-permute-start.2 = (bf16[80,1024]{1,0:T(8,128)(2,1)S(1)}, bf16[80,1024]{1,0:T(8,128)(2,1)S(1)}, u32[]{:S(2)}, u32[]{:S(2)}) collective-permute-start(bf16[80,1024]{1,0:T(8,128)(2,1)S(1)} %get-tuple-element.54), channel_id=1, source_target_pairs={{0,12},{1,13},{2,14},{3,15},{4,8},{5,9},{6,10},{7,11},{8,4},{9,5},... | collective-permute-start | bytes 491528 | tf_op jit(solution)/shard_map/ppermute | solution.py:62
  40.0 0.0 collective-permute-done.5
  40.0 0.1 add_convert_fusion.4.refs_6_
  40.1 0.2 collective-permute-start.9
  40.3 3.5 %collective-permute-done.2.refs_3_ = bf16[80,1024]{1,0:T(8,128)(2,1)S(1)} collective-permute-done((bf16[80,1024]{1,0:T(8,128)(2,1)S(1)}, bf16[80,1024]{1,0:T(8,128)(2,1)S(1)}, u32[]{:S(2)}, u32[]{:S(2)}) %collective-permute-start.2) | collective-permute-done | bytes 163872 | tf_op jit(solution)/shard_map/ppermute | solution.py:62
  43.7 0.1 mp_step.6
  43.8 4.3 %collective-permute-start.6 = (bf16[80,1024]{1,0:T(8,128)(2,1)S(1)}, bf16[80,1024]{1,0:T(8,128)(2,1)S(1)}, u32[]{:S(2)}, u32[]{:S(2)}) collective-permute-start(bf16[80,1024]{1,0:T(8,128)(2,1)S(1)} %get-tuple-element.65.refs_0_), channel_id=1, source_target_pairs={{0,28},{1,29},{2,30},{3,31},{4,24},{5,25},{6,26},{7,27},{8,20},{9,... | collective-permute-start | bytes 491528 | tf_op jit(solution)/shard_map/ppermute | solution.py:62
  48.1 0.0 collective-permute-done.8
  48.1 0.1 add_convert_fusion.7.refs_3_
  48.2 0.4 collective-permute-start.12
  48.6 1.3 %collective-permute-done.7 = bf16[352,512]{1,0:T(8,128)(2,1)S(1)} collective-permute-done((bf16[352,512]{1,0:T(8,128)(2,1)S(1)}, bf16[352,512]{1,0:T(8,128)(2,1)S(1)}, u32[]{:S(2)}, u32[]{:S(2)}) %collective-permute-start.7) | collective-permute-done | bytes 360480 | tf_op jit(solution)/shard_map/ppermute | solution.py:62
  49.9 0.1 add_convert_fusion.3.refs_2_
  50.1 1.3 %collective-permute-start.11 = (bf16[352,512]{1,0:T(8,128)(2,1)S(1)}, bf16[352,512]{1,0:T(8,128)(2,1)S(1)}, u32[]{:S(2)}, u32[]{:S(2)}) collective-permute-start(bf16[352,512]{1,0:T(8,128)(2,1)S(1)} %add_convert_fusion.3.refs_2_), channel_id=1, source_target_pairs={{0,32},{32,0},{64,96},{96,64},{128,160},{160,128},{192,224},{224,1... | collective-permute-start | bytes 1081352 | tf_op jit(solution)/shard_map/ppermute | solution.py:62
  51.4 0.0 collective-permute-done.9
  51.4 0.1 add_convert_fusion.2.refs_4_
  51.5 0.1 collective-permute-start.13
  51.6 0.0 collective-permute-done.6.refs_1_
  51.6 0.1 mp_step.7
  51.7 2.7 %collective-permute-start.10 = (bf16[80,1024]{1,0:T(8,128)(2,1)S(1)}, bf16[80,1024]{1,0:T(8,128)(2,1)S(1)}, u32[]{:S(2)}, u32[]{:S(2)}) collective-permute-start(bf16[80,1024]{1,0:T(8,128)(2,1)S(1)} %get-tuple-element.67.mine_ref), channel_id=1, source_target_pairs={{0,2},{1,3},{2,0},{3,1},{4,6},{5,7},{6,4},{7,5},{8,10},{9,11},{10,... | collective-permute-start | bytes 491528 | tf_op jit(solution)/shard_map/ppermute | solution.py:62
  54.4 1.0 %collective-permute-done.12 = bf16[320,512]{1,0:T(8,128)(2,1)S(1)} collective-permute-done((bf16[320,512]{1,0:T(8,128)(2,1)S(1)}, bf16[320,512]{1,0:T(8,128)(2,1)S(1)}, u32[]{:S(2)}, u32[]{:S(2)}) %collective-permute-start.12) | collective-permute-done | bytes 327712 | tf_op jit(solution)/shard_map/ppermute | solution.py:62
  55.5 0.1 add_convert_fusion.6.refs_1_
  55.5 1.3 %collective-permute-start.15 = (bf16[320,512]{1,0:T(8,128)(2,1)S(1)}, bf16[320,512]{1,0:T(8,128)(2,1)S(1)}, u32[]{:S(2)}, u32[]{:S(2)}) collective-permute-start(bf16[320,512]{1,0:T(8,128)(2,1)S(1)} %add_convert_fusion.6.refs_1_), channel_id=1, source_target_pairs={{0,32},{32,0},{64,96},{96,64},{128,160},{160,128},{192,224},{224,1... | collective-permute-start | bytes 983048 | tf_op jit(solution)/shard_map/ppermute | solution.py:62
  56.9 3.5 %collective-permute-done.13 = bf16[352,512]{1,0:T(8,128)(2,1)S(1)} collective-permute-done((bf16[352,512]{1,0:T(8,128)(2,1)S(1)}, bf16[352,512]{1,0:T(8,128)(2,1)S(1)}, u32[]{:S(2)}, u32[]{:S(2)}) %collective-permute-start.13) | collective-permute-done | bytes 360480 | tf_op jit(solution)/shard_map/ppermute | solution.py:62
  60.3 0.1 add_convert_fusion.refs_2_
  60.4 0.1 collective-permute-start.16
  60.5 0.0 collective-permute-done.11
  60.6 0.1 add_convert_fusion.1.refs_0_
  60.6 0.1 collective-permute-start.14
  60.8 0.0 copy-start.1
  60.8 6.3 %collective-permute-done.16 = bf16[352,512]{1,0:T(8,128)(2,1)S(1)} collective-permute-done((bf16[352,512]{1,0:T(8,128)(2,1)S(1)}, bf16[352,512]{1,0:T(8,128)(2,1)S(1)}, u32[]{:S(2)}, u32[]{:S(2)}) %collective-permute-start.16) | collective-permute-done | bytes 360480 | tf_op jit(solution)/shard_map/ppermute | solution.py:62
  67.2 0.3 collective-permute-start.21
  67.5 1.0 %collective-permute-done.14 = bf16[352,512]{1,0:T(8,128)(2,1)S(1)} collective-permute-done((bf16[352,512]{1,0:T(8,128)(2,1)S(1)}, bf16[352,512]{1,0:T(8,128)(2,1)S(1)}, u32[]{:S(2)}, u32[]{:S(2)}) %collective-permute-start.14) | collective-permute-done | bytes 360480 | tf_op jit(solution)/shard_map/ppermute | solution.py:62
  68.6 0.3 collective-permute-start.19
  68.9 0.0 collective-permute-done.15
  68.9 0.7 collective-permute-start.20
  69.6 0.0 collective-permute-done.10.got_ref
  69.6 1.3 %own_rows.1 = (bf16[64,1024]{1,0:T(8,128)(2,1)S(1)}, f32[8,8,128]{2,1,0:T(8,128)}) custom-call(s32[2]{0:T(128)S(1)} %pad_add_fusion.where, bf16[512,1024]{1,0:T(8,128)(2,1)S(1)} %copy-done, bf16[512,1024]{1,0:T(8,128)(2,1)S(1)} %copy-done.1, f32[1,1024]{1,0:T(1,128)S(1)} %bitcast.5, f32[1,1024]{1,0:T(1,128)S(1)} %get-tuple-element.66.gain_ref, ...), custom_call_target="tpu_custom_call" | custom-call | flops 1024 | bytes 1024 | tf_op jit(solution)/shard_map/own_rows/pallas_call | solution.py:290
  70.9 0.4 collective-permute-start.17
  71.3 5.3 %collective-permute-done.17 = bf16[64,1024]{1,0:T(8,128)(2,1)S(1)} collective-permute-done((bf16[64,1024]{1,0:T(8,128)(2,1)S(1)}, bf16[64,1024]{1,0:T(8,128)(2,1)S(1)}, u32[]{:S(2)}, u32[]{:S(2)}) %collective-permute-start.17) | collective-permute-done | bytes 131104 | tf_op jit(solution)/shard_map/ppermute | solution.py:62
  76.7 1.8 %collective-permute-start.18 = (bf16[128,1024]{1,0:T(8,128)(2,1)S(1)}, bf16[128,1024]{1,0:T(8,128)(2,1)}, u32[]{:S(2)}, u32[]{:S(2)}) collective-permute-start(bf16[128,1024]{1,0:T(8,128)(2,1)S(1)} %pad_maximum_fusion.1), channel_id=1, source_target_pairs={{0,4},{1,5},{2,6},{3,7},{4,0},{5,1},{6,2},{7,3},{8,12},{9,13},{10,... | collective-permute-start | bytes 786440 | tf_op jit(solution)/shard_map/ppermute | solution.py:62
  78.5 3.9 %all-to-all-start = ((f32[8,8,128]{2,1,0:T(8,128)}), f32[8,8,128]{2,1,0:T(8,128)S(1)}, u32[]{:S(2)}, u32[]{:S(2)}) async-start(f32[8,8,128]{2,1,0:T(8,128)} %get-tuple-element.83), calls=%async_computation | async-start | bytes 65536 | tf_op jit(solution)/shard_map/all_to_all | solution.py:427
  82.4 2.7 %place_early.1 = (bf16[1024,512]{1,0:T(8,128)(2,1)}, bf16[1024,512]{1,0:T(8,128)(2,1)}, bf16[1024,512]{1,0:T(8,128)(2,1)}, bf16[512,1024]{1,0:T(8,128)(2,1)}, f32[8,128]{1,0:T(8,128)}) custom-call(s32[2]{0:T(128)S(1)} %pad_add_fusion.where, bf16[704,512]{1,0:T(8,128)(2,1)S(1)} %constant_dynamic-update-slice_fusion.refs_0_, ...), custom_call_target="tpu_custom_call" | custom-call | flops 1024 | bytes 1024 | tf_op jit(solution)/shard_map/place_early/pallas_call | solution.py:333
  85.1 2.4 %all-to-all-done = f32[8,8,128]{2,1,0:T(8,128)S(1)} async-done(((f32[8,8,128]{2,1,0:T(8,128)}), f32[8,8,128]{2,1,0:T(8,128)S(1)}, u32[]{:S(2)}, u32[]{:S(2)}) %all-to-all-start) | async-done | bytes 32800 | tf_op jit(solution)/shard_map/all_to_all | solution.py:427
  87.5 0.6 reduce_sum.9
  88.1 1.0 pad_maximum_fusion.low_ref
  89.2 8.4 %collective-permute-start.22 = (bf16[256,1024]{1,0:T(8,128)(2,1)S(1)}, bf16[256,1024]{1,0:T(8,128)(2,1)S(1)}, u32[]{:S(2)}, u32[]{:S(2)}) collective-permute-start(bf16[256,1024]{1,0:T(8,128)(2,1)S(1)} %pad_maximum_fusion.low_ref), channel_id=1, source_target_pairs={{0,1},{1,0},{2,3},{3,2},{4,5},{5,4},{6,7},{7,6},{8,9},{9,8},{10,11... | collective-permute-start | bytes 1572872 | tf_op jit(solution)/shard_map/ppermute | solution.py:62
  97.6 2.9 %place_late.1 = (bf16[1024,512]{1,0:T(8,128)(2,1)}, bf16[1024,512]{1,0:T(8,128)(2,1)}, bf16[1024,512]{1,0:T(8,128)(2,1)}, bf16[512,1024]{1,0:T(8,128)(2,1)}) custom-call(s32[2]{0:T(128)S(1)} %pad_add_fusion.where, bf16[704,512]{1,0:T(8,128)(2,1)} %collective-permute-done.19.refs_0_, ...), custom_call_target="tpu_custom_call", output_to_operand_aliasing={{0}: (4, {}), {1}: (5, {}), {2}: (6, {}), {3}: (7, {})} | custom-call | flops 68719476736 | bytes 1024 | tf_op jit(solution)/shard_map/place_late/pallas_call | solution.py:333
  100.5 1.6 %place_rows.1 = bf16[512,1024]{1,0:T(8,128)(2,1)} custom-call(s32[2]{0:T(128)S(1)} %pad_add_fusion.where, bf16[256,1024]{1,0:T(8,128)(2,1)S(1)} %pad_maximum_fusion.low_ref, bf16[256,1024]{1,0:T(8,128)(2,1)S(1)} %collective-permute-done.22.high_ref), custom_call_target="tpu_custom_call" | custom-call | flops 1024 | bytes 2097152 | tf_op jit(solution)/shard_map/place_rows/pallas_call | solution.py:360
  (25 shorter events, 0.2 us)
Async XLA Ops:
  0.7 13.5 %copy-start = (bf16[512,1024]{1,0:T(8,128)(2,1)S(1)}, bf16[512,1024]{1,0:T(8,128)(2,1)}, u32[]{:S(2)}) copy-start(bf16[512,1024]{1,0:T(8,128)(2,1)} %x_ref.3) | copy-start | bytes 3145732
  0.7 13.5 %copy-start.3 = (bf16[1024,512]{1,0:T(8,128)(2,1)S(1)}, bf16[1024,512]{1,0:T(8,128)(2,1)}, u32[]{:S(2)}) copy-start(bf16[1024,512]{1,0:T(8,128)(2,1)} %wq_ref.1) | copy-start | bytes 3145732
  0.7 13.5 %copy-start.4 = (bf16[1024,512]{1,0:T(8,128)(2,1)S(1)}, bf16[1024,512]{1,0:T(8,128)(2,1)}, u32[]{:S(2)}) copy-start(bf16[1024,512]{1,0:T(8,128)(2,1)} %wk_ref.1) | copy-start | bytes 3145732
  0.7 13.5 %copy-start.5 = (bf16[1024,512]{1,0:T(8,128)(2,1)S(1)}, bf16[1024,512]{1,0:T(8,128)(2,1)}, u32[]{:S(2)}) copy-start(bf16[1024,512]{1,0:T(8,128)(2,1)} %wv_ref.1) | copy-start | bytes 3145732
  10.5 17.1 %collective-permute-start.4 = (bf16[640,512]{1,0:T(8,128)(2,1)S(1)}, bf16[640,512]{1,0:T(8,128)(2,1)S(1)}, u32[]{:S(2)}, u32[]{:S(2)}) collective-permute-start(bf16[640,512]{1,0:T(8,128)(2,1)S(1)} %get-tuple-element.59), channel_id=1, source_target_pairs={{0,192},{32,224},{64,128},{96,160},{128,64},{160,96},{192,0},{224,... | collective-permute-start | bytes 1966088 | tf_op jit(solution)/shard_map/ppermute | solution.py:62
  16.7 2.6 %collective-permute-start = (bf16[272,1024]{1,0:T(8,128)(2,1)S(1)}, bf16[272,1024]{1,0:T(8,128)(2,1)S(1)}, u32[]{:S(2)}, u32[]{:S(2)}) collective-permute-start(bf16[272,1024]{1,0:T(8,128)(2,1)S(1)} %get-tuple-element.50), channel_id=1, source_target_pairs={{0,1},{1,0},{2,3},{3,2},{4,5},{5,4},{6,7},{7,6},{8,9},{9,8},{10,11... | collective-permute-start | bytes 1671176 | tf_op jit(solution)/shard_map/ppermute | solution.py:62
  17.7 17.7 %collective-permute-start.3 = (bf16[704,512]{1,0:T(8,128)(2,1)S(1)}, bf16[704,512]{1,0:T(8,128)(2,1)S(1)}, u32[]{:S(2)}, u32[]{:S(2)}) collective-permute-start(bf16[704,512]{1,0:T(8,128)(2,1)S(1)} %get-tuple-element.56), channel_id=1, source_target_pairs={{0,64},{32,96},{64,0},{96,32},{128,192},{160,224},{192,128},{224,1... | collective-permute-start | bytes 2162696 | tf_op jit(solution)/shard_map/ppermute | solution.py:62
  17.7 22.2 %collective-permute-start.5 = (bf16[704,512]{1,0:T(8,128)(2,1)S(1)}, bf16[704,512]{1,0:T(8,128)(2,1)S(1)}, u32[]{:S(2)}, u32[]{:S(2)}) collective-permute-start(bf16[704,512]{1,0:T(8,128)(2,1)S(1)} %get-tuple-element.62), channel_id=1, source_target_pairs={{0,32},{32,0},{64,96},{96,64},{128,160},{160,128},{192,224},{224,1... | collective-permute-start | bytes 2162696 | tf_op jit(solution)/shard_map/ppermute | solution.py:62
  19.4 8.7 %collective-permute-start.1 = (bf16[144,1024]{1,0:T(8,128)(2,1)S(1)}, bf16[144,1024]{1,0:T(8,128)(2,1)S(1)}, u32[]{:S(2)}, u32[]{:S(2)}) collective-permute-start(bf16[144,1024]{1,0:T(8,128)(2,1)S(1)} %get-tuple-element.52), channel_id=1, source_target_pairs={{0,4},{1,5},{2,6},{3,7},{4,0},{5,1},{6,2},{7,3},{8,12},{9,13},{10,... | collective-permute-start | bytes 884744 | tf_op jit(solution)/shard_map/ppermute | solution.py:62
  28.2 19.9 %collective-permute-start.8 = (bf16[320,512]{1,0:T(8,128)(2,1)S(1)}, bf16[320,512]{1,0:T(8,128)(2,1)S(1)}, u32[]{:S(2)}, u32[]{:S(2)}) collective-permute-start(bf16[320,512]{1,0:T(8,128)(2,1)S(1)} %add_convert_fusion.8.refs_5_), channel_id=1, source_target_pairs={{0,32},{32,0},{64,96},{96,64},{128,160},{160,128},{192,224},{224,1... | collective-permute-start | bytes 983048 | tf_op jit(solution)/shard_map/ppermute | solution.py:62
  35.5 8.2 %collective-permute-start.2 = (bf16[80,1024]{1,0:T(8,128)(2,1)S(1)}, bf16[80,1024]{1,0:T(8,128)(2,1)S(1)}, u32[]{:S(2)}, u32[]{:S(2)}) collective-permute-start(bf16[80,1024]{1,0:T(8,128)(2,1)S(1)} %get-tuple-element.54), channel_id=1, source_target_pairs={{0,12},{1,13},{2,14},{3,15},{4,8},{5,9},{6,10},{7,11},{8,4},{9,5},... | collective-permute-start | bytes 491528 | tf_op jit(solution)/shard_map/ppermute | solution.py:62
  39.9 10.0 %collective-permute-start.7 = (bf16[352,512]{1,0:T(8,128)(2,1)S(1)}, bf16[352,512]{1,0:T(8,128)(2,1)S(1)}, u32[]{:S(2)}, u32[]{:S(2)}) collective-permute-start(bf16[352,512]{1,0:T(8,128)(2,1)S(1)} %add_convert_fusion.5.refs_4_), channel_id=1, source_target_pairs={{0,192},{32,224},{64,128},{96,160},{128,64},{160,96},{192,0},{224,... | collective-permute-start | bytes 1081352 | tf_op jit(solution)/shard_map/ppermute | solution.py:62
  40.1 11.3 %collective-permute-start.9 = (bf16[352,512]{1,0:T(8,128)(2,1)S(1)}, bf16[352,512]{1,0:T(8,128)(2,1)S(1)}, u32[]{:S(2)}, u32[]{:S(2)}) collective-permute-start(bf16[352,512]{1,0:T(8,128)(2,1)S(1)} %add_convert_fusion.4.refs_6_), channel_id=1, source_target_pairs={{0,64},{32,96},{64,0},{96,32},{128,192},{160,224},{192,128},{224,1... | collective-permute-start | bytes 1081352 | tf_op jit(solution)/shard_map/ppermute | solution.py:62
  43.8 7.8 %collective-permute-start.6 = (bf16[80,1024]{1,0:T(8,128)(2,1)S(1)}, bf16[80,1024]{1,0:T(8,128)(2,1)S(1)}, u32[]{:S(2)}, u32[]{:S(2)}) collective-permute-start(bf16[80,1024]{1,0:T(8,128)(2,1)S(1)} %get-tuple-element.65.refs_0_), channel_id=1, source_target_pairs={{0,28},{1,29},{2,30},{3,31},{4,24},{5,25},{6,26},{7,27},{8,20},{9,... | collective-permute-start | bytes 491528 | tf_op jit(solution)/shard_map/ppermute | solution.py:62
  48.2 7.2 %collective-permute-start.12 = (bf16[320,512]{1,0:T(8,128)(2,1)S(1)}, bf16[320,512]{1,0:T(8,128)(2,1)S(1)}, u32[]{:S(2)}, u32[]{:S(2)}) collective-permute-start(bf16[320,512]{1,0:T(8,128)(2,1)S(1)} %add_convert_fusion.7.refs_3_), channel_id=1, source_target_pairs={{0,64},{32,96},{64,0},{96,32},{128,192},{160,224},{192,128},{224,1... | collective-permute-start | bytes 983048 | tf_op jit(solution)/shard_map/ppermute | solution.py:62
  50.1 10.5 %collective-permute-start.11 = (bf16[352,512]{1,0:T(8,128)(2,1)S(1)}, bf16[352,512]{1,0:T(8,128)(2,1)S(1)}, u32[]{:S(2)}, u32[]{:S(2)}) collective-permute-start(bf16[352,512]{1,0:T(8,128)(2,1)S(1)} %add_convert_fusion.3.refs_2_), channel_id=1, source_target_pairs={{0,32},{32,0},{64,96},{96,64},{128,160},{160,128},{192,224},{224,1... | collective-permute-start | bytes 1081352 | tf_op jit(solution)/shard_map/ppermute | solution.py:62
  51.5 8.8 %collective-permute-start.13 = (bf16[352,512]{1,0:T(8,128)(2,1)S(1)}, bf16[352,512]{1,0:T(8,128)(2,1)S(1)}, u32[]{:S(2)}, u32[]{:S(2)}) collective-permute-start(bf16[352,512]{1,0:T(8,128)(2,1)S(1)} %add_convert_fusion.2.refs_4_), channel_id=1, source_target_pairs={{0,192},{32,224},{64,128},{96,160},{128,64},{160,96},{192,0},{224,... | collective-permute-start | bytes 1081352 | tf_op jit(solution)/shard_map/ppermute | solution.py:62
  51.7 17.9 %collective-permute-start.10 = (bf16[80,1024]{1,0:T(8,128)(2,1)S(1)}, bf16[80,1024]{1,0:T(8,128)(2,1)S(1)}, u32[]{:S(2)}, u32[]{:S(2)}) collective-permute-start(bf16[80,1024]{1,0:T(8,128)(2,1)S(1)} %get-tuple-element.67.mine_ref), channel_id=1, source_target_pairs={{0,2},{1,3},{2,0},{3,1},{4,6},{5,7},{6,4},{7,5},{8,10},{9,11},{10,... | collective-permute-start | bytes 491528 | tf_op jit(solution)/shard_map/ppermute | solution.py:62
  55.5 13.3 %collective-permute-start.15 = (bf16[320,512]{1,0:T(8,128)(2,1)S(1)}, bf16[320,512]{1,0:T(8,128)(2,1)S(1)}, u32[]{:S(2)}, u32[]{:S(2)}) collective-permute-start(bf16[320,512]{1,0:T(8,128)(2,1)S(1)} %add_convert_fusion.6.refs_1_), channel_id=1, source_target_pairs={{0,32},{32,0},{64,96},{96,64},{128,160},{160,128},{192,224},{224,1... | collective-permute-start | bytes 983048 | tf_op jit(solution)/shard_map/ppermute | solution.py:62
  60.4 6.7 %collective-permute-start.16 = (bf16[352,512]{1,0:T(8,128)(2,1)S(1)}, bf16[352,512]{1,0:T(8,128)(2,1)S(1)}, u32[]{:S(2)}, u32[]{:S(2)}) collective-permute-start(bf16[352,512]{1,0:T(8,128)(2,1)S(1)} %add_convert_fusion.refs_2_), channel_id=1, source_target_pairs={{0,64},{32,96},{64,0},{96,32},{128,192},{160,224},{192,128},{224,1... | collective-permute-start | bytes 1081352 | tf_op jit(solution)/shard_map/ppermute | solution.py:62
  60.6 7.9 %collective-permute-start.14 = (bf16[352,512]{1,0:T(8,128)(2,1)S(1)}, bf16[352,512]{1,0:T(8,128)(2,1)S(1)}, u32[]{:S(2)}, u32[]{:S(2)}) collective-permute-start(bf16[352,512]{1,0:T(8,128)(2,1)S(1)} %add_convert_fusion.1.refs_0_), channel_id=1, source_target_pairs={{0,192},{32,224},{64,128},{96,160},{128,64},{160,96},{192,0},{224,... | collective-permute-start | bytes 1081352 | tf_op jit(solution)/shard_map/ppermute | solution.py:62
  60.8 8.8 %copy-start.1 = (bf16[512,1024]{1,0:T(8,128)(2,1)S(1)}, bf16[512,1024]{1,0:T(8,128)(2,1)}, u32[]{:S(2)}) copy-start(bf16[512,1024]{1,0:T(8,128)(2,1)} %og_ref.1) | copy-start | bytes 3145732
  67.2 22.0 %collective-permute-start.21 = (bf16[704,512]{1,0:T(8,128)(2,1)S(1)}, bf16[704,512]{1,0:T(8,128)(2,1)S(1)}, u32[]{:S(2)}, u32[]{:S(2)}) collective-permute-start(bf16[704,512]{1,0:T(8,128)(2,1)S(1)} %constant_dynamic-update-slice_fusion.4.refs_2_), channel_id=1, source_target_pairs={{0,32},{32,0},{64,96},{96,64},{128,160},{160,128},{192,224},{224,1... | collective-permute-start | bytes 2162696 | tf_op jit(solution)/shard_map/ppermute | solution.py:62
  68.6 20.5 %collective-permute-start.19 = (bf16[704,512]{1,0:T(8,128)(2,1)S(1)}, bf16[704,512]{1,0:T(8,128)(2,1)}, u32[]{:S(2)}, u32[]{:S(2)}) collective-permute-start(bf16[704,512]{1,0:T(8,128)(2,1)S(1)} %constant_dynamic-update-slice_fusion.refs_0_), channel_id=1, source_target_pairs={{0,64},{32,96},{64,0},{96,32},{128,192},{160,224},{192,128},{224,1... | collective-permute-start | bytes 2162696 | tf_op jit(solution)/shard_map/ppermute | solution.py:62
  68.9 0.7 copy-start.2
  68.9 20.2 %collective-permute-start.20 = (bf16[640,512]{1,0:T(8,128)(2,1)S(1)}, bf16[640,512]{1,0:T(8,128)(2,1)}, u32[]{:S(2)}, u32[]{:S(2)}) collective-permute-start(bf16[640,512]{1,0:T(8,128)(2,1)S(1)} %constant_dynamic-update-slice_fusion.2.refs_1_), channel_id=1, source_target_pairs={{0,192},{32,224},{64,128},{96,160},{128,64},{160,96},{192,0},{224,... | collective-permute-start | bytes 1966088 | tf_op jit(solution)/shard_map/ppermute | solution.py:62
  70.9 5.7 %collective-permute-start.17 = (bf16[64,1024]{1,0:T(8,128)(2,1)S(1)}, bf16[64,1024]{1,0:T(8,128)(2,1)S(1)}, u32[]{:S(2)}, u32[]{:S(2)}) collective-permute-start(bf16[64,1024]{1,0:T(8,128)(2,1)S(1)} %get-tuple-element.72), channel_id=1, source_target_pairs={{0,12},{1,13},{2,14},{3,15},{4,8},{5,9},{6,10},{7,11},{8,4},{9,5},... | collective-permute-start | bytes 393224 | tf_op jit(solution)/shard_map/ppermute | solution.py:62
  76.7 11.5 %collective-permute-start.18 = (bf16[128,1024]{1,0:T(8,128)(2,1)S(1)}, bf16[128,1024]{1,0:T(8,128)(2,1)}, u32[]{:S(2)}, u32[]{:S(2)}) collective-permute-start(bf16[128,1024]{1,0:T(8,128)(2,1)S(1)} %pad_maximum_fusion.1), channel_id=1, source_target_pairs={{0,4},{1,5},{2,6},{3,7},{4,0},{5,1},{6,2},{7,3},{8,12},{9,13},{10,... | collective-permute-start | bytes 786440 | tf_op jit(solution)/shard_map/ppermute | solution.py:62
  78.5 9.0 %all-to-all-start = ((f32[8,8,128]{2,1,0:T(8,128)}), f32[8,8,128]{2,1,0:T(8,128)S(1)}, u32[]{:S(2)}, u32[]{:S(2)}) async-start(f32[8,8,128]{2,1,0:T(8,128)} %get-tuple-element.83), calls=%async_computation | async-start | bytes 65536 | tf_op jit(solution)/shard_map/all_to_all | solution.py:427
  89.2 11.3 %collective-permute-start.22 = (bf16[256,1024]{1,0:T(8,128)(2,1)S(1)}, bf16[256,1024]{1,0:T(8,128)(2,1)S(1)}, u32[]{:S(2)}, u32[]{:S(2)}) collective-permute-start(bf16[256,1024]{1,0:T(8,128)(2,1)S(1)} %pad_maximum_fusion.low_ref), channel_id=1, source_target_pairs={{0,1},{1,0},{2,3},{3,2},{4,5},{5,4},{6,7},{7,6},{8,9},{9,8},{10,11... | collective-permute-start | bytes 1572872 | tf_op jit(solution)/shard_map/ppermute | solution.py:62

commit v5 on v4

--- a/solution.py
+++ b/solution.py
@@ -415,7 +415,7 @@
     third = [swap(v, o[2]) for v, o in zip(mine, ORDERS)]
     send, gain = mp_step(gain, (send, r4), 64, 0, mine)
     r5 = swap(send, "xh")
-    quarter = [after(plus(v, t), [send]) for v, t in zip(mine, third)]
+    quarter = [plus(v, t) for v, t in zip(mine, third)]
     back = [swap(v, o[1]) for v, o in zip(quarter, ORDERS)]
     half = [jnp.concatenate([v, b]) for v, b in zip(quarter, back)]
     last = [swap(v, o[0]) for v, o in zip(half, ORDERS)]

time: 102 us -> 104 us (1.020)
  starting transfers between devices: 40.4 us -> 51 us
  waiting for transfers between devices: 37 us -> 27.5 us
    ppermute x23, starting transfers between devices: 36.5 us -> 47.7 us  [swap(): return lax.ppermute(value, axis, pairs)]
    ppermute x23, waiting for transfers between devices: 34.6 us -> 24.7 us  [swap(): return lax.ppermute(value, axis, pairs)]
  transfers between devices with their start and end apart: 24 -> 24, of which waited for: 12 -> 10; matrix products, arithmetic and copies ran while one was open for 3% -> 3% of each run, Pallas kernels for 9% -> 9%
where the time goes in v5:
time: 104 us; the launch traced here: 103 us
  starting transfers between devices  51 us (49%)
  waiting for transfers between devices  27.5 us (26%)
  Pallas kernels  21 us (20%)
  other arithmetic  2.75 us (3%)
    ppermute x23, starting transfers between devices, swap(): return lax.ppermute(value, axis, pairs)  47.7 us
    ppermute x23, waiting for transfers between devices, swap(): return lax.ppermute(value, axis, pairs)  24.7 us
    pallas_call x1, Pallas kernels, front(): pl.pallas_call(front_kernel, in_specs=[SCALARS, *[pl.BlockSpec(memory_spa...  9.79 us
    pallas_call x2, Pallas kernels, place(): pl.pallas_call(functools.partial(place_kernel, late), in_specs=[SCALARS,...  5.55 us
    all_to_all x1, starting transfers between devices, shards(): gains = lax.all_to_all(after(gains, half), 'dp', 0, 0)  3.34 us
    all_to_all x1, waiting for transfers between devices, shards(): gains = lax.all_to_all(after(gains, half), 'dp', 0, 0)  2.75 us
    pallas_call x1, Pallas kernels, total_share(): pl.pallas_call(total_kernel, in_specs=[SCALARS, *whole(7)], out_specs=who...  2.48 us
  transfers between devices with their start and end apart: 24, of which 10 were waited for; matrix products, arithmetic and copies ran while one was open for 3% of the time, Pallas kernels for 9%

profile of v5, /device:TPU:1, one launch (start us, length us, event | category | flops | bytes accessed | tf_op | source)
XLA Modules:
  0.0 103.3 jit_solution(2920391308735193882)
XLA Ops:
  0.6 0.1 pad_add_fusion.where
  0.7 9.8 %front.1 = (bf16[704,512]{1,0:T(8,128)(2,1)S(1)}, bf16[704,512]{1,0:T(8,128)(2,1)S(1)}, bf16[640,512]{1,0:T(8,128)(2,1)S(1)}, bf16[640,512]{1,0:T(8,128)(2,1)S(1...) custom-call(s32[2]{0:T(128)S(1)} %pad_add_fusion.where, ...), custom_call_target="tpu_custom_call" | custom-call | flops 8589934592 | bytes 16777216 | tf_op jit(solution)/shard_map/front/pallas_call | solution.py:191
  10.5 2.2 %collective-permute-start.3 = (bf16[704,512]{1,0:T(8,128)(2,1)S(1)}, bf16[704,512]{1,0:T(8,128)(2,1)S(1)}, u32[]{:S(2)}, u32[]{:S(2)}) collective-permute-start(bf16[704,512]{1,0:T(8,128)(2,1)S(1)} %get-tuple-element.53), channel_id=1, source_target_pairs={{0,64},{32,96},{64,0},{96,32},{128,192},{160,224},{192,128},{224,1... | collective-permute-start | bytes 2162696 | tf_op jit(solution)/shard_map/ppermute | solution.py:62
  12.7 2.5 %total_share.1 = (bf16[272,1024]{1,0:T(8,128)(2,1)S(1)}, bf16[256,1024]{1,0:T(8,128)(2,1)S(1)}, f32[1,1024]{1,0:T(1,128)S(1)}) custom-call(s32[2]{0:T(128)S(1)} %pad_add_fusion.where, bf16[512,1024]{1,0:T(8,128)(2,1)S(1)} %copy-done, bf16[512,512]{1,0:T(8,128)(2,1)S(1)} %get-tuple-element.42.gq_ref, bf16[512,512]{1,0:T(8,128)(2,1)S(1)} %get-tuple-element.43.gk_ref, ...), custom_call_target="tpu_custom_call" | custom-call | flops 2147483648 | bytes 8388608 | tf_op jit(solution)/shard_map/total_share/pallas_call | solution.py:227
  15.2 1.2 %collective-permute-start = (bf16[272,1024]{1,0:T(8,128)(2,1)S(1)}, bf16[272,1024]{1,0:T(8,128)(2,1)S(1)}, u32[]{:S(2)}, u32[]{:S(2)}) collective-permute-start(bf16[272,1024]{1,0:T(8,128)(2,1)S(1)} %get-tuple-element.47), channel_id=1, source_target_pairs={{0,1},{1,0},{2,3},{3,2},{4,5},{5,4},{6,7},{7,6},{8,9},{9,8},{10,11... | collective-permute-start | bytes 1671176 | tf_op jit(solution)/shard_map/ppermute | solution.py:62
  16.5 1.0 collective-permute-start.5
  17.5 1.9 %collective-permute-start.4 = (bf16[640,512]{1,0:T(8,128)(2,1)S(1)}, bf16[640,512]{1,0:T(8,128)(2,1)S(1)}, u32[]{:S(2)}, u32[]{:S(2)}) collective-permute-start(bf16[640,512]{1,0:T(8,128)(2,1)S(1)} %get-tuple-element.56), channel_id=1, source_target_pairs={{0,192},{32,224},{64,128},{96,160},{128,64},{160,96},{192,0},{224,... | collective-permute-start | bytes 1966088 | tf_op jit(solution)/shard_map/ppermute | solution.py:62
  19.4 0.1 mp_step.4
  19.5 1.7 %collective-permute-start.1 = (bf16[144,1024]{1,0:T(8,128)(2,1)S(1)}, bf16[144,1024]{1,0:T(8,128)(2,1)S(1)}, u32[]{:S(2)}, u32[]{:S(2)}) collective-permute-start(bf16[144,1024]{1,0:T(8,128)(2,1)S(1)} %get-tuple-element.49), channel_id=1, source_target_pairs={{0,4},{1,5},{2,6},{3,7},{4,0},{5,1},{6,2},{7,3},{8,12},{9,13},{10,... | collective-permute-start | bytes 884744 | tf_op jit(solution)/shard_map/ppermute | solution.py:62
  21.3 6.1 %collective-permute-done.3 = bf16[704,512]{1,0:T(8,128)(2,1)S(1)} collective-permute-done((bf16[704,512]{1,0:T(8,128)(2,1)S(1)}, bf16[704,512]{1,0:T(8,128)(2,1)S(1)}, u32[]{:S(2)}, u32[]{:S(2)}) %collective-permute-start.3) | collective-permute-done | bytes 720928 | tf_op jit(solution)/shard_map/ppermute | solution.py:62
  27.4 0.1 add_convert_fusion.5.refs_4_
  27.4 0.5 collective-permute-done.1.refs_2_
  27.9 0.1 mp_step.5
  28.0 3.6 %collective-permute-start.7 = (bf16[352,512]{1,0:T(8,128)(2,1)S(1)}, bf16[352,512]{1,0:T(8,128)(2,1)S(1)}, u32[]{:S(2)}, u32[]{:S(2)}) collective-permute-start(bf16[352,512]{1,0:T(8,128)(2,1)S(1)} %add_convert_fusion.5.refs_4_), channel_id=1, source_target_pairs={{0,192},{32,224},{64,128},{96,160},{128,64},{160,96},{192,0},{224,... | collective-permute-start | bytes 1081352 | tf_op jit(solution)/shard_map/ppermute | solution.py:62
  31.6 2.5 %collective-permute-done.5 = bf16[704,512]{1,0:T(8,128)(2,1)S(1)} collective-permute-done((bf16[704,512]{1,0:T(8,128)(2,1)S(1)}, bf16[704,512]{1,0:T(8,128)(2,1)S(1)}, u32[]{:S(2)}, u32[]{:S(2)}) %collective-permute-start.5) | collective-permute-done | bytes 720928 | tf_op jit(solution)/shard_map/ppermute | solution.py:62
  34.2 0.1 add_convert_fusion.4.refs_6_
  34.3 4.2 %collective-permute-start.2 = (bf16[80,1024]{1,0:T(8,128)(2,1)S(1)}, bf16[80,1024]{1,0:T(8,128)(2,1)S(1)}, u32[]{:S(2)}, u32[]{:S(2)}) collective-permute-start(bf16[80,1024]{1,0:T(8,128)(2,1)S(1)} %get-tuple-element.51), channel_id=1, source_target_pairs={{0,12},{1,13},{2,14},{3,15},{4,8},{5,9},{6,10},{7,11},{8,4},{9,5},... | collective-permute-start | bytes 491528 | tf_op jit(solution)/shard_map/ppermute | solution.py:62
  38.5 0.2 collective-permute-start.9
  38.7 0.0 collective-permute-done.4
  38.7 0.1 add_convert_fusion.8.refs_5_
  38.8 1.3 %collective-permute-start.8 = (bf16[320,512]{1,0:T(8,128)(2,1)S(1)}, bf16[320,512]{1,0:T(8,128)(2,1)S(1)}, u32[]{:S(2)}, u32[]{:S(2)}) collective-permute-start(bf16[320,512]{1,0:T(8,128)(2,1)S(1)} %add_convert_fusion.8.refs_5_), channel_id=1, source_target_pairs={{0,32},{32,0},{64,96},{96,64},{128,160},{160,128},{192,224},{224,1... | collective-permute-start | bytes 983048 | tf_op jit(solution)/shard_map/ppermute | solution.py:62
  40.1 2.2 %collective-permute-done.2.refs_3_ = bf16[80,1024]{1,0:T(8,128)(2,1)S(1)} collective-permute-done((bf16[80,1024]{1,0:T(8,128)(2,1)S(1)}, bf16[80,1024]{1,0:T(8,128)(2,1)S(1)}, u32[]{:S(2)}, u32[]{:S(2)}) %collective-permute-start.2) | collective-permute-done | bytes 163872 | tf_op jit(solution)/shard_map/ppermute | solution.py:62
  42.3 0.1 mp_step.6
  42.4 4.3 %collective-permute-start.6 = (bf16[80,1024]{1,0:T(8,128)(2,1)S(1)}, bf16[80,1024]{1,0:T(8,128)(2,1)S(1)}, u32[]{:S(2)}, u32[]{:S(2)}) collective-permute-start(bf16[80,1024]{1,0:T(8,128)(2,1)S(1)} %get-tuple-element.62.refs_0_), channel_id=1, source_target_pairs={{0,28},{1,29},{2,30},{3,31},{4,24},{5,25},{6,26},{7,27},{8,20},{9,... | collective-permute-start | bytes 491528 | tf_op jit(solution)/shard_map/ppermute | solution.py:62
  46.7 0.0 collective-permute-done.7
  46.7 0.1 add_convert_fusion.3.refs_2_
  46.8 1.3 %collective-permute-start.11 = (bf16[352,512]{1,0:T(8,128)(2,1)S(1)}, bf16[352,512]{1,0:T(8,128)(2,1)S(1)}, u32[]{:S(2)}, u32[]{:S(2)}) collective-permute-start(bf16[352,512]{1,0:T(8,128)(2,1)S(1)} %add_convert_fusion.3.refs_2_), channel_id=1, source_target_pairs={{0,32},{32,0},{64,96},{96,64},{128,160},{160,128},{192,224},{224,1... | collective-permute-start | bytes 1081352 | tf_op jit(solution)/shard_map/ppermute | solution.py:62
  48.1 0.0 collective-permute-done.9
  48.1 0.1 add_convert_fusion.2.refs_4_
  48.3 2.0 %collective-permute-start.13 = (bf16[352,512]{1,0:T(8,128)(2,1)S(1)}, bf16[352,512]{1,0:T(8,128)(2,1)S(1)}, u32[]{:S(2)}, u32[]{:S(2)}) collective-permute-start(bf16[352,512]{1,0:T(8,128)(2,1)S(1)} %add_convert_fusion.2.refs_4_), channel_id=1, source_target_pairs={{0,192},{32,224},{64,128},{96,160},{128,64},{160,96},{192,0},{224,... | collective-permute-start | bytes 1081352 | tf_op jit(solution)/shard_map/ppermute | solution.py:62
  50.2 0.0 collective-permute-done.8
  50.2 0.1 add_convert_fusion.7.refs_3_
  50.4 0.5 collective-permute-start.12
  50.8 3.9 %collective-permute-done.11 = bf16[352,512]{1,0:T(8,128)(2,1)S(1)} collective-permute-done((bf16[352,512]{1,0:T(8,128)(2,1)S(1)}, bf16[352,512]{1,0:T(8,128)(2,1)S(1)}, u32[]{:S(2)}, u32[]{:S(2)}) %collective-permute-start.11) | collective-permute-done | bytes 360480 | tf_op jit(solution)/shard_map/ppermute | solution.py:62
  54.7 0.1 add_convert_fusion.1.refs_0_
  54.8 2.0 %collective-permute-start.14 = (bf16[352,512]{1,0:T(8,128)(2,1)S(1)}, bf16[352,512]{1,0:T(8,128)(2,1)S(1)}, u32[]{:S(2)}, u32[]{:S(2)}) collective-permute-start(bf16[352,512]{1,0:T(8,128)(2,1)S(1)} %add_convert_fusion.1.refs_0_), channel_id=1, source_target_pairs={{0,192},{32,224},{64,128},{96,160},{128,64},{160,96},{192,0},{224,... | collective-permute-start | bytes 1081352 | tf_op jit(solution)/shard_map/ppermute | solution.py:62
  56.8 0.3 collective-permute-done.13
  57.1 0.1 add_convert_fusion.refs_2_
  57.2 0.2 collective-permute-start.16
  57.4 0.1 add_convert_fusion.6.refs_1_
  57.5 1.3 %collective-permute-start.15 = (bf16[320,512]{1,0:T(8,128)(2,1)S(1)}, bf16[320,512]{1,0:T(8,128)(2,1)S(1)}, u32[]{:S(2)}, u32[]{:S(2)}) collective-permute-start(bf16[320,512]{1,0:T(8,128)(2,1)S(1)} %add_convert_fusion.6.refs_1_), channel_id=1, source_target_pairs={{0,32},{32,0},{64,96},{96,64},{128,160},{160,128},{192,224},{224,1... | collective-permute-start | bytes 983048 | tf_op jit(solution)/shard_map/ppermute | solution.py:62
  58.8 0.0 collective-permute-done.6.refs_1_
  58.8 0.1 mp_step.7
  58.8 2.5 %collective-permute-start.10 = (bf16[80,1024]{1,0:T(8,128)(2,1)S(1)}, bf16[80,1024]{1,0:T(8,128)(2,1)S(1)}, u32[]{:S(2)}, u32[]{:S(2)}) collective-permute-start(bf16[80,1024]{1,0:T(8,128)(2,1)S(1)} %get-tuple-element.64.mine_ref), channel_id=1, source_target_pairs={{0,2},{1,3},{2,0},{3,1},{4,6},{5,7},{6,4},{7,5},{8,10},{9,11},{10,... | collective-permute-start | bytes 491528 | tf_op jit(solution)/shard_map/ppermute | solution.py:62
  61.4 4.0 %collective-permute-done.14 = bf16[352,512]{1,0:T(8,128)(2,1)S(1)} collective-permute-done((bf16[352,512]{1,0:T(8,128)(2,1)S(1)}, bf16[352,512]{1,0:T(8,128)(2,1)S(1)}, u32[]{:S(2)}, u32[]{:S(2)}) %collective-permute-start.14) | collective-permute-done | bytes 360480 | tf_op jit(solution)/shard_map/ppermute | solution.py:62
  65.4 0.0 copy-start.1
  65.4 0.0 copy-start.2
  65.4 0.1 collective-permute-start.19
  65.5 0.0 collective-permute-done.16
  65.6 0.1 collective-permute-start.21
  65.8 2.0 %collective-permute-start.20 = (bf16[640,512]{1,0:T(8,128)(2,1)S(1)}, bf16[640,512]{1,0:T(8,128)(2,1)}, u32[]{:S(2)}, u32[]{:S(2)}) collective-permute-start(bf16[640,512]{1,0:T(8,128)(2,1)S(1)} %pad_maximum_fusion.2.refs_1_), channel_id=1, source_target_pairs={{0,192},{32,224},{64,128},{96,160},{128,64},{160,96},{192,0},{224,... | collective-permute-start | bytes 1966088 | tf_op jit(solution)/shard_map/ppermute | solution.py:62
  67.7 0.9 collective-permute-done.10.got_ref
  68.6 1.3 %own_rows.1 = (bf16[64,1024]{1,0:T(8,128)(2,1)S(1)}, f32[8,8,128]{2,1,0:T(8,128)}) custom-call(s32[2]{0:T(128)S(1)} %pad_add_fusion.where, bf16[512,1024]{1,0:T(8,128)(2,1)S(1)} %copy-done, bf16[512,1024]{1,0:T(8,128)(2,1)S(1)} %copy-done.1, f32[1,1024]{1,0:T(1,128)S(1)} %bitcast.5, f32[1,1024]{1,0:T(1,128)S(1)} %get-tuple-element.63.gain_ref, ...), custom_call_target="tpu_custom_call" | custom-call | flops 1024 | bytes 1024 | tf_op jit(solution)/shard_map/own_rows/pallas_call | solution.py:290
  69.9 1.6 %collective-permute-start.17 = (bf16[64,1024]{1,0:T(8,128)(2,1)S(1)}, bf16[64,1024]{1,0:T(8,128)(2,1)S(1)}, u32[]{:S(2)}, u32[]{:S(2)}) collective-permute-start(bf16[64,1024]{1,0:T(8,128)(2,1)S(1)} %get-tuple-element.66), channel_id=1, source_target_pairs={{0,12},{1,13},{2,14},{3,15},{4,8},{5,9},{6,10},{7,11},{8,4},{9,5},... | collective-permute-start | bytes 393224 | tf_op jit(solution)/shard_map/ppermute | solution.py:62
  71.6 4.3 %collective-permute-done.17 = bf16[64,1024]{1,0:T(8,128)(2,1)S(1)} collective-permute-done((bf16[64,1024]{1,0:T(8,128)(2,1)S(1)}, bf16[64,1024]{1,0:T(8,128)(2,1)S(1)}, u32[]{:S(2)}, u32[]{:S(2)}) %collective-permute-start.17) | collective-permute-done | bytes 131104 | tf_op jit(solution)/shard_map/ppermute | solution.py:62
  75.9 1.9 %collective-permute-start.18 = (bf16[128,1024]{1,0:T(8,128)(2,1)S(1)}, bf16[128,1024]{1,0:T(8,128)(2,1)}, u32[]{:S(2)}, u32[]{:S(2)}) collective-permute-start(bf16[128,1024]{1,0:T(8,128)(2,1)S(1)} %pad_maximum_fusion.4), channel_id=1, source_target_pairs={{0,4},{1,5},{2,6},{3,7},{4,0},{5,1},{6,2},{7,3},{8,12},{9,13},{10,... | collective-permute-start | bytes 786440 | tf_op jit(solution)/shard_map/ppermute | solution.py:62
  77.8 3.3 %all-to-all-start = ((f32[8,8,128]{2,1,0:T(8,128)}), f32[8,8,128]{2,1,0:T(8,128)S(1)}, u32[]{:S(2)}, u32[]{:S(2)}) async-start(f32[8,8,128]{2,1,0:T(8,128)} %get-tuple-element.77), calls=%async_computation | async-start | bytes 65536 | tf_op jit(solution)/shard_map/all_to_all | solution.py:427
  81.1 2.7 %place_early.1 = (bf16[1024,512]{1,0:T(8,128)(2,1)}, bf16[1024,512]{1,0:T(8,128)(2,1)}, bf16[1024,512]{1,0:T(8,128)(2,1)}, bf16[512,1024]{1,0:T(8,128)(2,1)}, f32[8,128]{1,0:T(8,128)}) custom-call(s32[2]{0:T(128)S(1)} %pad_add_fusion.where, bf16[704,512]{1,0:T(8,128)(2,1)S(1)} %pad_maximum_fusion.refs_0_, bf16[640,512]{1,0:T(8,128)(2,1)S(1)} %pad_maximum_fusion.2.refs_1_, ...), custom_call_target="tpu_custom_call" | custom-call | flops 1024 | bytes 1024 | tf_op jit(solution)/shard_map/place_early/pallas_call | solution.py:333
  83.8 2.7 %all-to-all-done = f32[8,8,128]{2,1,0:T(8,128)S(1)} async-done(((f32[8,8,128]{2,1,0:T(8,128)}), f32[8,8,128]{2,1,0:T(8,128)S(1)}, u32[]{:S(2)}, u32[]{:S(2)}) %all-to-all-start) | async-done | bytes 32800 | tf_op jit(solution)/shard_map/all_to_all | solution.py:427
  86.5 0.6 reduce_sum.9
  87.2 1.0 pad_maximum_fusion.3.low_ref
  88.2 10.5 %collective-permute-start.22 = (bf16[256,1024]{1,0:T(8,128)(2,1)S(1)}, bf16[256,1024]{1,0:T(8,128)(2,1)S(1)}, u32[]{:S(2)}, u32[]{:S(2)}) collective-permute-start(bf16[256,1024]{1,0:T(8,128)(2,1)S(1)} %pad_maximum_fusion.3.low_ref), channel_id=1, source_target_pairs={{0,1},{1,0},{2,3},{3,2},{4,5},{5,4},{6,7},{7,6},{8,9},{9,8},{10,11... | collective-permute-start | bytes 1572872 | tf_op jit(solution)/shard_map/ppermute | solution.py:62
  98.7 2.9 %place_late.1 = (bf16[1024,512]{1,0:T(8,128)(2,1)}, bf16[1024,512]{1,0:T(8,128)(2,1)}, bf16[1024,512]{1,0:T(8,128)(2,1)}, bf16[512,1024]{1,0:T(8,128)(2,1)}) custom-call(s32[2]{0:T(128)S(1)} %pad_add_fusion.where, bf16[704,512]{1,0:T(8,128)(2,1)S(1)} %collective-permute-done.19.refs_0_, ...), custom_call_target="tpu_custom_call", output_to_operand_aliasing={{0}: (4, {}), {1}: (5, {}), {2}: (6, {}), {3}: (7, {})} | custom-call | flops 68719476736 | bytes 1024 | tf_op jit(solution)/shard_map/place_late/pallas_call | solution.py:333
  101.6 1.6 %place_rows.1 = bf16[512,1024]{1,0:T(8,128)(2,1)} custom-call(s32[2]{0:T(128)S(1)} %pad_add_fusion.where, bf16[256,1024]{1,0:T(8,128)(2,1)S(1)} %pad_maximum_fusion.3.low_ref, bf16[256,1024]{1,0:T(8,128)(2,1)S(1)} %collective-permute-done.22.high_ref), custom_call_target="tpu_custom_call" | custom-call | flops 1024 | bytes 2097152 | tf_op jit(solution)/shard_map/place_rows/pallas_call | solution.py:360
  (22 shorter events, 0.2 us)
Async XLA Ops:
  0.7 12.0 %copy-start = (bf16[512,1024]{1,0:T(8,128)(2,1)S(1)}, bf16[512,1024]{1,0:T(8,128)(2,1)}, u32[]{:S(2)}) copy-start(bf16[512,1024]{1,0:T(8,128)(2,1)} %x_ref.3) | copy-start | bytes 3145732
  0.7 12.0 %copy-start.3 = (bf16[1024,512]{1,0:T(8,128)(2,1)S(1)}, bf16[1024,512]{1,0:T(8,128)(2,1)}, u32[]{:S(2)}) copy-start(bf16[1024,512]{1,0:T(8,128)(2,1)} %wq_ref.1) | copy-start | bytes 3145732
  0.7 12.0 %copy-start.4 = (bf16[1024,512]{1,0:T(8,128)(2,1)S(1)}, bf16[1024,512]{1,0:T(8,128)(2,1)}, u32[]{:S(2)}) copy-start(bf16[1024,512]{1,0:T(8,128)(2,1)} %wk_ref.1) | copy-start | bytes 3145732
  0.7 12.0 %copy-start.5 = (bf16[1024,512]{1,0:T(8,128)(2,1)S(1)}, bf16[1024,512]{1,0:T(8,128)(2,1)}, u32[]{:S(2)}) copy-start(bf16[1024,512]{1,0:T(8,128)(2,1)} %wv_ref.1) | copy-start | bytes 3145732
  10.5 16.8 %collective-permute-start.3 = (bf16[704,512]{1,0:T(8,128)(2,1)S(1)}, bf16[704,512]{1,0:T(8,128)(2,1)S(1)}, u32[]{:S(2)}, u32[]{:S(2)}) collective-permute-start(bf16[704,512]{1,0:T(8,128)(2,1)S(1)} %get-tuple-element.53), channel_id=1, source_target_pairs={{0,64},{32,96},{64,0},{96,32},{128,192},{160,224},{192,128},{224,1... | collective-permute-start | bytes 2162696 | tf_op jit(solution)/shard_map/ppermute | solution.py:62
  15.2 4.2 %collective-permute-start = (bf16[272,1024]{1,0:T(8,128)(2,1)S(1)}, bf16[272,1024]{1,0:T(8,128)(2,1)S(1)}, u32[]{:S(2)}, u32[]{:S(2)}) collective-permute-start(bf16[272,1024]{1,0:T(8,128)(2,1)S(1)} %get-tuple-element.47), channel_id=1, source_target_pairs={{0,1},{1,0},{2,3},{3,2},{4,5},{5,4},{6,7},{7,6},{8,9},{9,8},{10,11... | collective-permute-start | bytes 1671176 | tf_op jit(solution)/shard_map/ppermute | solution.py:62
  16.5 17.7 %collective-permute-start.5 = (bf16[704,512]{1,0:T(8,128)(2,1)S(1)}, bf16[704,512]{1,0:T(8,128)(2,1)S(1)}, u32[]{:S(2)}, u32[]{:S(2)}) collective-permute-start(bf16[704,512]{1,0:T(8,128)(2,1)S(1)} %get-tuple-element.59), channel_id=1, source_target_pairs={{0,32},{32,0},{64,96},{96,64},{128,160},{160,128},{192,224},{224,1... | collective-permute-start | bytes 2162696 | tf_op jit(solution)/shard_map/ppermute | solution.py:62
  17.5 21.2 %collective-permute-start.4 = (bf16[640,512]{1,0:T(8,128)(2,1)S(1)}, bf16[640,512]{1,0:T(8,128)(2,1)S(1)}, u32[]{:S(2)}, u32[]{:S(2)}) collective-permute-start(bf16[640,512]{1,0:T(8,128)(2,1)S(1)} %get-tuple-element.56), channel_id=1, source_target_pairs={{0,192},{32,224},{64,128},{96,160},{128,64},{160,96},{192,0},{224,... | collective-permute-start | bytes 1966088 | tf_op jit(solution)/shard_map/ppermute | solution.py:62
  19.5 8.4 %collective-permute-start.1 = (bf16[144,1024]{1,0:T(8,128)(2,1)S(1)}, bf16[144,1024]{1,0:T(8,128)(2,1)S(1)}, u32[]{:S(2)}, u32[]{:S(2)}) collective-permute-start(bf16[144,1024]{1,0:T(8,128)(2,1)S(1)} %get-tuple-element.49), channel_id=1, source_target_pairs={{0,4},{1,5},{2,6},{3,7},{4,0},{5,1},{6,2},{7,3},{8,12},{9,13},{10,... | collective-permute-start | bytes 884744 | tf_op jit(solution)/shard_map/ppermute | solution.py:62
  28.0 18.6 %collective-permute-start.7 = (bf16[352,512]{1,0:T(8,128)(2,1)S(1)}, bf16[352,512]{1,0:T(8,128)(2,1)S(1)}, u32[]{:S(2)}, u32[]{:S(2)}) collective-permute-start(bf16[352,512]{1,0:T(8,128)(2,1)S(1)} %add_convert_fusion.5.refs_4_), channel_id=1, source_target_pairs={{0,192},{32,224},{64,128},{96,160},{128,64},{160,96},{192,0},{224,... | collective-permute-start | bytes 1081352 | tf_op jit(solution)/shard_map/ppermute | solution.py:62
  34.3 8.0 %collective-permute-start.2 = (bf16[80,1024]{1,0:T(8,128)(2,1)S(1)}, bf16[80,1024]{1,0:T(8,128)(2,1)S(1)}, u32[]{:S(2)}, u32[]{:S(2)}) collective-permute-start(bf16[80,1024]{1,0:T(8,128)(2,1)S(1)} %get-tuple-element.51), channel_id=1, source_target_pairs={{0,12},{1,13},{2,14},{3,15},{4,8},{5,9},{6,10},{7,11},{8,4},{9,5},... | collective-permute-start | bytes 491528 | tf_op jit(solution)/shard_map/ppermute | solution.py:62
  38.5 9.6 %collective-permute-start.9 = (bf16[352,512]{1,0:T(8,128)(2,1)S(1)}, bf16[352,512]{1,0:T(8,128)(2,1)S(1)}, u32[]{:S(2)}, u32[]{:S(2)}) collective-permute-start(bf16[352,512]{1,0:T(8,128)(2,1)S(1)} %add_convert_fusion.4.refs_6_), channel_id=1, source_target_pairs={{0,64},{32,96},{64,0},{96,32},{128,192},{160,224},{192,128},{224,1... | collective-permute-start | bytes 1081352 | tf_op jit(solution)/shard_map/ppermute | solution.py:62
  38.8 11.5 %collective-permute-start.8 = (bf16[320,512]{1,0:T(8,128)(2,1)S(1)}, bf16[320,512]{1,0:T(8,128)(2,1)S(1)}, u32[]{:S(2)}, u32[]{:S(2)}) collective-permute-start(bf16[320,512]{1,0:T(8,128)(2,1)S(1)} %add_convert_fusion.8.refs_5_), channel_id=1, source_target_pairs={{0,32},{32,0},{64,96},{96,64},{128,160},{160,128},{192,224},{224,1... | collective-permute-start | bytes 983048 | tf_op jit(solution)/shard_map/ppermute | solution.py:62
  42.4 16.4 %collective-permute-start.6 = (bf16[80,1024]{1,0:T(8,128)(2,1)S(1)}, bf16[80,1024]{1,0:T(8,128)(2,1)S(1)}, u32[]{:S(2)}, u32[]{:S(2)}) collective-permute-start(bf16[80,1024]{1,0:T(8,128)(2,1)S(1)} %get-tuple-element.62.refs_0_), channel_id=1, source_target_pairs={{0,28},{1,29},{2,30},{3,31},{4,24},{5,25},{6,26},{7,27},{8,20},{9,... | collective-permute-start | bytes 491528 | tf_op jit(solution)/shard_map/ppermute | solution.py:62
  46.8 7.9 %collective-permute-start.11 = (bf16[352,512]{1,0:T(8,128)(2,1)S(1)}, bf16[352,512]{1,0:T(8,128)(2,1)S(1)}, u32[]{:S(2)}, u32[]{:S(2)}) collective-permute-start(bf16[352,512]{1,0:T(8,128)(2,1)S(1)} %add_convert_fusion.3.refs_2_), channel_id=1, source_target_pairs={{0,32},{32,0},{64,96},{96,64},{128,160},{160,128},{192,224},{224,1... | collective-permute-start | bytes 1081352 | tf_op jit(solution)/shard_map/ppermute | solution.py:62
  48.3 8.8 %collective-permute-start.13 = (bf16[352,512]{1,0:T(8,128)(2,1)S(1)}, bf16[352,512]{1,0:T(8,128)(2,1)S(1)}, u32[]{:S(2)}, u32[]{:S(2)}) collective-permute-start(bf16[352,512]{1,0:T(8,128)(2,1)S(1)} %add_convert_fusion.2.refs_4_), channel_id=1, source_target_pairs={{0,192},{32,224},{64,128},{96,160},{128,64},{160,96},{192,0},{224,... | collective-permute-start | bytes 1081352 | tf_op jit(solution)/shard_map/ppermute | solution.py:62
  50.4 7.0 %collective-permute-start.12 = (bf16[320,512]{1,0:T(8,128)(2,1)S(1)}, bf16[320,512]{1,0:T(8,128)(2,1)S(1)}, u32[]{:S(2)}, u32[]{:S(2)}) collective-permute-start(bf16[320,512]{1,0:T(8,128)(2,1)S(1)} %add_convert_fusion.7.refs_3_), channel_id=1, source_target_pairs={{0,64},{32,96},{64,0},{96,32},{128,192},{160,224},{192,128},{224,1... | collective-permute-start | bytes 983048 | tf_op jit(solution)/shard_map/ppermute | solution.py:62
  54.8 10.6 %collective-permute-start.14 = (bf16[352,512]{1,0:T(8,128)(2,1)S(1)}, bf16[352,512]{1,0:T(8,128)(2,1)S(1)}, u32[]{:S(2)}, u32[]{:S(2)}) collective-permute-start(bf16[352,512]{1,0:T(8,128)(2,1)S(1)} %add_convert_fusion.1.refs_0_), channel_id=1, source_target_pairs={{0,192},{32,224},{64,128},{96,160},{128,64},{160,96},{192,0},{224,... | collective-permute-start | bytes 1081352 | tf_op jit(solution)/shard_map/ppermute | solution.py:62
  57.2 8.3 %collective-permute-start.16 = (bf16[352,512]{1,0:T(8,128)(2,1)S(1)}, bf16[352,512]{1,0:T(8,128)(2,1)S(1)}, u32[]{:S(2)}, u32[]{:S(2)}) collective-permute-start(bf16[352,512]{1,0:T(8,128)(2,1)S(1)} %add_convert_fusion.refs_2_), channel_id=1, source_target_pairs={{0,64},{32,96},{64,0},{96,32},{128,192},{160,224},{192,128},{224,1... | collective-permute-start | bytes 1081352 | tf_op jit(solution)/shard_map/ppermute | solution.py:62
  57.5 8.2 %collective-permute-start.15 = (bf16[320,512]{1,0:T(8,128)(2,1)S(1)}, bf16[320,512]{1,0:T(8,128)(2,1)S(1)}, u32[]{:S(2)}, u32[]{:S(2)}) collective-permute-start(bf16[320,512]{1,0:T(8,128)(2,1)S(1)} %add_convert_fusion.6.refs_1_), channel_id=1, source_target_pairs={{0,32},{32,0},{64,96},{96,64},{128,160},{160,128},{192,224},{224,1... | collective-permute-start | bytes 983048 | tf_op jit(solution)/shard_map/ppermute | solution.py:62
  58.8 9.8 %collective-permute-start.10 = (bf16[80,1024]{1,0:T(8,128)(2,1)S(1)}, bf16[80,1024]{1,0:T(8,128)(2,1)S(1)}, u32[]{:S(2)}, u32[]{:S(2)}) collective-permute-start(bf16[80,1024]{1,0:T(8,128)(2,1)S(1)} %get-tuple-element.64.mine_ref), channel_id=1, source_target_pairs={{0,2},{1,3},{2,0},{3,1},{4,6},{5,7},{6,4},{7,5},{8,10},{9,11},{10,... | collective-permute-start | bytes 491528 | tf_op jit(solution)/shard_map/ppermute | solution.py:62
  65.4 3.2 %copy-start.1 = (bf16[512,1024]{1,0:T(8,128)(2,1)S(1)}, bf16[512,1024]{1,0:T(8,128)(2,1)}, u32[]{:S(2)}) copy-start(bf16[512,1024]{1,0:T(8,128)(2,1)} %og_ref.1) | copy-start | bytes 3145732
  65.4 3.2 %copy-start.2 = (f32[1024]{0:T(1024)S(1)}, f32[1024]{0:T(1024)}, u32[]{:S(2)}) copy-start(f32[1024]{0:T(1024)} %param.11) | copy-start | bytes 12292
  65.4 22.7 %collective-permute-start.19 = (bf16[704,512]{1,0:T(8,128)(2,1)S(1)}, bf16[704,512]{1,0:T(8,128)(2,1)S(1)}, u32[]{:S(2)}, u32[]{:S(2)}) collective-permute-start(bf16[704,512]{1,0:T(8,128)(2,1)S(1)} %pad_maximum_fusion.refs_0_), channel_id=1, source_target_pairs={{0,64},{32,96},{64,0},{96,32},{128,192},{160,224},{192,128},{224,1... | collective-permute-start | bytes 2162696 | tf_op jit(solution)/shard_map/ppermute | solution.py:62
  65.6 22.6 %collective-permute-start.21 = (bf16[704,512]{1,0:T(8,128)(2,1)S(1)}, bf16[704,512]{1,0:T(8,128)(2,1)}, u32[]{:S(2)}, u32[]{:S(2)}) collective-permute-start(bf16[704,512]{1,0:T(8,128)(2,1)S(1)} %pad_maximum_fusion.1.refs_2_), channel_id=1, source_target_pairs={{0,32},{32,0},{64,96},{96,64},{128,160},{160,128},{192,224},{224,1... | collective-permute-start | bytes 2162696 | tf_op jit(solution)/shard_map/ppermute | solution.py:62
  65.8 22.4 %collective-permute-start.20 = (bf16[640,512]{1,0:T(8,128)(2,1)S(1)}, bf16[640,512]{1,0:T(8,128)(2,1)}, u32[]{:S(2)}, u32[]{:S(2)}) collective-permute-start(bf16[640,512]{1,0:T(8,128)(2,1)S(1)} %pad_maximum_fusion.2.refs_1_), channel_id=1, source_target_pairs={{0,192},{32,224},{64,128},{96,160},{128,64},{160,96},{192,0},{224,... | collective-permute-start | bytes 1966088 | tf_op jit(solution)/shard_map/ppermute | solution.py:62
  69.9 5.9 %collective-permute-start.17 = (bf16[64,1024]{1,0:T(8,128)(2,1)S(1)}, bf16[64,1024]{1,0:T(8,128)(2,1)S(1)}, u32[]{:S(2)}, u32[]{:S(2)}) collective-permute-start(bf16[64,1024]{1,0:T(8,128)(2,1)S(1)} %get-tuple-element.66), channel_id=1, source_target_pairs={{0,12},{1,13},{2,14},{3,15},{4,8},{5,9},{6,10},{7,11},{8,4},{9,5},... | collective-permute-start | bytes 393224 | tf_op jit(solution)/shard_map/ppermute | solution.py:62
  75.9 11.3 %collective-permute-start.18 = (bf16[128,1024]{1,0:T(8,128)(2,1)S(1)}, bf16[128,1024]{1,0:T(8,128)(2,1)}, u32[]{:S(2)}, u32[]{:S(2)}) collective-permute-start(bf16[128,1024]{1,0:T(8,128)(2,1)S(1)} %pad_maximum_fusion.4), channel_id=1, source_target_pairs={{0,4},{1,5},{2,6},{3,7},{4,0},{5,1},{6,2},{7,3},{8,12},{9,13},{10,... | collective-permute-start | bytes 786440 | tf_op jit(solution)/shard_map/ppermute | solution.py:62
  77.8 8.8 %all-to-all-start = ((f32[8,8,128]{2,1,0:T(8,128)}), f32[8,8,128]{2,1,0:T(8,128)S(1)}, u32[]{:S(2)}, u32[]{:S(2)}) async-start(f32[8,8,128]{2,1,0:T(8,128)} %get-tuple-element.77), calls=%async_computation | async-start | bytes 65536 | tf_op jit(solution)/shard_map/all_to_all | solution.py:427
  88.2 13.4 %collective-permute-start.22 = (bf16[256,1024]{1,0:T(8,128)(2,1)S(1)}, bf16[256,1024]{1,0:T(8,128)(2,1)S(1)}, u32[]{:S(2)}, u32[]{:S(2)}) collective-permute-start(bf16[256,1024]{1,0:T(8,128)(2,1)S(1)} %pad_maximum_fusion.3.low_ref), channel_id=1, source_target_pairs={{0,1},{1,0},{2,3},{3,2},{4,5},{5,4},{6,7},{7,6},{8,9},{9,8},{10,11... | collective-permute-start | bytes 1572872 | tf_op jit(solution)/shard_map/ppermute | solution.py:62
